TPU v7x, 32 devices: a whole 2x2x4 slice. The times are simulated.
32 devices in a mesh: seq: 4 (over y, core), ctx: 8 (over z, x).
Axes of the slice: x: 2, y: 2, z: 4, core: 2. Of those that a mesh axis runs over, the one named last changes fastest.
Arguments:
- tokens: bfloat16 [8, 1024, 768], P('seq', 'ctx'), may hold values from -6 to 6
- grad_out: bfloat16 [8, 1024, 768], P('seq', 'ctx'), may hold values from -6 to 6
- timestep: int32 [8], P('seq'), may hold values from 0 to 1999
- w_time: bfloat16 [768, 768], P('seq'), may hold values from -0.21875 to 0.21875
- b_time: bfloat16 [768], P('seq'), may hold values from -3 to 3
- ln1_gain: bfloat16 [768], P('seq'), may hold values from 0.099609375 to 1.8984375
- ln1_bias: bfloat16 [768], P('seq'), may hold values from -3 to 3
- w_qkv: bfloat16 [768, 2304], P('seq'), may hold values from -0.3125 to 0.3125
- b_query: bfloat16 [768], P('seq'), may hold values from -3 to 3
- b_value: bfloat16 [768], P('seq'), may hold values from -3 to 3
- w_out: bfloat16 [768, 768], P('seq'), may hold values from -1 to 1
- b_out: bfloat16 [768], P('seq'), may hold values from -3 to 3
- ln2_gain: bfloat16 [768], P('seq'), may hold values from 0.099609375 to 1.8984375
- ln2_bias: bfloat16 [768], P('seq'), may hold values from -3 to 3
- w_up: bfloat16 [768, 3072], P('seq'), may hold values from -0.21875 to 0.21875
- b_up: bfloat16 [3072], P('seq'), may hold values from -3 to 3
- w_down: bfloat16 [3072, 768], P('seq'), may hold values from -0.109375 to 0.109375
- b_down: bfloat16 [768], P('seq'), may hold values from -3 to 3
Outputs:
- output: bfloat16 [8, 1024, 768], P('seq', 'ctx')
- grad_tokens: bfloat16 [8, 1024, 768], P('seq', 'ctx')
- grad_w_time: float32 [768, 768], P('seq')
- grad_b_time: float32 [768], P('seq')
- grad_ln1_gain: float32 [768], P('seq')
- grad_ln1_bias: float32 [768], P('seq')
- grad_w_qkv: float32 [768, 2304], P('seq')
- grad_b_query: float32 [768], P('seq')
- grad_b_value: float32 [768], P('seq')
- grad_w_out: float32 [768, 768], P('seq')
- grad_b_out: float32 [768], P('seq')
- grad_ln2_gain: float32 [768], P('seq')
- grad_ln2_bias: float32 [768], P('seq')
- grad_w_up: float32 [768, 3072], P('seq')
- grad_b_up: float32 [3072], P('seq')
- grad_w_down: float32 [3072, 768], P('seq')
- grad_b_down: float32 [768], P('seq')
All inputs are finite; a program needn't handle non-finite values.
Results may differ from a plain program's by a relative error of at most 0.028.
Values may be sent and summed in bfloat16 or wider, within the bound.
No kernel may reach another device: no remote copies, remote signals or barrier semaphores. Data moves between devices by JAX's collectives and lax.ppermute only.
A program may use at most 320 MiB of HBM per device.

v0:
```python
import math

import jax
import jax.numpy as jnp
from jax import lax
from jax.sharding import PartitionSpec as P

HEADS = 12
HEAD_DIM = 64


norm_eps = 1e-05
block_keys = 1024


def layer_norm(hidden, norm_gain, offset):
    center = hidden - jnp.mean(hidden, axis=-1, keepdims=True)
    variance = jnp.mean(center * center, axis=-1, keepdims=True)
    return center * lax.rsqrt(variance + norm_eps) * norm_gain + offset


def gelu_exact(values):
    return jax.nn.gelu(values, approximate=False)


def sinusoid(timestep, model_width):
    half_width = model_width // 2
    frequency = jnp.exp(
        -math.log(10000.0) * jnp.arange(half_width).astype(jnp.float32) / half_width
    )
    angles = timestep.astype(jnp.float32)[:, None] * frequency[None, :]
    return jnp.concatenate([jnp.sin(angles), jnp.cos(angles)], axis=-1)


def scores_of(queries, keys_blk, score_scale):
    return score_scale * jnp.einsum(
        "sphe,skhe->shpk", queries, keys_blk, preferred_element_type=jnp.float32
    )


def token_sum(values):
    return jnp.sum(values.astype(jnp.float32), axis=(0, 1))


def softmax_totals(query_low, key_all, score_scale, block_len):
    seq_count, row_count, head_count, head_width = query_low.shape
    blocks = key_all.shape[1] // block_len

    def softmax_block_step(carry, block_index):
        top_now, running = carry
        keys_blk = lax.dynamic_slice_in_dim(key_all, block_index * block_len, block_len, 1)
        scores = scores_of(query_low, keys_blk, score_scale)
        top_new = jnp.maximum(top_now, jnp.max(scores, axis=-1))
        running = running * jnp.exp(top_now - top_new) + jnp.sum(
            jnp.exp(scores - top_new[..., None]), axis=-1
        )
        return ((top_new, running), None)

    initial = (
        jnp.full((seq_count, head_count, row_count), -jnp.inf, jnp.float32),
        jnp.zeros((seq_count, head_count, row_count), jnp.float32),
    )
    (top_now, running), unused = lax.scan(softmax_block_step, initial, jnp.arange(blocks))
    return top_now + jnp.log(running)


def attend(query_low, key_all, value_all, log_totals, score_scale, block_len):
    blocks = key_all.shape[1] // block_len

    def attend_block_step(running, block_index):
        offset = block_index * block_len
        keys_blk = lax.dynamic_slice_in_dim(key_all, offset, block_len, 1)
        values_blk = lax.dynamic_slice_in_dim(value_all, offset, block_len, 1)
        probs_low = jnp.exp(
            scores_of(query_low, keys_blk, score_scale) - log_totals[..., None]
        ).astype(jnp.bfloat16)
        running = running + jnp.einsum(
            "shpk,skhe->sphe", probs_low, values_blk, preferred_element_type=jnp.float32
        )
        return (running, None)

    result, unused = lax.scan(
        attend_block_step, jnp.zeros(query_low.shape, jnp.float32), jnp.arange(blocks)
    )
    return result


def backward_reduce(
    query_low, key_all, value_all, grad_attn, log_totals, delta, score_scale, block_len
):
    blocks = key_all.shape[1] // block_len

    def backward_block_step(carry, block_index):
        grad_query, grad_key, grad_value = carry
        offset = block_index * block_len
        keys_blk = lax.dynamic_slice_in_dim(key_all, offset, block_len, 1)
        values_blk = lax.dynamic_slice_in_dim(value_all, offset, block_len, 1)
        weights = jnp.exp(scores_of(query_low, keys_blk, score_scale) - log_totals[..., None])
        probs_low = weights.astype(jnp.bfloat16)
        value_part = jnp.einsum(
            "shpk,sphe->skhe", probs_low, grad_attn, preferred_element_type=jnp.float32
        )
        grad_probs = jnp.einsum(
            "sphe,skhe->shpk", grad_attn, values_blk, preferred_element_type=jnp.float32
        )
        grad_scores = (weights * (grad_probs - delta[..., None])).astype(jnp.bfloat16)
        grad_query = grad_query + score_scale * jnp.einsum(
            "shpk,skhe->sphe", grad_scores, keys_blk, preferred_element_type=jnp.float32
        )
        key_part = score_scale * jnp.einsum(
            "shpk,sphe->skhe", grad_scores, query_low, preferred_element_type=jnp.float32
        )
        grad_key = lax.dynamic_update_slice_in_dim(grad_key, key_part, offset, 1)
        grad_value = lax.dynamic_update_slice_in_dim(grad_value, value_part, offset, 1)
        return ((grad_query, grad_key, grad_value), None)

    initial = (
        jnp.zeros(query_low.shape, jnp.float32),
        jnp.zeros(key_all.shape, jnp.float32),
        jnp.zeros(value_all.shape, jnp.float32),
    )
    result, unused = lax.scan(backward_block_step, initial, jnp.arange(blocks))
    return result


def body(
    tokens,
    grad_out,
    timestep,
    w_time,
    b_time,
    ln1_gain,
    ln1_bias,
    w_qkv,
    b_query,
    b_value,
    w_out,
    b_out,
    ln2_gain,
    ln2_bias,
    w_up,
    b_up,
    w_down,
    b_down,
):
    (
        time_full,
        time_bias,
        gain_one,
        bias_one,
        qkv_full,
        query_bias,
        value_bias,
        out_full,
        out_bias,
        gain_two,
        bias_two,
        up_full,
        up_bias,
        down_full,
        down_bias,
    ) = (
        lax.all_gather(w_time, "seq", axis=0, tiled=True),
        lax.all_gather(b_time, "seq", axis=0, tiled=True),
        lax.all_gather(ln1_gain, "seq", axis=0, tiled=True),
        lax.all_gather(ln1_bias, "seq", axis=0, tiled=True),
        lax.all_gather(w_qkv, "seq", axis=0, tiled=True),
        lax.all_gather(b_query, "seq", axis=0, tiled=True),
        lax.all_gather(b_value, "seq", axis=0, tiled=True),
        lax.all_gather(w_out, "seq", axis=0, tiled=True),
        lax.all_gather(b_out, "seq", axis=0, tiled=True),
        lax.all_gather(ln2_gain, "seq", axis=0, tiled=True),
        lax.all_gather(ln2_bias, "seq", axis=0, tiled=True),
        lax.all_gather(w_up, "seq", axis=0, tiled=True),
        lax.all_gather(b_up, "seq", axis=0, tiled=True),
        lax.all_gather(w_down, "seq", axis=0, tiled=True),
        lax.all_gather(b_down, "seq", axis=0, tiled=True),
    )
    seq_count, piece_len, model_width = tokens.shape
    score_scale = 1.0 / math.sqrt(HEAD_DIM)
    split_shape = (seq_count, piece_len, HEADS, HEAD_DIM)
    flat_shape = (seq_count, piece_len, model_width)
    sinus_low = sinusoid(timestep, model_width).astype(jnp.bfloat16)
    time_embed = jnp.dot(
        sinus_low, time_full, preferred_element_type=jnp.float32
    ) + time_bias.astype(jnp.float32)
    hidden = tokens.astype(jnp.float32) + time_embed[:, None, :]
    attn_in = layer_norm(hidden, gain_one.astype(jnp.float32), bias_one.astype(jnp.float32)).astype(
        jnp.bfloat16
    )
    qkv_bias = jnp.concatenate([query_bias, jnp.zeros_like(query_bias), value_bias]).astype(
        jnp.float32
    )
    projected = (
        jnp.einsum("spd,de->spe", attn_in, qkv_full, preferred_element_type=jnp.float32) + qkv_bias
    )
    query_low = projected[..., :model_width].astype(jnp.bfloat16).reshape(split_shape)
    key_low = (
        projected[..., model_width : 2 * model_width].astype(jnp.bfloat16).reshape(split_shape)
    )
    value_low = projected[..., 2 * model_width :].astype(jnp.bfloat16).reshape(split_shape)
    key_all, value_all = (
        lax.all_gather(key_low, "ctx", axis=1, tiled=True),
        lax.all_gather(value_low, "ctx", axis=1, tiled=True),
    )
    block_len = min(key_all.shape[1], block_keys)
    log_totals = softmax_totals(query_low, key_all, score_scale, block_len)
    attn = attend(query_low, key_all, value_all, log_totals, score_scale, block_len)
    attn_low = attn.reshape(flat_shape).astype(jnp.bfloat16)
    hidden_two = (
        hidden
        + jnp.einsum("spd,de->spe", attn_low, out_full, preferred_element_type=jnp.float32)
        + out_bias.astype(jnp.float32)
    )
    mlp_in = layer_norm(
        hidden_two, gain_two.astype(jnp.float32), bias_two.astype(jnp.float32)
    ).astype(jnp.bfloat16)
    pre_act = jnp.einsum(
        "spd,df->spf", mlp_in, up_full, preferred_element_type=jnp.float32
    ) + up_bias.astype(jnp.float32)
    act_low = gelu_exact(pre_act).astype(jnp.bfloat16)
    output = (
        hidden_two
        + jnp.einsum("spf,fd->spd", act_low, down_full, preferred_element_type=jnp.float32)
        + down_bias.astype(jnp.float32)
    ).astype(jnp.bfloat16)
    qkv_back, out_back, up_back, down_back, gain_one_back, gain_two_back = (
        lax.all_gather(w_qkv, "seq", axis=0, tiled=True),
        lax.all_gather(w_out, "seq", axis=0, tiled=True),
        lax.all_gather(w_up, "seq", axis=0, tiled=True),
        lax.all_gather(w_down, "seq", axis=0, tiled=True),
        lax.all_gather(ln1_gain, "seq", axis=0, tiled=True),
        lax.all_gather(ln2_gain, "seq", axis=0, tiled=True),
    )
    grad_w_down = jnp.einsum("spf,spd->fd", act_low, grad_out, preferred_element_type=jnp.float32)
    grad_b_down = token_sum(grad_out)
    grad_act = jnp.einsum("spd,fd->spf", grad_out, down_back, preferred_element_type=jnp.float32)
    unused, gelu_pull = jax.vjp(gelu_exact, pre_act)
    grad_pre = gelu_pull(grad_act)[0].astype(jnp.bfloat16)
    grad_w_up = jnp.einsum("spd,spf->df", mlp_in, grad_pre, preferred_element_type=jnp.float32)
    grad_b_up = token_sum(grad_pre)
    grad_mlp = jnp.einsum("spf,df->spd", grad_pre, up_back, preferred_element_type=jnp.float32)
    unused, norm_two_pull = jax.vjp(
        layer_norm, hidden_two, gain_two_back.astype(jnp.float32), bias_two.astype(jnp.float32)
    )
    grad_hidden_two, grad_ln2_gain, grad_ln2_bias = norm_two_pull(grad_mlp)
    grad_hidden_two = grad_hidden_two + grad_out.astype(jnp.float32)
    grad_branch = grad_hidden_two.astype(jnp.bfloat16)
    grad_w_out = jnp.einsum(
        "spd,spe->de", attn_low, grad_branch, preferred_element_type=jnp.float32
    )
    grad_b_out = token_sum(grad_branch)
    grad_attn = (
        jnp.einsum("spe,de->spd", grad_branch, out_back, preferred_element_type=jnp.float32)
        .astype(jnp.bfloat16)
        .reshape(split_shape)
    )
    delta = jnp.transpose(jnp.sum(grad_attn.astype(jnp.float32) * attn, axis=-1), (0, 2, 1))
    grad_query, key_terms, value_terms = backward_reduce(
        query_low, key_all, value_all, grad_attn, log_totals, delta, score_scale, block_len
    )
    grad_key, grad_value = (
        lax.psum_scatter(key_terms, "ctx", scatter_dimension=1, tiled=True),
        lax.psum_scatter(value_terms, "ctx", scatter_dimension=1, tiled=True),
    )
    grad_qkv = jnp.concatenate(
        [
            grad_query.reshape(flat_shape),
            grad_key.reshape(flat_shape),
            grad_value.reshape(flat_shape),
        ],
        axis=-1,
    ).astype(jnp.bfloat16)
    grad_w_qkv = jnp.einsum("spd,spe->de", attn_in, grad_qkv, preferred_element_type=jnp.float32)
    grad_b_query = token_sum(grad_qkv[..., :model_width])
    grad_b_value = token_sum(grad_qkv[..., 2 * model_width :])
    grad_norm = jnp.einsum("spe,de->spd", grad_qkv, qkv_back, preferred_element_type=jnp.float32)
    unused, norm_one_pull = jax.vjp(
        layer_norm, hidden, gain_one_back.astype(jnp.float32), bias_one.astype(jnp.float32)
    )
    grad_hidden_part, grad_ln1_gain, grad_ln1_bias = norm_one_pull(grad_norm)
    grad_hidden = grad_hidden_two + grad_hidden_part
    grad_tokens = grad_hidden.astype(jnp.bfloat16)
    grad_embed = jnp.sum(grad_hidden, axis=1)
    grad_w_time = jnp.einsum(
        "sd,se->de", sinus_low.astype(jnp.float32), grad_embed, precision=lax.Precision.HIGHEST
    )
    grad_b_time = jnp.sum(grad_embed, axis=0)
    shares = (
        lax.psum_scatter(
            grad_w_time.astype(jnp.bfloat16), "seq", scatter_dimension=0, tiled=True
        ).astype(jnp.float32),
        lax.psum_scatter(
            grad_b_time.astype(jnp.bfloat16), "seq", scatter_dimension=0, tiled=True
        ).astype(jnp.float32),
        lax.psum_scatter(
            grad_ln1_gain.astype(jnp.bfloat16), "seq", scatter_dimension=0, tiled=True
        ).astype(jnp.float32),
        lax.psum_scatter(
            grad_ln1_bias.astype(jnp.bfloat16), "seq", scatter_dimension=0, tiled=True
        ).astype(jnp.float32),
        lax.psum_scatter(
            grad_w_qkv.astype(jnp.bfloat16), "seq", scatter_dimension=0, tiled=True
        ).astype(jnp.float32),
        lax.psum_scatter(
            grad_b_query.astype(jnp.bfloat16), "seq", scatter_dimension=0, tiled=True
        ).astype(jnp.float32),
        lax.psum_scatter(
            grad_b_value.astype(jnp.bfloat16), "seq", scatter_dimension=0, tiled=True
        ).astype(jnp.float32),
        lax.psum_scatter(
            grad_w_out.astype(jnp.bfloat16), "seq", scatter_dimension=0, tiled=True
        ).astype(jnp.float32),
        lax.psum_scatter(
            grad_b_out.astype(jnp.bfloat16), "seq", scatter_dimension=0, tiled=True
        ).astype(jnp.float32),
        lax.psum_scatter(
            grad_ln2_gain.astype(jnp.bfloat16), "seq", scatter_dimension=0, tiled=True
        ).astype(jnp.float32),
        lax.psum_scatter(
            grad_ln2_bias.astype(jnp.bfloat16), "seq", scatter_dimension=0, tiled=True
        ).astype(jnp.float32),
        lax.psum_scatter(
            grad_w_up.astype(jnp.bfloat16), "seq", scatter_dimension=0, tiled=True
        ).astype(jnp.float32),
        lax.psum_scatter(
            grad_b_up.astype(jnp.bfloat16), "seq", scatter_dimension=0, tiled=True
        ).astype(jnp.float32),
        lax.psum_scatter(
            grad_w_down.astype(jnp.bfloat16), "seq", scatter_dimension=0, tiled=True
        ).astype(jnp.float32),
        lax.psum_scatter(
            grad_b_down.astype(jnp.bfloat16), "seq", scatter_dimension=0, tiled=True
        ).astype(jnp.float32),
    )
    (
        total_w_time,
        total_b_time,
        total_ln1_gain,
        total_ln1_bias,
        total_w_qkv,
        total_b_query,
        total_b_value,
        total_w_out,
        total_b_out,
        total_ln2_gain,
        total_ln2_bias,
        total_w_up,
        total_b_up,
        total_w_down,
        total_b_down,
    ) = lax.psum(
        (
            shares[0],
            shares[1],
            shares[2],
            shares[3],
            shares[4],
            shares[5],
            shares[6],
            shares[7],
            shares[8],
            shares[9],
            shares[10],
            shares[11],
            shares[12],
            shares[13],
            shares[14],
        ),
        "ctx",
    )
    return (
        output,
        grad_tokens,
        total_w_time,
        total_b_time,
        total_ln1_gain,
        total_ln1_bias,
        total_w_qkv,
        total_b_query,
        total_b_value,
        total_w_out,
        total_b_out,
        total_ln2_gain,
        total_ln2_bias,
        total_w_up,
        total_b_up,
        total_w_down,
        total_b_down,
    )


def solution(mesh):
    placed = (
        P("seq", "ctx", None),
        P("seq", "ctx", None),
        P("seq"),
        P("seq", None),
        P("seq"),
        P("seq"),
        P("seq"),
        P("seq", None),
        P("seq"),
        P("seq"),
        P("seq", None),
        P("seq"),
        P("seq"),
        P("seq"),
        P("seq", None),
        P("seq"),
        P("seq", None),
        P("seq"),
    )
    return jax.shard_map(
        body,
        mesh=mesh,
        in_specs=placed,
        out_specs=(
            P("seq", "ctx", None),
            P("seq", "ctx", None),
            P("seq", None),
            P("seq"),
            P("seq"),
            P("seq"),
            P("seq", None),
            P("seq"),
            P("seq"),
            P("seq", None),
            P("seq"),
            P("seq"),
            P("seq"),
            P("seq", None),
            P("seq"),
            P("seq", None),
            P("seq"),
        ),
        check_vma=False,
    )
```

profile of v0, /device:TPU:0, one launch (start us, length us, event | category | flops | bytes accessed | tf_op | source)
XLA Modules:
  0.0 1070.9 jit_solution(3242901366263145930)
XLA Ops:
  17.4 12.9 %all-reduce.21 = (bf16[768]{0:T(1024)(128)(2,1)S(1)}, bf16[768]{0:T(1024)(128)(2,1)S(1)}, bf16[768]{0:T(1024)(128)(2,1)S(1)}, bf16[768]{0:T(1024)(128)(2,1)S(1)}...) all-reduce(bf16[768]{0:T(1024)(128)(2,1)S(1)} %dynamic-update-slice, ...), channel_id=1, replica_groups=mesh['seq'=4,'ctx'=8] {'seq'}, use_global_device_ids=true, to_apply=%add.4 | all-reduce | flops 6144 | bytes 24576
  31.3 1.5 convolution_add_fusion.2
  34.3 28.1 %all-gather.11.cloned.1.call-done = bf16[768,2304]{1,0:T(8,128)(2,1)} async-done(((bf16[192,2304]{1,0:T(8,128)(2,1)}), bf16[768,2304]{1,0:T(8,128)(2,1)}) %all-gather.11.cloned.1.call-update) | async-done | bytes 3538960 | tf_op jit(solution)/shard_map/all_gather | solution.py:167
  62.4 3.2 fusion.12
  69.6 5.3 all-gather
  75.2 54.6 %all-gather.15.cloned.1.call-done = bf16[2,1024,12,64]{1,3,2,0:T(8,128)(2,1)} async-done(((bf16[2,128,12,64]{1,3,2,0:T(8,128)(2,1)}), bf16[2,1024,12,64]{1,3,2,0:T(8,128)(2,1)}) %all-gather.15.cloned.1.call-update) | async-done | bytes 3145744 | tf_op jit(solution)/shard_map/all_gather | solution.py:203
  129.8 3.8 multiply_reduce_fusion
  133.7 2.7 exponential_reduce_fusion
  136.4 1.8 copy-done
  138.2 55.4 %all-gather.13.cloned.1.call-done = bf16[2,1024,12,64]{1,3,2,0:T(8,128)(2,1)} async-done(((bf16[2,128,12,64]{1,3,2,0:T(8,128)(2,1)}), bf16[2,1024,12,64]{1,3,2,0:T(8,128)(2,1)}) %all-gather.13.cloned.1.call-update) | async-done | bytes 3145744 | tf_op jit(solution)/shard_map/all_gather | solution.py:204
  193.6 8.9 fusion.64
  202.5 8.2 all-gather.17.cloned.1.call-done
  210.7 1.9 fusion.65
  212.8 36.8 %all-gather.19.cloned.1.call-done = bf16[768,3072]{1,0:T(8,128)(2,1)} async-done(((bf16[192,3072]{1,0:T(8,128)(2,1)}), bf16[768,3072]{1,0:T(8,128)(2,1)}) %all-gather.19.cloned.1.call-update) | async-done | bytes 4718608 | tf_op jit(solution)/shard_map/all_gather | solution.py:174
  249.6 4.8 fusion.43
  254.4 1.7 copy-done.11
  256.1 8.2 multiply_convert_fusion.1
  264.3 24.4 %all-gather.21.cloned.1.call-done = bf16[3072,768]{1,0:T(8,128)(2,1)} async-done(((bf16[768,768]{1,0:T(8,128)(2,1)}), bf16[3072,768]{1,0:T(8,128)(2,1)}) %all-gather.21.cloned.1.call-update) | async-done | bytes 4718608 | tf_op jit(solution)/shard_map/all_gather | solution.py:176
  288.7 6.9 fusion.66
  295.6 5.1 multiply_reduce_fusion.1
  304.7 1.9 copy.62
  306.7 1.3 multiply_reduce_fusion.4
  308.0 7.7 multiply_convert_fusion
  315.8 2.7 copy-done.1
  318.5 3.7 multiply_bitcast_fusion
  322.2 9.9 convolution_bitcast_fusion
  332.2 2.6 bitcast_convert_fusion.3
  334.9 5.1 bitcast_convert_fusion.1
  340.4 4.6 bitcast_convert_fusion
  345.1 7.4 bitcast_reduce_fusion
  352.5 2.0 copy.63
  354.5 86.1 %reduce-scatter.8.cloned.1.call-done = f32[2,128,12,64]{1,3,2,0:T(8,128)} async-done(((f32[2,1024,12,64]{1,3,2,0:T(8,128)}), f32[2,128,12,64]{1,3,2,0:T(8,128)}) %reduce-scatter.8.cloned.1.call-update) | async-done | bytes 786448 | tf_op jit(solution)/shard_map/reduce_scatter | solution.py:263
  440.7 1.9 convert.33
  442.6 1.9 copy.64
  444.5 117.3 %reduce-scatter.10.cloned.1.call-done = f32[2,128,12,64]{1,3,2,0:T(8,128)} async-done(((f32[2,1024,12,64]{1,3,2,0:T(8,128)}), f32[2,128,12,64]{1,3,2,0:T(8,128)}) %reduce-scatter.10.cloned.1.call-update) | async-done | bytes 786448 | tf_op jit(solution)/shard_map/reduce_scatter | solution.py:264
  561.8 2.5 fusion.59
  564.3 1.9 copy.65
  566.3 4.2 fusion.54
  573.4 2.1 convolution_convert_fusion
  575.6 4.1 bitcast_convert_fusion.2
  581.6 8.1 reduce-scatter.16.cloned.1.call-done
  589.7 50.6 %reduce-scatter.18.cloned.1.call-done = bf16[192,3072]{1,0:T(8,128)(2,1)} async-done(((bf16[768,3072]{1,0:T(8,128)(2,1)}), bf16[192,3072]{1,0:T(8,128)(2,1)}) %reduce-scatter.18.cloned.1.call-update) | async-done | bytes 1179664 | tf_op jit(solution)/shard_map/reduce_scatter | solution.py:323
  640.3 50.3 %reduce-scatter.20.cloned.1.call-done = bf16[768,768]{1,0:T(8,128)(2,1)} async-done(((bf16[3072,768]{1,0:T(8,128)(2,1)}), bf16[768,768]{1,0:T(8,128)(2,1)}) %reduce-scatter.20.cloned.1.call-update) | async-done | bytes 1179664 | tf_op jit(solution)/shard_map/reduce_scatter | solution.py:329
  690.7 10.3 all-reduce.20
  701.5 4.6 fusion.31
  706.1 13.6 %reduce-scatter.12.cloned.1.call-done = bf16[192,768]{1,0:T(8,128)(2,1)} async-done(((bf16[768,768]{1,0:T(8,128)(2,1)}), bf16[192,768]{1,0:T(8,128)(2,1)}) %reduce-scatter.12.cloned.1.call-update) | async-done | bytes 294928 | tf_op jit(solution)/shard_map/reduce_scatter | solution.py:290
  719.7 42.9 %reduce-scatter.14.cloned.1.call-done = bf16[192,2304]{1,0:T(8,128)(2,1)} async-done(((bf16[768,2304]{1,0:T(8,128)(2,1)}), bf16[192,2304]{1,0:T(8,128)(2,1)}) %reduce-scatter.14.cloned.1.call-update) | async-done | bytes 884752 | tf_op jit(solution)/shard_map/reduce_scatter | solution.py:302
  762.6 301.4 %all-reduce.23 = (f32[192,768]{1,0:T(8,128)}, f32[192]{0:T(256)}, f32[192]{0:T(256)}, f32[192]{0:T(256)}, f32[192,2304]{1,0:T(8,128)}, /*index=5*/f32[192]{0:T(2...) all-reduce(bf16[192,768]{1,0:T(8,128)(2,1)} %reduce-scatter.12.clon, ...), channel_id=1, replica_groups=mesh['seq'=4,'ctx'=8] {'ctx'}, use_global_device_ids=true, to_apply=%region_15.16 | all-reduce | flops 1919424 | bytes 11521536 | tf_op jit(solution)/shard_map/psum | solution.py:352
  (195 shorter events, 24.7 us)
Async XLA Ops:
  7.2 26.8 %copy-start.2 = (bf16[2,128,768]{2,1,0:T(8,128)(2,1)S(1)}, bf16[2,128,768]{2,1,0:T(8,128)(2,1)}, u32[]{:S(2)}) copy-start(bf16[2,128,768]{2,1,0:T(8,128)(2,1)} %param.18) | copy-start | bytes 1179652
  7.2 24.1 %all-gather.9.cloned.1.call-start = ((), (), s32[]{:S(2)}) async-start(), calls=%async_computation.7 | async-start | bytes 1474560 | tf_op jit(solution)/shard_map/all_gather | solution.py:163
  7.9 54.4 %all-gather.11.cloned.1.call-start = ((), (), s32[]{:S(2)}) async-start(), calls=%async_computation.8 | async-start | bytes 4423680 | tf_op jit(solution)/shard_map/all_gather | solution.py:167
  8.7 121.1 %all-gather.15.cloned.1.call-start = ((), (), s32[]{:S(2)}) async-start(), calls=%async_computation.10 | async-start | bytes 3538944 | tf_op jit(solution)/shard_map/all_gather | solution.py:203
  31.0 31.3 %copy-start.22 = (f32[768]{0:T(1024)}, f32[768]{0:T(1024)S(1)}, u32[]{:S(2)}) copy-start(f32[768]{0:T(1024)S(1)} %convert_element_type.187) | copy-start | bytes 9220
  31.0 31.3 %copy-start.47 = (f32[768]{0:T(1024)}, f32[768]{0:T(1024)S(1)}, u32[]{:S(2)}) copy-start(f32[768]{0:T(1024)S(1)} %convert_element_type.188) | copy-start | bytes 9220
  31.2 31.1 %copy-start.32 = (bf16[2,384]{1,0:T(2,128)(2,1)}, bf16[2,384]{1,0:T(2,128)(2,1)S(1)}, u32[]{:S(2)}) copy-start(bf16[2,384]{1,0:T(2,128)(2,1)S(1)} %get-tuple-element.139) | copy-start | bytes 4612
  31.2 31.1 %copy-start.34 = (bf16[2,384]{1,0:T(2,128)(2,1)}, bf16[2,384]{1,0:T(2,128)(2,1)S(1)}, u32[]{:S(2)}) copy-start(bf16[2,384]{1,0:T(2,128)(2,1)S(1)} %get-tuple-element.140) | copy-start | bytes 4612
  32.8 177.9 %copy-start.16 = (f32[2,768]{1,0:T(2,128)}, f32[2,768]{1,0:T(2,128)S(1)}, u32[]{:S(2)}) copy-start(f32[2,768]{1,0:T(2,128)S(1)} %convolution_add_fusion.2) | copy-start | bytes 18436
  34.0 28.3 %copy-start.26 = (f32[2,128]{1,0:T(2,128)}, f32[2,128]{1,0:T(2,128)S(1)}, u32[]{:S(2)}) copy-start(f32[2,128]{1,0:T(2,128)S(1)} %broadcast_multiply_fusion.1) | copy-start | bytes 3076
  34.2 28.1 %copy-start.38 = (f32[2,128]{1,0:T(2,128)}, f32[2,128]{1,0:T(2,128)S(1)}, u32[]{:S(2)}) copy-start(f32[2,128]{1,0:T(2,128)S(1)} %multiply_reduce_fusion.7) | copy-start | bytes 3076
  34.3 28.1 %copy-start.36 = (f32[2,128]{1,0:T(2,128)}, f32[2,128]{1,0:T(2,128)S(1)}, u32[]{:S(2)}) copy-start(f32[2,128]{1,0:T(2,128)S(1)} %fusion.48) | copy-start | bytes 3076
  66.6 127.0 %all-gather.13.cloned.1.call-start = ((), (), s32[]{:S(2)}) async-start(), calls=%async_computation.9 | async-start | bytes 3538944 | tf_op jit(solution)/shard_map/all_gather | solution.py:204
  67.6 143.1 %all-gather.17.cloned.1.call-start = ((), (), s32[]{:S(2)}) async-start(), calls=%async_computation.11 | async-start | bytes 1474560 | tf_op jit(solution)/shard_map/all_gather | solution.py:170
  68.2 181.4 %all-gather.19.cloned.1.call-start = ((), (), s32[]{:S(2)}) async-start(), calls=%async_computation.12 | async-start | bytes 5898240 | tf_op jit(solution)/shard_map/all_gather | solution.py:174
  68.8 219.9 %all-gather.21.cloned.1.call-start = ((), (), s32[]{:S(2)}) async-start(), calls=%async_computation.13 | async-start | bytes 5898240 | tf_op jit(solution)/shard_map/all_gather | solution.py:176
  69.5 371.1 %reduce-scatter.8.cloned.1.call-start = ((), (), s32[]{:S(2)}) async-start(), calls=%async_computation.14 | async-start | bytes 7077888 | tf_op jit(solution)/shard_map/reduce_scatter | solution.py:263
  69.6 226.0 %copy-start.18 = (f32[768]{0:T(1024)}, f32[768]{0:T(1024)S(1)}, u32[]{:S(2)}) copy-start(f32[768]{0:T(1024)S(1)} %convert_element_type.195) | copy-start | bytes 9220
  69.6 180.0 %copy-start.20 = (f32[768]{0:T(1024)}, f32[768]{0:T(1024)S(1)}, u32[]{:S(2)}) copy-start(f32[768]{0:T(1024)S(1)} %convert_element_type.196) | copy-start | bytes 9220
  75.2 58.4 %copy-start.3 = (bf16[2,128,768]{1,2,0:T(8,128)(2,1)}, bf16[2,128,768]{1,2,0:T(8,128)(2,1)S(1)}, u32[]{:S(2)}) copy-start(bf16[2,128,768]{1,2,0:T(8,128)(2,1)S(1)} %copy.59) | copy-start | bytes 1179652
  202.5 51.9 %copy-start.10 = (bf16[2,128,12,64]{1,3,2,0:T(8,128)(2,1)}, bf16[2,128,12,64]{1,3,2,0:T(8,128)(2,1)S(1)}, u32[]{:S(2)}) copy-start(bf16[2,128,12,64]{1,3,2,0:T(8,128)(2,1)S(1)} %get-tuple-element.145) | copy-start | bytes 1179652
  212.6 83.0 %copy-start.24 = (f32[2,128]{1,0:T(2,128)}, f32[2,128]{1,0:T(2,128)S(1)}, u32[]{:S(2)}) copy-start(f32[2,128]{1,0:T(2,128)S(1)} %broadcast_multiply_fusion) | copy-start | bytes 3076
  212.8 82.8 %copy-start.30 = (f32[2,128]{1,0:T(2,128)}, f32[2,128]{1,0:T(2,128)S(1)}, u32[]{:S(2)}) copy-start(f32[2,128]{1,0:T(2,128)S(1)} %fusion.49) | copy-start | bytes 3076
  256.1 32.6 %copy-start.6 = (bf16[2,128,768]{2,1,0:T(8,128)(2,1)S(1)}, bf16[2,128,768]{2,1,0:T(8,128)(2,1)}, u32[]{:S(2)}) copy-start(bf16[2,128,768]{2,1,0:T(8,128)(2,1)} %param.19) | copy-start | bytes 1179652
  295.6 5.1 copy-start.12
  295.6 6.3 copy-start.7
  308.0 10.5 copy-start.4
  322.1 239.6 %reduce-scatter.10.cloned.1.call-start = ((), (), s32[]{:S(2)}) async-start(), calls=%async_computation.15 | async-start | bytes 7077888 | tf_op jit(solution)/shard_map/reduce_scatter | solution.py:264
  332.2 257.5 %reduce-scatter.16.cloned.1.call-start = ((), (), s32[]{:S(2)}) async-start(), calls=%async_computation.18 | async-start | bytes 1474560 | tf_op jit(solution)/shard_map/reduce_scatter | solution.py:311
  334.8 305.5 %reduce-scatter.18.cloned.1.call-start = ((), (), s32[]{:S(2)}) async-start(), calls=%async_computation.19 | async-start | bytes 5898240 | tf_op jit(solution)/shard_map/reduce_scatter | solution.py:323
  340.1 350.5 %reduce-scatter.20.cloned.1.call-start = ((), (), s32[]{:S(2)}) async-start(), calls=%async_computation.20 | async-start | bytes 5898240 | tf_op jit(solution)/shard_map/reduce_scatter | solution.py:329
  345.0 374.7 %reduce-scatter.12.cloned.1.call-start = ((), (), s32[]{:S(2)}) async-start(), calls=%async_computation.16 | async-start | bytes 1474560 | tf_op jit(solution)/shard_map/reduce_scatter | solution.py:290
  352.5 213.7 %copy-start.17 = (f32[2,768]{1,0:T(2,128)S(1)}, f32[2,768]{1,0:T(2,128)}, u32[]{:S(2)}) copy-start(f32[2,768]{1,0:T(2,128)} %copy-done.16) | copy-start | bytes 18436
  352.5 213.7 %copy-start.23 = (f32[768]{0:T(1024)S(1)}, f32[768]{0:T(1024)}, u32[]{:S(2)}) copy-start(f32[768]{0:T(1024)} %copy-done.22) | copy-start | bytes 9220
  352.5 213.7 %copy-start.27 = (f32[2,128]{1,0:T(2,128)S(1)}, f32[2,128]{1,0:T(2,128)}, u32[]{:S(2)}) copy-start(f32[2,128]{1,0:T(2,128)} %copy-done.26) | copy-start | bytes 3076
  566.3 5.3 copy-start.8
  566.3 5.3 copy-start.41
  575.6 187.0 %reduce-scatter.14.cloned.1.call-start = ((), (), s32[]{:S(2)}) async-start(), calls=%async_computation.17 | async-start | bytes 4423680 | tf_op jit(solution)/shard_map/reduce_scatter | solution.py:302
  579.8 110.8 %copy-start.29 = (bf16[12,64]{1,0:T(8,128)(2,1)S(1)}, bf16[12,64]{1,0:T(8,128)(2,1)}, u32[]{:S(2)}) copy-start(bf16[12,64]{1,0:T(8,128)(2,1)} %get-tuple-element.129) | copy-start | bytes 4612
  579.8 110.9 %copy-start.42 = (bf16[768]{0:T(1024)(128)(2,1)S(1)}, bf16[768]{0:T(1024)(128)(2,1)}, u32[]{:S(2)}) copy-start(bf16[768]{0:T(1024)(128)(2,1)} %get-tuple-element.127) | copy-start | bytes 4612
  579.8 110.9 %copy-start.43 = (bf16[768]{0:T(1024)(128)(2,1)S(1)}, bf16[768]{0:T(1024)(128)(2,1)}, u32[]{:S(2)}) copy-start(bf16[768]{0:T(1024)(128)(2,1)} %get-tuple-element.138) | copy-start | bytes 4612
  579.8 110.9 %copy-start.44 = (bf16[768]{0:T(1024)(128)(2,1)S(1)}, bf16[768]{0:T(1024)(128)(2,1)}, u32[]{:S(2)}) copy-start(bf16[768]{0:T(1024)(128)(2,1)} %get-tuple-element.84) | copy-start | bytes 4612
  579.8 110.9 %copy-start.45 = (bf16[768]{0:T(1024)(128)(2,1)S(1)}, bf16[768]{0:T(1024)(128)(2,1)}, u32[]{:S(2)}) copy-start(bf16[768]{0:T(1024)(128)(2,1)} %get-tuple-element.89) | copy-start | bytes 4612
  579.8 110.9 %copy-start.46 = (bf16[3072]{0:T(1024)(128)(2,1)S(1)}, bf16[3072]{0:T(1024)(128)(2,1)}, u32[]{:S(2)}) copy-start(bf16[3072]{0:T(1024)(128)(2,1)} %get-tuple-element.154) | copy-start | bytes 18436
  579.8 110.9 %copy-start.49 = (bf16[768]{0:T(1024)(128)(2,1)S(1)}, bf16[768]{0:T(1024)(128)(2,1)}, u32[]{:S(2)}) copy-start(bf16[768]{0:T(1024)(128)(2,1)} %get-tuple-element.72) | copy-start | bytes 4612
  579.8 110.9 %copy-start.50 = (bf16[768]{0:T(1024)(128)(2,1)S(1)}, bf16[768]{0:T(1024)(128)(2,1)}, u32[]{:S(2)}) copy-start(bf16[768]{0:T(1024)(128)(2,1)} %get-tuple-element.86) | copy-start | bytes 4612
  579.8 110.9 %copy-start.51 = (bf16[768]{0:T(1024)(128)(2,1)S(1)}, bf16[768]{0:T(1024)(128)(2,1)}, u32[]{:S(2)}) copy-start(bf16[768]{0:T(1024)(128)(2,1)} %get-tuple-element.87) | copy-start | bytes 4612
  701.5 61.1 %copy-start.15 = (bf16[192,768]{1,0:T(8,128)(2,1)S(1)}, bf16[192,768]{1,0:T(8,128)(2,1)}, u32[]{:S(2)}) copy-start(bf16[192,768]{1,0:T(8,128)(2,1)} %reduce-scatter.16.cloned.1.call-done) | copy-start | bytes 884740
  (19 other events, 51.8 us)
Sparse Core Ops, SparseCore 0:
  9.6 20.3 all-gather.8
  31.6 30.7 all-gather.10
  66.7 63.0 all-gather.14
  132.3 61.2 all-gather.12
  195.0 15.6 all-gather.16
  212.1 37.4 all-gather.18
  251.2 37.4 all-gather.20
  322.3 118.3 reduce-scatter.7
  444.3 117.4 reduce-scatter.9
  564.8 24.8 reduce-scatter.15
  592.4 47.8 reduce-scatter.17
  642.7 47.8 reduce-scatter.19
  693.9 25.7 reduce-scatter.11
  722.1 40.4 reduce-scatter.13
where the time goes:
time: 1080 us; the launch traced here: 1070 us
  waiting for transfers between devices  580 us (54%)
  blocking collectives  330 us (31%)
  matrix products  93.5 us (9%)
  local copies, waits for them, and re-layouts  25.5 us (2%)
  other arithmetic  24.6 us (2%)
  between operations  17 us (2%)
    psum x1, blocking collectives, body(): lax.psum((shares[0], shares[1], shares[2], shares[3], shares[4], shares[5...  301 us
    reduce_scatter x1, waiting for transfers between devices, body(): lax.psum_scatter(value_terms, 'ctx', scatter_dimension=1, tiled=True)  117 us
    reduce_scatter x1, waiting for transfers between devices, body(): lax.psum_scatter(key_terms, 'ctx', scatter_dimension=1, tiled=True)  86.1 us
    all_gather x1, waiting for transfers between devices, body(): lax.all_gather(value_low, 'ctx', axis=1, tiled=True)  55.4 us
    all_gather x1, waiting for transfers between devices, body(): lax.all_gather(key_low, 'ctx', axis=1, tiled=True)  54.6 us
    reduce_scatter x1, waiting for transfers between devices, body(): lax.psum_scatter(grad_w_up.astype(jnp.bfloat16), 'seq', scatter_dimension...  50.6 us
    reduce_scatter x1, waiting for transfers between devices, body(): lax.psum_scatter(grad_w_down.astype(jnp.bfloat16), 'seq', scatter_dimensi...  50.3 us
    reduce_scatter x1, waiting for transfers between devices, body(): lax.psum_scatter(grad_w_qkv.astype(jnp.bfloat16), 'seq', scatter_dimensio...  42.9 us
  transfers between devices with their start and end apart: 14, of which 13 were waited for; matrix products, arithmetic and copies ran while one was open for 10% of the time, Pallas kernels for 0%

commit v1 on v0

--- a/solution.py
+++ b/solution.py
@@ -3,6 +3,9 @@
 import jax
 import jax.numpy as jnp
 from jax import lax
+from jax.experimental import pallas as pl
+from jax.experimental.pallas import tpu as pltpu
+from jax.sharding import Mesh
 from jax.sharding import PartitionSpec as P
 
 HEADS = 12
@@ -390,6 +393,633 @@
     )
 
 
+F32 = jnp.float32
+BF16 = jnp.bfloat16
+VMEM_BYTES = 56 * 1024 * 1024
+RATE = 1.15e9
+
+
+def swap(value, axis):
+    return lax.ppermute(value, axis, [(0, 1), (1, 0)])
+
+
+def across(value):
+    return lax.ppermute(value, ("zl", "x"), [(i, i ^ 3) for i in range(4)])
+
+
+def pick(value, index):
+    return lax.dynamic_index_in_dim(value, index, 0, keepdims=False)
+
+
+def dot(left, right, left_dim=1, right_dim=0):
+    return lax.dot_general(
+        left, right, (((left_dim,), (right_dim,)), ((), ())), preferred_element_type=F32
+    )
+
+
+class Steps:
+    def __init__(self, ids):
+        self.ids = ids
+        self.last = None
+
+    def __call__(self, kernel, inputs, outputs, micros, scratch=(), behind=()):
+        behind = [*behind] + ([self.last] if self.last is not None else [])
+        shapes = [jax.ShapeDtypeStruct(shape, dtype) for shape, dtype in outputs]
+        count = 1 + len(inputs)
+
+        def run(*refs):
+            kernel(*refs[:count], *refs[count + len(behind) :])
+
+        results = pl.pallas_call(
+            run,
+            out_shape=shapes,
+            in_specs=[pl.BlockSpec(memory_space=pltpu.SMEM)]
+            + [pl.BlockSpec(memory_space=pltpu.VMEM)] * len(inputs)
+            + [pl.BlockSpec(memory_space=pl.ANY)] * len(behind),
+            out_specs=[pl.BlockSpec(memory_space=pltpu.VMEM)] * len(shapes),
+            scratch_shapes=list(scratch),
+            compiler_params=pltpu.CompilerParams(vmem_limit_bytes=VMEM_BYTES),
+            cost_estimate=pl.CostEstimate(
+                flops=int(micros * RATE), bytes_accessed=1, transcendentals=0
+            ),
+            name=kernel.__name__,
+        )(self.ids, *inputs, *behind)
+        self.last = results[0]
+        return results
+
+
+SEQ, MEMBER, HALF = 0, 1, 2
+
+
+def normalize(hidden):
+    center = hidden - jnp.mean(hidden, axis=-1, keepdims=True)
+    rstd = lax.rsqrt(jnp.mean(center * center, axis=-1, keepdims=True) + norm_eps)
+    return center * rstd, rstd
+
+
+def norm_back(e, x, r):
+    return r * (e - jnp.mean(e, -1, keepdims=True) - x * jnp.mean(e * x, -1, keepdims=True))
+
+
+def time_row(ids, te_a, te_b, vec):
+    at = pl.ds(2 * ids[SEQ] + ids[HALF], 1)
+    return te_a[at, :] + te_b[at, :] + vec[0:1, :]
+
+
+def token_kernel(ids, tokens, mine, far):
+    mine[...] = tokens[ids[HALF]]
+    far[...] = tokens[1 - ids[HALF]]
+
+
+def pick_kernel(ids, grad_out, far):
+    far[...] = grad_out[1 - ids[HALF]]
+
+
+def column_kernel(ids, w_qkv, out):
+    part = out.shape[1] // 3
+    width = w_qkv.shape[1] // 3
+    for member in range(4):
+
+        @pl.when(ids[MEMBER] == member)
+        def _():
+            for t in range(3):
+                at = t * width + member * part
+                out[:, t * part : (t + 1) * part] = w_qkv[:, at : at + part]
+
+
+def up_kernel(ids, w_up, own, y, c, yc):
+    ff = own.shape[1]
+    for ref, flip in ((own, 0), (y, 2), (c, 1), (yc, 3)):
+        ref[...] = w_up[:, pl.ds(pl.multiple_of((ids[SEQ] ^ flip) * ff, ff), ff)]
+
+
+def add_kernel(ids, left, right, out):
+    out[...] = left[...] + right[...]
+
+
+def own_kernel(ids, grad_out, far, own):
+    half = far.shape[0]
+    own[:half] = grad_out[ids[HALF]]
+    own[half:] = far[...]
+
+
+def second_kernel(ids, keep, recv, out):
+    out[...] = (keep[...] + recv[1].astype(F32)).astype(BF16)
+
+
+def total4_kernel(ids, a, b, c, d, out):
+    total = a[...].astype(F32) + b[...].astype(F32) + c[...].astype(F32) + d[...].astype(F32)
+    out[...] = total.astype(BF16)
+
+
+def both_kernel(ids, left, right, out):
+    out[...] = (left[...].astype(F32) + right[...].astype(F32)).astype(BF16)
+
+
+def chain_kernel(ids, keep, c, first, second):
+    first[...] = (keep[0].astype(F32) + c[0].astype(F32)).astype(BF16)
+    second[...] = (keep[1].astype(F32) + c[1].astype(F32)).astype(BF16)
+
+
+def join_kernel(ids, first, y, a, b, c, d, out):
+    rows = first.shape[0]
+    out[:rows] = (first[...].astype(F32) + y[...].astype(F32)).astype(BF16)
+    total = a[...].astype(F32) + b[...].astype(F32) + c[...].astype(F32) + d[...].astype(F32)
+    out[rows:] = total.astype(BF16)
+
+
+def attend_kernel(
+    ids, tok_own, tok_x, tok_z, tok_d, far_own, far_x, far_z, far_d, te_a, te_b, vec, small, wq_own, wq_y, wq_c, wq_yc,
+    attn_in, qkv_t, o_full, o_send, lse, w_t, w_rows,
+):
+    part = wq_own.shape[1] // 3
+    rows = wq_own.shape[0]
+    piece, width = tok_own.shape
+    own = 2 * piece
+    si, gi = ids[SEQ], ids[MEMBER]
+    for ref, flip in ((wq_own, 0), (wq_y, 2), (wq_c, 1), (wq_yc, 3)):
+        w_rows[si ^ flip] = ref[...]
+    for block in range(4):
+        w_t[:, block * rows : (block + 1) * rows] = w_rows[block].T
+    te_row = time_row(ids, te_a, te_b, vec)
+    gain, offset = vec[1:2, :], vec[2:3, :]
+    bias = small[gi].astype(F32).T
+    pairs = ((tok_own, far_own), (tok_x, far_x), (tok_z, far_z), (tok_d, far_d))
+    for block, (tok, far) in enumerate(pairs):
+        normed, _ = normalize(jnp.concatenate([tok[...], far[...]]).astype(F32) + te_row)
+        low = (normed * gain + offset).astype(BF16)
+        attn_in[block] = low
+        qkv = dot(w_t[...], low, 1, 1)
+        qkv_t[block, 0:part, :] = (qkv[:part] + bias[:, 3:4]).astype(BF16)
+        qkv_t[block, part : 2 * part, :] = qkv[part : 2 * part].astype(BF16)
+        qkv_t[block, 2 * part :, :] = (qkv[2 * part :] + bias[:, 4:5]).astype(BF16)
+
+    @pl.loop(0, part // HEAD_DIM)
+    def _(head):
+        at = pl.multiple_of(head * HEAD_DIM, HEAD_DIM)
+        k_t = jnp.concatenate([qkv_t[j, pl.ds(part + at, HEAD_DIM), :] for j in range(4)], 1)
+        v_t = jnp.concatenate([qkv_t[j, pl.ds(2 * part + at, HEAD_DIM), :] for j in range(4)], 1)
+        for block in range(4):
+            q_t = qkv_t[block, pl.ds(at, HEAD_DIM), :] * jnp.asarray(0.125, BF16)
+            scores = dot(k_t, q_t, 0, 0)
+            top = jnp.max(scores, 0, keepdims=True)
+            weights = jnp.exp(scores - top)
+            total = jnp.sum(weights, 0, keepdims=True)
+            attn = dot(v_t, weights.astype(BF16)) / total
+            o_full[block, pl.ds(at, HEAD_DIM), :] = attn
+            o_send[gi ^ block, pl.ds(at, HEAD_DIM), :] = attn.astype(BF16)
+            lse[head * 4 + block] = jnp.broadcast_to(top + jnp.log(total), (8, own))
+
+
+def branch_kernel(
+    ids, attn, w_out, tok_own, far_own, te_a, te_b, vec, mlp_in, hidden_two, a_own, a_y, a_c, a_yc
+):
+    rows = attn.shape[1]
+    te_row = time_row(ids, te_a, te_b, vec)
+    hidden = jnp.concatenate([tok_own[...], far_own[...]]).astype(F32) + te_row + vec[5:6, :]
+    for block in range(4):
+        hidden = hidden + dot(attn[block], w_out[block * rows : (block + 1) * rows, :], 0, 0)
+    hidden_two[...] = hidden
+    normed, _ = normalize(hidden)
+    mlp_in[...] = (normed * vec[6:7, :] + vec[7:8, :]).astype(BF16)
+    for ref, flip in ((a_own, 0), (a_y, 2), (a_c, 1), (a_yc, 3)):
+        ref[...] = attn[ids[SEQ] ^ flip]
+
+
+def feed_kernel(
+    ids, m_own, m_y, m_c, m_yc, go_all, u_own, u_y, u_c, u_yc, w_down, b_up,
+    gm_own, gm_pair, gm_send, out_own, out_pair, out_send, act_all, gp_all, w_up,
+):
+    si = ids[SEQ]
+    rows = u_own.shape[0]
+    for ref, flip in ((u_own, 0), (u_y, 2), (u_c, 1), (u_yc, 3)):
+        w_up[pl.ds(pl.multiple_of((si ^ flip) * rows, rows), rows), :] = ref[...]
+    for block, (ref, flip) in enumerate(((m_own, 0), (m_y, 2), (m_c, 1), (m_yc, 3))):
+        grad_out = go_all[si ^ flip]
+        pre = dot(ref[...], w_up[...]) + b_up[...]
+        cdf = 0.5 * (1.0 + lax.erf(pre * (0.5**0.5)))
+        act = (pre * cdf).astype(BF16)
+        grad_act = dot(grad_out, w_down[...], 1, 1)
+        slope = cdf + pre * (jnp.exp(-0.5 * pre * pre) * (0.5 / math.pi) ** 0.5)
+        grad_pre = (grad_act * slope).astype(BF16)
+        act_all[block] = act
+        gp_all[block] = grad_pre
+        gm = dot(grad_pre, w_up[...], 1, 1)
+        out = dot(act, w_down[...])
+        if block < 2:
+            (gm_own, gm_pair)[block][...] = gm
+            (out_own, out_pair)[block][...] = out
+        else:
+            gm_send[block - 2] = gm.astype(BF16)
+            out_send[block - 2] = out.astype(BF16)
+
+
+def feed_grad_kernel(
+    ids, m_own, m_y, m_c, m_yc, go_all, act_all, gp_all, d_own, d_x, d_z, d_d, u_own, u_x, u_z, u_d, grad
+):
+    si, gi = ids[SEQ], ids[MEMBER]
+    width = m_own.shape[1]
+    ff = act_all.shape[2]
+    part = ff // 4
+    rows = width // 4
+    fine = rows // 4
+    orders = ((m_own, 0), (m_y, 2), (m_c, 1), (m_yc, 3))
+    for s in range(4):
+        cols = slice(s * part, (s + 1) * part)
+        total = jnp.zeros((part, width), F32)
+        for block, (_, flip) in enumerate(orders):
+            total = total + dot(act_all[block, :, cols], go_all[si ^ flip], 0, 0)
+        grad[cols, :] = total.astype(BF16)
+    for ref, flip in ((d_own, 0), (d_x, 1), (d_z, 2), (d_d, 3)):
+        ref[:part, :] = grad[pl.ds(pl.multiple_of((gi ^ flip) * part, 16), part), :]
+    for s in range(4):
+        cols = slice(s * rows, (s + 1) * rows)
+        total = jnp.zeros((rows, ff), F32)
+        for block, (ref, _) in enumerate(orders):
+            total = total + dot(ref[:, cols], gp_all[block], 0, 0)
+        grad[cols, :] = total.astype(BF16)
+    for ref, flip in ((u_own, 0), (u_x, 1), (u_z, 2), (u_d, 3)):
+        for s in range(4):
+            ref[s] = grad[pl.ds(pl.multiple_of(s * rows + (gi ^ flip) * fine, 16), fine), :]
+    b_up = jnp.zeros((1, ff), F32)
+    b_down = jnp.zeros((1, width), F32)
+    for block in range(4):
+        b_up = b_up + jnp.sum(gp_all[block].astype(F32), 0, keepdims=True)
+        b_down = b_down + jnp.sum(go_all[block].astype(F32), 0, keepdims=True)
+    line = lax.broadcasted_iota(jnp.int32, (16, width), 0)
+    extra = jnp.where(line == 0, b_up, jnp.where(line == 1, b_down, 0.0))
+    for ref, flip in ((d_own, 0), (d_x, 1), (d_z, 2), (d_d, 3)):
+        ref[part:, :] = jnp.where(gi == flip, extra, 0.0).astype(BF16)
+
+
+def back_kernel(
+    ids, gm_keep, gm_c, gm_y, hidden_two, go_own, w_out, vec,
+    grad_two, branch, ga_send, sums,
+):
+    rows = w_out.shape[0] // 4
+    grad_mlp = gm_keep[...] + gm_c[0].astype(F32) + gm_y[...].astype(F32)
+    normed, rstd = normalize(hidden_two[...])
+    grad = go_own[...].astype(F32) + norm_back(grad_mlp * vec[6:7, :], normed, rstd)
+    grad_two[...] = grad
+    low = grad.astype(BF16)
+    branch[...] = low
+    for block in range(4):
+        ga_send[block] = dot(w_out[block * rows : (block + 1) * rows, :], low, 1, 1).astype(BF16)
+    sums[0:1, :] = jnp.sum(grad_mlp * normed, 0, keepdims=True)
+    sums[1:2, :] = jnp.sum(grad_mlp, 0, keepdims=True)
+    sums[2:3, :] = jnp.sum(low.astype(F32), 0, keepdims=True)
+    sums[3:4, :] = jnp.sum(grad, 0, keepdims=True)
+    sums[4:8, :] = jnp.zeros((4, sums.shape[1]), F32)
+
+
+def out_grad_kernel(ids, a_own, a_y, a_c, a_yc, branch, w_own, w_x, w_z, w_d, grads):
+    si, gi = ids[SEQ], ids[MEMBER]
+    narrow = w_own.shape[1]
+    fine = a_own.shape[0] // 4
+    third = fine // 3
+    grad = jnp.zeros((a_own.shape[0], branch.shape[2]), F32)
+    for ref, flip in ((a_own, 0), (a_y, 2), (a_c, 1), (a_yc, 3)):
+        grad = grad + dot(ref[...], branch[si ^ flip])
+    grads[...] = grad.astype(BF16)
+    for ref, flip in ((w_own, 0), (w_x, 1), (w_z, 2), (w_d, 3)):
+        lines = grads[pl.ds(pl.multiple_of((gi ^ flip) * fine, 16), fine), :]
+        ref[:fine, :] = lines[:, :narrow]
+        ref[fine:, :] = jnp.concatenate([lines[i * third : (i + 1) * third, narrow:] for i in range(3)], 1)
+
+
+def out_kernel(ids, hidden_two, out_keep, out_c, out_y, vec, mine, other):
+    out = hidden_two[...] + vec[8:9, :] + out_keep[...] + out_c[0].astype(F32) + out_y[...].astype(F32)
+    half = mine.shape[0]
+    mine[...] = out[:half].astype(BF16)
+    other[...] = out[half:].astype(BF16)
+
+
+def attend_back_kernel(
+    ids, qkv_t, lse, o_full, ga, w_t, tok_own, tok_x, tok_z, tok_d, far_own, far_x, far_z, far_d, te_a, te_b, vec,
+    dqkv_t, gh_own, gh_x, gh_z, gh_d, sums, dk, dv,
+):
+    part = o_full.shape[1]
+    own = 2 * tok_own.shape[0]
+    si, gi = ids[SEQ], ids[MEMBER]
+
+    @pl.loop(0, part // HEAD_DIM)
+    def _(head):
+        at = pl.multiple_of(head * HEAD_DIM, HEAD_DIM)
+        k_t = jnp.concatenate([qkv_t[j, pl.ds(part + at, HEAD_DIM), :] for j in range(4)], 1)
+        v_t = jnp.concatenate([qkv_t[j, pl.ds(2 * part + at, HEAD_DIM), :] for j in range(4)], 1)
+        for block in range(4):
+            q_t = qkv_t[block, pl.ds(at, HEAD_DIM), :] * jnp.asarray(0.125, BF16)
+            do_t = ga[gi ^ block, pl.ds(at, HEAD_DIM), :]
+            delta = jnp.sum(do_t.astype(F32) * o_full[block, pl.ds(at, HEAD_DIM), :], 0, keepdims=True)
+            weights = jnp.exp(dot(k_t, q_t, 0, 0) - lse[head * 4 + block, 0:1, :])
+            grad_probs = dot(v_t, do_t, 0, 0)
+            grad_scores = (weights * (grad_probs - delta)).astype(BF16)
+            value_part = dot(do_t, weights.astype(BF16), 1, 1)
+            key_part = dot(q_t, grad_scores, 1, 1)
+            dqkv_t[block, pl.ds(at, HEAD_DIM), :] = (dot(k_t, grad_scores) * 0.125).astype(BF16)
+            if block == 0:
+                dv[...] = value_part
+                dk[...] = key_part
+            else:
+                dv[...] += value_part
+                dk[...] += key_part
+        for block in range(4):
+            lanes = slice(block * own, (block + 1) * own)
+            dqkv_t[block, pl.ds(part + at, HEAD_DIM), :] = dk[:, lanes].astype(BF16)
+            dqkv_t[block, pl.ds(2 * part + at, HEAD_DIM), :] = dv[:, lanes].astype(BF16)
+
+    te_row = time_row(ids, te_a, te_b, vec)
+    gain = vec[1:2, :]
+    sum_gain = jnp.zeros_like(gain)
+    sum_bias = jnp.zeros_like(gain)
+    sum_hidden = jnp.zeros_like(gain)
+    pairs = (
+        (tok_own, far_own, gh_own), (tok_x, far_x, gh_x), (tok_z, far_z, gh_z), (tok_d, far_d, gh_d)
+    )
+    for block, (tok, far, to) in enumerate(pairs):
+        normed, rstd = normalize(jnp.concatenate([tok[...], far[...]]).astype(F32) + te_row)
+        grad_norm = dot(dqkv_t[block], w_t[...], 0, 0)
+        grad = norm_back(grad_norm * gain, normed, rstd)
+        to[...] = grad.astype(BF16)
+        sum_gain = sum_gain + jnp.sum(grad_norm * normed, 0, keepdims=True)
+        sum_bias = sum_bias + jnp.sum(grad_norm, 0, keepdims=True)
+        sum_hidden = sum_hidden + jnp.sum(grad, 0, keepdims=True)
+    sums[0:1, :] = sum_gain
+    sums[1:2, :] = sum_bias
+    sums[2:3, :] = sum_hidden
+    sums[3:8, :] = jnp.zeros((5, sums.shape[1]), F32)
+
+
+def qkv_grad_kernel(ids, attn_in, dqkv_t, sums_two, sums_one, keep, give):
+    si, gi = ids[SEQ], ids[MEMBER]
+    cols = dqkv_t.shape[1]
+    part = cols // 3
+    rows = part
+    width = attn_in.shape[2]
+    half = width // 2
+    grad = jnp.zeros((cols, width), F32)
+    tok_sum = jnp.zeros((16, cols), F32)
+    for block in range(4):
+        grad = grad + dot(dqkv_t[block], attn_in[block])
+        tok_sum = tok_sum + dot(jnp.ones((16, dqkv_t.shape[2]), BF16), dqkv_t[block], 1, 1)
+    grad = grad.astype(BF16)
+    line = lax.broadcasted_iota(jnp.int32, (32, cols), 0)
+    embed = sums_one[2:3, :] + sums_two[3:4, :]
+    slot = 8 + 2 * (2 * si + ids[HALF])
+    lanes = lax.broadcasted_iota(jnp.int32, (1, cols), 1)
+    wide = [jnp.concatenate([e, jnp.zeros((1, cols - half), F32)], 1) for e in (embed[:, :half], embed[:, half:])]
+    common = jnp.where(line == slot, wide[0], jnp.where(line == slot + 1, wide[1], 0.0))
+    for s in range(4):
+        here = slice(s * rows, (s + 1) * rows)
+        extra = common
+        vectors = (
+            sums_two[0:1, here], sums_two[1:2, here], sums_two[2:3, here], sums_one[0:1, here], sums_one[1:2, here],
+        )
+        for i, vector in enumerate(vectors):
+            full = jnp.concatenate([vector, jnp.zeros((1, cols - rows), F32)], 1)
+            extra = jnp.where(line == i, full, extra)
+        extra = jnp.where((line == 5) & (gi == s), tok_sum[0:1, :], extra)
+        block = grad[:, here].T
+        flip = si ^ s
+
+        @pl.when(flip % 2 == 0)
+        def _():
+            keep[flip // 2, :rows, :] = block
+            keep[flip // 2, rows:, :] = extra.astype(BF16)
+
+        @pl.when(flip % 2 == 1)
+        def _():
+            give[flip // 2, :rows, :] = block
+            give[flip // 2, rows:, :] = extra.astype(BF16)
+
+
+def hidden_grad_kernel(ids, grad_two, a, b, c, d, mine, other):
+    half = mine.shape[0]
+    grad = grad_two[...]
+    for ref in (a, b, c, d):
+        grad = grad + ref[...].astype(F32)
+    mine[...] = grad[:half].astype(BF16)
+    other[...] = grad[half:].astype(BF16)
+
+
+def feed_total_kernel(ids, d_own, d_x, d_z, d_d, u_own, u_x, u_z, u_d, w_down, w_up, small):
+    gi = ids[MEMBER]
+    quarter = w_down.shape[1]
+    fine = w_up.shape[1]
+    ff = w_down.shape[2]
+    for ref, flip in ((d_own, 0), (d_x, 1), (d_z, 2), (d_d, 3)):
+        w_down[gi ^ flip] = ref[:quarter, :].astype(F32)
+
+        @pl.when(gi == flip)
+        def _():
+            small[...] = ref[quarter:, :].astype(F32)
+
+    for ref, flip in ((u_own, 0), (u_x, 1), (u_z, 2), (u_d, 3)):
+        for s in range(4):
+            w_up[gi ^ flip, :, s * ff : (s + 1) * ff] = ref[s].astype(F32)
+
+
+def total_kernel(ids, g_own, g_x, g_z, g_d, sinus, w_qkv, w_out, w_time, vectors, embeds, totals):
+    si, gi = ids[SEQ], ids[MEMBER]
+    rows = w_qkv.shape[0]
+    cols = g_own.shape[1]
+    width = w_qkv.shape[1] // 3
+    part = cols // 3
+    fine = rows // 4
+    third = fine // 3
+    for member in range(4):
+        for ref, flip in ((g_own, 0), (g_x, 1), (g_z, 2), (g_d, 3)):
+
+            @pl.when(gi ^ flip == member)
+            def _():
+                for t in range(3):
+                    at = t * width + member * part
+                    w_qkv[:, at : at + part] = ref[:rows, t * part : (t + 1) * part].astype(F32)
+                lines = ref[rows + 32 :, :].astype(F32)
+                w_out[member, :, :cols] = lines[:fine]
+                for i in range(3):
+                    w_out[member, i * third : (i + 1) * third, cols:] = lines[fine:, i * part : (i + 1) * part]
+
+    small = jnp.zeros((32, cols), F32)
+    for ref in (g_own, g_x, g_z, g_d):
+        small = small + ref[rows : rows + 32, :].astype(F32)
+    vectors[...] = small[:8]
+    half = width // 2
+    totals[...] = small
+    for b in range(8):
+        embeds[b : b + 1, :half] = totals[8 + 2 * b : 9 + 2 * b, :half]
+        embeds[b : b + 1, half:] = totals[9 + 2 * b : 10 + 2 * b, :half]
+    w_time[...] = lax.dot_general(
+        sinus[...], embeds[...], (((0,), (0,)), ((), ())), precision=lax.Precision.HIGHEST,
+        preferred_element_type=F32,
+    )
+
+
+def pair_kernel(ids, mine, other, out):
+    out[ids[HALF]] = mine[...]
+    out[1 - ids[HALF]] = other[...]
+
+
+def group_body(
+    tokens, grad_out, timestep, w_time, b_time, ln1_gain, ln1_bias, w_qkv, b_query, b_value,
+    w_out, b_out, ln2_gain, ln2_bias, w_up, b_up, w_down, b_down,
+):
+    seqs, piece, width = tokens.shape
+    rows = w_qkv.shape[0]
+    ff = w_down.shape[0]
+    own = 2 * piece
+    part = width // 4
+    heads = part // HEAD_DIM
+    yi, ci = lax.axis_index("y"), lax.axis_index("c")
+    hi, zi, xi = lax.axis_index("h"), lax.axis_index("zl"), lax.axis_index("x")
+    si = 2 * yi + ci
+    gi = 2 * zi + xi
+    step = Steps(jnp.stack([si, gi, hi]).astype(jnp.int32))
+
+    def members(value):
+        return lax.all_to_all(value, ("zl", "x"), split_axis=0, concat_axis=0, tiled=True)
+
+    def gather4(value):
+        return [value, swap(value, "x"), swap(value, "zl"), across(value)]
+
+    def trade4(keep, x, z, d):
+        return [keep, swap(x, "x"), swap(z, "zl"), across(d)]
+
+    def across_seq(value):
+        return lax.ppermute(value, ("y", "c"), [(i, i ^ 3) for i in range(4)])
+
+    w_out_f = lax.all_gather(w_out, ("y", "c"), axis=0, tiled=True)
+    tok_own, tok_far = step(token_kernel, [tokens], [((piece, width), BF16)] * 2, 1)
+    far_own = swap(tok_far, "h")
+    toks = gather4(tok_own)
+    fars = gather4(far_own)
+    (wq_own,) = step(column_kernel, [w_qkv], [((rows, 3 * part), BF16)], 2)
+    wq_y = swap(wq_own, "y")
+    wq_c = swap(wq_own, "c")
+    wq_yc = swap(wq_y, "c")
+    low_bits = (timestep % 64).astype(BF16)
+    high_bits = (timestep // 64).astype(BF16)
+    steps_row = jnp.concatenate([high_bits, low_bits, jnp.zeros((rows - 2 * seqs,), BF16)])
+    blank = jnp.zeros((rows,), BF16)
+    small = jnp.stack(
+        [b_time, ln1_gain, ln1_bias, b_query, b_value, b_out, ln2_gain, ln2_bias, b_down, steps_row] + [blank] * 6
+    )
+    small_all = lax.all_gather(small, ("y", "c"))
+    vec = jnp.transpose(small_all, (1, 0, 2)).reshape(16, width).astype(F32)
+    steps = (small_all[:, 9, :seqs].astype(F32) * 64 + small_all[:, 9, seqs : 2 * seqs].astype(F32)).reshape(-1)
+    half = width // 2
+    place = si * rows + jnp.arange(rows)
+    freq = jnp.exp(-math.log(10000.0) * (place % half).astype(F32) / half)
+    angles = steps[:, None] * freq[None, :]
+    sinus_rows = jnp.where(place < half, jnp.sin(angles), jnp.cos(angles)).astype(BF16)
+    te = dot(sinus_rows, w_time)
+    up_own, up_y, up_c, up_yc = step(up_kernel, [w_up], [((rows, ff), BF16)] * 4, 2)
+    ups = [up_own, swap(up_y, "y"), swap(up_c, "c"), across_seq(up_yc)]
+    (te_a,) = step(add_kernel, [te, swap(te, "y")], [((4 * seqs, width), F32)], 1, behind=[far_own])
+    te_b = swap(te_a, "c")
+    (go_send,) = step(pick_kernel, [grad_out], [((piece, width), BF16)], 1)
+    go_far = swap(go_send, "h")
+
+    attn_in, qkv_t, o_full, o_send, lse, w_t = step(
+        attend_kernel, [*toks, *fars, te_a, te_b, vec, small_all, wq_own, wq_y, wq_c, wq_yc],
+        [((4, own, width), BF16), ((4, 3 * part, own), BF16), ((4, part, own), F32), ((4, part, own), BF16),
+         ((4 * heads, 8, own), F32), ((3 * part, width), BF16)],
+        15, [pltpu.VMEM((4, rows, 3 * part), BF16)], ups[1:],
+    )
+    attn = members(o_send)
+    (go_own,) = step(own_kernel, [grad_out, go_far], [((own, width), BF16)], 1)
+    go_all = lax.all_gather(go_own, ("y", "c"))
+    mlp_own, hidden_two, a_own, a_y, a_c, a_yc = step(
+        branch_kernel, [attn, w_out_f, tok_own, far_own, te_a, te_b, vec],
+        [((own, width), BF16), ((own, width), F32)] + [((part, own), BF16)] * 4, 3,
+    )
+    mlp_y = swap(mlp_own, "y")
+    mlp_c = swap(mlp_own, "c")
+    mlp_yc = swap(mlp_y, "c")
+    mlps = [mlp_own, mlp_y, mlp_c, mlp_yc]
+    a_s = [a_own, swap(a_y, "y"), swap(a_c, "c"), across_seq(a_yc)]
+    two = (2, own, width)
+    gm_own, gm_far, gm_send, out_own, out_far, out_send, act_all, gp_all = step(
+        feed_kernel, [*mlps, go_all, *ups, w_down, b_up.astype(F32).reshape(1, ff)],
+        [*[((own, width), F32)] * 2, (two, BF16), *[((own, width), F32)] * 2, (two, BF16), *[((4, own, ff), BF16)] * 2], 10,
+        [pltpu.VMEM((width, ff), BF16)], a_s[1:],
+    )
+    gm_c = swap(gm_send, "c")
+    out_c = swap(out_send, "c")
+    (gm_pair,) = step(second_kernel, [gm_far, gm_c], [((own, width), BF16)], 1)
+    gm_y = swap(gm_pair, "y")
+    quarters = [((ff // 4 + 16, width), BF16)] * 4 + [((4, rows // 4, ff), BF16)] * 4
+    *gd, gu_own, gu_x, gu_z, gu_d = step(
+        feed_grad_kernel, [*mlps, go_all, act_all, gp_all], quarters, 7, [pltpu.VMEM((width, width), BF16)]
+    )
+    gds = trade4(*gd)
+    grad_two, branch, ga_send, sums_two = step(
+        back_kernel, [gm_own, gm_c, gm_y, hidden_two, go_own, w_out_f, vec],
+        [((own, width), F32), ((own, width), BF16), ((4, part, own), BF16), ((8, width), F32)], 4,
+    )
+    ga = members(ga_send)
+    branch_s = lax.all_gather(branch, ("y", "c"))
+    (out_pair,) = step(second_kernel, [out_far, out_c], [((own, width), BF16)], 1)
+    out_y = swap(out_pair, "y")
+    gus = trade4(gu_own, gu_x, gu_z, gu_d)
+
+    dqkv_t, gh_own, gh_x, gh_z, gh_d, sums_one = step(
+        attend_back_kernel, [qkv_t, lse, o_full, ga, w_t, *toks, *fars, te_a, te_b, vec],
+        [((4, 3 * part, own), BF16)] + [((own, width), BF16)] * 4 + [((8, width), F32)],
+        15, [pltpu.VMEM((HEAD_DIM, 4 * own), F32)] * 2,
+    )
+    ghs = trade4(gh_own, gh_x, gh_z, gh_d)
+    (gd_sum,) = step(total4_kernel, gds, [((ff // 4 + 16, width), BF16)], 1)
+    gd_h = swap(gd_sum, "h")
+    chain = (2, rows + 32, 3 * part)
+    ch_keep, ch_give = step(qkv_grad_kernel, [attn_in, dqkv_t, sums_two, sums_one], [(chain, BF16), (chain, BF16)], 5)
+    ch_c = swap(ch_give, "c")
+    (gu_sum,) = step(total4_kernel, gus, [((4, rows // 4, ff), BF16)], 1)
+    gu_h = swap(gu_sum, "h")
+    folded = ((rows // 4 + rows // 12, 3 * part), BF16)
+    wo = step(out_grad_kernel, [*a_s, branch_s], [folded] * 4, 2, [pltpu.VMEM((rows, width), BF16)])
+    wos = trade4(*wo)
+    first, second = step(chain_kernel, [ch_keep, ch_c], [(chain[1:], BF16)] * 2, 1)
+    ch_y = swap(second, "y")
+    (gd_sum,) = step(both_kernel, [gd_sum, gd_h], [((ff // 4 + 16, width), BF16)], 1)
+    gds = gather4(gd_sum)
+    out_mine, out_other = step(
+        out_kernel, [hidden_two, out_own, out_c, out_y, vec], [((piece, width), BF16), ((piece, width), BF16)], 2
+    )
+    out_recv = swap(out_other, "h")
+    joined = ((rows + 32 + rows // 3, 3 * part), BF16)
+    (now,) = step(join_kernel, [first, ch_y, *wos], [joined], 1)
+    ch_h = swap(now, "h")
+    (gu_sum,) = step(both_kernel, [gu_sum, gu_h], [((4, rows // 4, ff), BF16)], 1)
+    gu_s = lax.all_to_all(gu_sum, ("y", "c"), split_axis=0, concat_axis=0, tiled=True)
+    gt_mine, gt_other = step(
+        hidden_grad_kernel, [grad_two, *ghs], [((piece, width), BF16), ((piece, width), BF16)], 2
+    )
+    gt_recv = swap(gt_other, "h")
+    (now,) = step(both_kernel, [now, ch_h], [joined], 1)
+    gqs = gather4(now)
+    gus = gather4(gu_s)
+    (output,) = step(pair_kernel, [out_mine, out_recv], [((seqs, piece, width), BF16)], 1.5)
+    (grad_tokens,) = step(pair_kernel, [gt_mine, gt_recv], [((seqs, piece, width), BF16)], 1.5)
+    t_qkv, t_out, total_w_time, tv, embeds = step(
+        total_kernel, [*gqs, sinus_rows.astype(F32)],
+        [((rows, 3 * width), F32), ((4, rows // 4, width), F32), ((rows, width), F32), ((8, 3 * part), F32),
+         ((8, width), F32)],
+        3, [pltpu.VMEM((32, 3 * part), F32)],
+    )
+    t_down, t_up, t_small = step(
+        feed_total_kernel, [*gds, *gus],
+        [((4, ff // 4, width), F32), ((4, rows // 4, 4 * ff), F32), ((16, width), F32)], 4,
+    )
+    total_b_time = lax.dynamic_slice_in_dim(jnp.sum(embeds, 0), si * rows, rows, 0)
+    total_b_down = lax.dynamic_slice_in_dim(t_small[1], si * rows, rows, 0)
+    return (
+        output, grad_tokens, total_w_time, total_b_time, tv[3, :rows], tv[4, :rows], t_qkv,
+        tv[5, :part], tv[5, 2 * part :], t_out.reshape(rows, width), tv[2, :rows], tv[0, :rows], tv[1, :rows],
+        t_up.reshape(rows, 4 * ff), t_small[0], t_down.reshape(ff, width), total_b_down,
+    )
+
+
 def solution(mesh):
     placed = (
         P("seq", "ctx", None),
@@ -411,28 +1041,44 @@
         P("seq", None),
         P("seq"),
     )
+    out_placed = (
+        P("seq", "ctx", None),
+        P("seq", "ctx", None),
+        P("seq", None),
+        P("seq"),
+        P("seq"),
+        P("seq"),
+        P("seq", None),
+        P("seq"),
+        P("seq"),
+        P("seq", None),
+        P("seq"),
+        P("seq"),
+        P("seq"),
+        P("seq", None),
+        P("seq"),
+        P("seq", None),
+        P("seq"),
+    )
+    sizes = dict(mesh.shape)
+    if sizes["seq"] == 4 and sizes["ctx"] == 8:
+        fine = Mesh(mesh.devices.reshape((2,) * 5), ("y", "c", "h", "zl", "x"))
+        split = {"seq": ("y", "c"), "ctx": ("h", "zl", "x"), None: None}
+
+        def finer(spec):
+            return P(*(split[axis] for axis in spec))
+
+        return jax.shard_map(
+            group_body,
+            mesh=fine,
+            in_specs=tuple(finer(spec) for spec in placed),
+            out_specs=tuple(finer(spec) for spec in out_placed),
+            check_vma=False,
+        )
     return jax.shard_map(
         body,
         mesh=mesh,
         in_specs=placed,
-        out_specs=(
-            P("seq", "ctx", None),
-            P("seq", "ctx", None),
-            P("seq", None),
-            P("seq"),
-            P("seq"),
-            P("seq"),
-            P("seq", None),
-            P("seq"),
-            P("seq"),
-            P("seq", None),
-            P("seq"),
-            P("seq"),
-            P("seq"),
-            P("seq", None),
-            P("seq"),
-            P("seq", None),
-            P("seq"),
-        ),
+        out_specs=out_placed,
         check_vma=False,
     )

time: 1080 us -> 309 us (0.29)
  waiting for transfers between devices: 580 us -> 90.4 us
  blocking collectives: 330 us -> 16.3 us
  Pallas kernels: 0 us -> 108 us
  matrix products: 93.5 us -> 0.24 us
  starting transfers between devices: 0.81 us -> 59.7 us
  other arithmetic: 24.6 us -> 1.52 us
    reduce_scatter x7 -> x0, waiting for transfers between devices: 369 us -> none  [the longest x1 117 us: body(): lax.psum_scatter(value_terms, 'ctx', scatter_dimension=1, tiled=True)]
    psum x1 -> x0, blocking collectives: 301 us -> none  [body(): lax.psum((shares[0], shares[1], shares[2], shares[3], shares[4], shares[5...]
    all_gather x7 -> x3, waiting for transfers between devices: 207 us -> 0.02 us  [the longest x1 0.02 us: group_body(): go_all = lax.all_gather(go_own, ('y', 'c'))]
    pallas_call x0 -> x29, Pallas kernels: none -> 108 us  [__call__(): pl.pallas_call(run, out_shape=shapes, in_specs=[pl.BlockSpec(memory_space...]
    dot_general x20 -> x1, matrix products: 93.5 us -> 0.24 us  [dot(): lax.dot_general(left, right, (((left_dim,), (right_dim,)), ((), ())), pre...]
    ppermute x0 -> x54, waiting for transfers between devices: none -> 90.3 us  [the longest x43 62.4 us: swap(): return lax.ppermute(value, axis, [(0, 1), (1, 0)])]
    ppermute x0 -> x54, starting transfers between devices: none -> 52.4 us  [the longest x43 39.7 us: swap(): return lax.ppermute(value, axis, [(0, 1), (1, 0)])]
    unnamed x2 -> x0, blocking collectives: 23.2 us -> none
  transfers between devices with their start and end apart: 14 -> 59, of which waited for: 13 -> 19; matrix products, arithmetic and copies ran while one was open for 10% -> 1% of each run, Pallas kernels for 0% -> 30%
where the time goes in v1:
time: 309 us; the launch traced here: 308 us
  Pallas kernels  108 us (35%)
  waiting for transfers between devices  90.4 us (29%)
  starting transfers between devices  59.7 us (19%)
  local copies, waits for them, and re-layouts  17.2 us (6%)
  blocking collectives  16.3 us (5%)
  between operations  14.5 us (5%)
    pallas_call x29, Pallas kernels, __call__(): pl.pallas_call(run, out_shape=shapes, in_specs=[pl.BlockSpec(memory_space...  108 us
    ppermute x43, waiting for transfers between devices, swap(): return lax.ppermute(value, axis, [(0, 1), (1, 0)])  62.4 us
    ppermute x43, starting transfers between devices, swap(): return lax.ppermute(value, axis, [(0, 1), (1, 0)])  39.7 us
    ppermute x9, waiting for transfers between devices, across(): return lax.ppermute(value, ('zl', 'x'), [(i, i ^ 3) for i in range(4)])  24.3 us
    unnamed x176, local copies, waits for them, and re-layouts  11.5 us
    all_to_all x1, blocking collectives, members(): lax.all_to_all(value, ('zl', 'x'), split_axis=0, concat_axis=0, tiled=True)  11.2 us
    ppermute x9, starting transfers between devices, across(): return lax.ppermute(value, ('zl', 'x'), [(i, i ^ 3) for i in range(4)])  9.87 us
  transfers between devices with their start and end apart: 59, of which 19 were waited for; matrix products, arithmetic and copies ran while one was open for 1% of the time, Pallas kernels for 30%

profile of v1, /device:TPU:0, one launch (start us, length us, event | category | flops | bytes accessed | tf_op | source)
XLA Modules:
  0.0 307.7 jit_solution(15927592474817001125)
XLA Ops:
  9.8 2.9 collective-permute-start
  14.3 2.6 collective-permute-start.3
  17.3 5.2 %all-gather = bf16[64,192]{1,0:T(8,128)(2,1)S(1)} all-gather(bf16[16,192]{1,0:T(8,128)(2,1)S(1)} %stack.67), channel_id=2, replica_groups=mesh['y'=2,'c'=2,'h'=2,'zl'=2,'x'=2] {'y','c'}, dimensions={0}, use_global_device_ids=true | all-gather | bytes 30720 | tf_op jit(solution)/shard_map/all_gather | solution.py:907
  24.4 2.0 column_kernel.1.refs_2_.refs_13_
  26.4 2.4 up_kernel.1
  33.0 4.7 %collective-permute-done.2.refs_4_.refs_9_ = bf16[128,768]{1,0:T(8,128)(2,1)S(1)} collective-permute-done((bf16[128,768]{1,0:T(8,128)(2,1)S(1)}, bf16[128,768]{1,0:T(8,128)(2,1)S(1)}, u32[]{:S(2)}, u32[]{:S(2)}) %collective-permute-start.2) | collective-permute-done | bytes 196640 | tf_op jit(solution)/shard_map/ppermute | solution.py:407
  40.4 3.8 %collective-permute-done.9.refs_14_ = bf16[192,576]{1,0:T(8,128)(2,1)S(1)} collective-permute-done((bf16[192,576]{1,0:T(8,128)(2,1)S(1)}, bf16[192,576]{1,0:T(8,128)(2,1)S(1)}, u32[]{:S(2)}, u32[]{:S(2)}) %collective-permute-start.9) | collective-permute-done | bytes 221216 | tf_op jit(solution)/shard_map/ppermute | solution.py:403
  45.2 2.5 collective-permute-start.6
  50.3 2.3 collective-permute-done.14.refs_19_.refs_9_
  52.6 2.4 collective-permute-done.6.refs_8_.refs_13_
  56.3 14.6 %attend_kernel.1 = (bf16[4,256,768]{2,1,0:T(8,128)(2,1)}, bf16[4,576,256]{2,1,0:T(8,128)(2,1)}, f32[4,192,256]{2,1,0:T(8,128)}, bf16[4,192,256]{2,1,0:T(8,128)(2...) custom-call(s32[3]{0:T(128)} %pad_add_fusion.refs_0_, ...), custom_call_target="tpu_custom_call" | custom-call | flops 17250000896 | bytes 1 | tf_op jit(solution)/shard_map/attend_kernel/pallas_call | solution.py:433
  73.5 11.2 %all_to_all.15.refs_1_ = bf16[4,192,256]{2,1,0:T(8,128)(2,1)} all-to-all(bf16[4,192,256]{2,1,0:T(8,128)(2,1)S(1)} %copy-done.2), channel_id=1, replica_groups=mesh['y'=2,'c'=2,'h'=2,'zl'=2,'x'=2] {'zl','x'}, dimensions={0} | all-to-all | bytes 786432 | tf_op jit(solution)/shard_map/all_to_all | solution.py:880
  84.7 3.3 %branch_kernel.1 = (bf16[256,768]{1,0:T(8,128)(2,1)}, f32[256,768]{1,0:T(8,128)}, bf16[192,256]{1,0:T(8,128)(2,1)}, bf16[192,256]{1,0:T(8,128)(2,1)}, bf16[192,2...) custom-call(s32[3]{0:T(128)} %pad_add_fusion.refs_0_, bf16[4,192,256]{2,1,0:T(8,128)(2,1)} %all_to_all.15.refs_1_, ...), custom_call_target="tpu_custom_call" | custom-call | flops 3449999872 | bytes 1 | tf_op jit(solution)/shard_map/branch_kernel/pallas_call | solution.py:433
  88.0 10.8 %collective-permute-done.16.refs_2_ = bf16[256,768]{1,0:T(8,128)(2,1)S(1)} collective-permute-done((bf16[256,768]{1,0:T(8,128)(2,1)}, bf16[256,768]{1,0:T(8,128)(2,1)S(1)}, u32[]{:S(2)}, u32[]{:S(2)}) %collective-permute-start.16) | collective-permute-done | bytes 393248 | tf_op jit(solution)/shard_map/ppermute | solution.py:403
  101.5 3.1 collective-permute-done.19.refs_12_.refs_2_
  106.8 9.7 %feed_kernel.1 = (f32[256,768]{1,0:T(8,128)}, f32[256,768]{1,0:T(8,128)}, bf16[2,256,768]{2,1,0:T(8,128)(2,1)}, f32[256,768]{1,0:T(8,128)}, f32[256,768]{1,0:T(8...) custom-call(s32[3]{0:T(128)} %pad_add_fusion.refs_0_, ...), custom_call_target="tpu_custom_call" | custom-call | flops 11500000256 | bytes 1 | tf_op jit(solution)/shard_map/feed_kernel/pallas_call | solution.py:433
  117.1 2.0 collective-permute-done.23.refs_2_
  120.0 2.2 second_kernel.2.refs_8_
  122.6 7.5 %feed_grad_kernel.1 = (bf16[208,768]{1,0:T(8,128)(2,1)}, bf16[208,768]{1,0:T(8,128)(2,1)}, bf16[208,768]{1,0:T(8,128)(2,1)}, bf16[208,768]{1,0:T(8,128)(2,1)}, b...) custom-call(s32[3]{0:T(128)} %pad_add_fusion.refs_0_, ...), custom_call_target="tpu_custom_call" | custom-call | flops 8049999872 | bytes 1 | tf_op jit(solution)/shard_map/feed_grad_kernel/pallas_call | solution.py:433
  130.1 3.5 %collective-permute-done.24.refs_3_ = bf16[256,768]{1,0:T(8,128)(2,1)S(1)} collective-permute-done((bf16[256,768]{1,0:T(8,128)(2,1)}, bf16[256,768]{1,0:T(8,128)(2,1)S(1)}, u32[]{:S(2)}, u32[]{:S(2)}) %collective-permute-start.24) | collective-permute-done | bytes 393248 | tf_op jit(solution)/shard_map/ppermute | solution.py:403
  134.4 4.3 %back_kernel.1 = (f32[256,768]{1,0:T(8,128)}, bf16[256,768]{1,0:T(8,128)(2,1)}, bf16[4,192,256]{2,1,0:T(8,128)(2,1)}, f32[8,768]{1,0:T(8,128)}) custom-call(s32[3]{0:T(128)} %pad_add_fusion.refs_0_, f32[256,768]{1,0:T(8,128)} %get-tuple-element.97.refs_3_.refs_1_, bf16[2,256,768]{2,1,0:T(8,128)(2,1)} %copy-done.9, bf16[256,768]{1,0:T(8,128)(2,1)} %copy-done.22, ...), custom_call_target="tpu_custom_call" | custom-call | flops 4600000000 | bytes 1 | tf_op jit(solution)/shard_map/back_kernel/pallas_call | solution.py:433
  138.7 3.7 %all-to-all-start.1 = ((bf16[4,192,256]{2,1,0:T(8,128)(2,1)}), bf16[4,192,256]{2,1,0:T(8,128)(2,1)S(1)}, u32[]{:S(2)}, u32[]{:S(2)}) async-start(bf16[4,192,256]{2,1,0:T(8,128)(2,1)} %get-tuple-element.110), calls=%async_computation.1 | async-start | bytes 786432 | tf_op jit(solution)/shard_map/all_to_all | solution.py:880
  149.4 2.2 second_kernel.3.refs_17_
  152.4 14.6 %attend_back_kernel.1 = (bf16[4,576,256]{2,1,0:T(8,128)(2,1)}, bf16[256,768]{1,0:T(8,128)(2,1)}, bf16[256,768]{1,0:T(8,128)(2,1)}, bf16[256,768]{1,0:T(8,128)(2,...) custom-call(s32[3]{0:T(128)} %pad_add_fusion.refs_0_, bf16[4,576,256]{2,1,0:T(8,128)(2,1)} %get-tuple-element.107.refs_1_, ...), custom_call_target="tpu_custom_call" | custom-call | flops 17250000896 | bytes 1 | tf_op jit(solution)/shard_map/attend_back_kernel/pallas_call | solution.py:433
  168.5 2.1 total4_kernel.2.refs_5_.refs_1_
  170.6 4.9 %qkv_grad_kernel.1 = (bf16[2,224,576]{2,1,0:T(8,128)(2,1)}, bf16[2,224,576]{2,1,0:T(8,128)(2,1)}) custom-call(s32[3]{0:T(128)} %pad_add_fusion.refs_0_, bf16[4,256,768]{2,1,0:T(8,128)(2,1)} %get-tuple-element.88.refs_3_.refs_1_, bf16[4,576,256]{2,1,0:T(8,128)(2,1)} %get-tuple-element.112.refs_5_.refs_2_, f32[8,768]{1,0:T(8,128)} %get-tuple-element.113.refs_3_, ...), custom_call_target="tpu_custom_call" | custom-call | flops 5750000128 | bytes 1 | tf_op jit(solution)/shard_map/qkv_grad_kernel/pallas_call | solution.py:433
  176.1 2.4 collective-permute-start.29
  179.2 2.1 total4_kernel.3.refs_6_.refs_1_
  181.3 2.9 out_grad_kernel.1
  185.1 2.2 chain_kernel.1
  194.8 2.0 both_kernel.3.refs_6_.refs_1_
  196.8 3.5 %collective-permute-start.43 = (bf16[4,48,768]{2,1,0:T(8,128)(2,1)S(1)}, bf16[4,48,768]{2,1,0:T(8,128)(2,1)S(1)}, u32[]{:S(2)}, u32[]{:S(2)}) collective-permute-start(bf16[4,48,768]{2,1,0:T(8,128)(2,1)S(1)} %copy-done.43), channel_id=1, source_target_pairs={{0,4},{4,0},{1,5},{5,1},{2,6},{6,2},{3,7},{7,3},{8,12},{12,8},{9,1... | collective-permute-start | bytes 884744 | tf_op jit(solution)/shard_map/ppermute | solution.py:403
  201.7 2.3 collective-permute-start.42
  204.0 2.6 out_kernel.1
  207.3 2.0 join_kernel.1.refs_3_.refs_1_
  209.4 3.9 %collective-permute-done.43.refs_2_ = bf16[4,48,768]{2,1,0:T(8,128)(2,1)S(1)} collective-permute-done((bf16[4,48,768]{2,1,0:T(8,128)(2,1)S(1)}, bf16[4,48,768]{2,1,0:T(8,128)(2,1)S(1)}, u32[]{:S(2)}, u32[]{:S(2)}) %collective-permute-start.43) | collective-permute-done | bytes 294944 | tf_op jit(solution)/shard_map/ppermute | solution.py:403
  215.9 13.9 %collective-permute-done.41.refs_4_ = bf16[256,768]{1,0:T(8,128)(2,1)S(1)} collective-permute-done((bf16[256,768]{1,0:T(8,128)(2,1)S(1)}, bf16[256,768]{1,0:T(8,128)(2,1)S(1)}, u32[]{:S(2)}, u32[]{:S(2)}) %collective-permute-start.41) | collective-permute-done | bytes 393248 | tf_op jit(solution)/shard_map/ppermute | solution.py:403
  229.8 8.2 %collective-permute-done.42.refs_5_ = bf16[256,768]{1,0:T(8,128)(2,1)S(1)} collective-permute-done((bf16[256,768]{1,0:T(8,128)(2,1)S(1)}, bf16[256,768]{1,0:T(8,128)(2,1)S(1)}, u32[]{:S(2)}, u32[]{:S(2)}) %collective-permute-start.42) | collective-permute-done | bytes 393248 | tf_op jit(solution)/shard_map/ppermute | solution.py:407
  238.8 2.5 hidden_grad_kernel.1
  242.0 2.0 both_kernel.5.refs_3_.refs_1_
  248.2 3.5 %all-to-all-start.2 = ((bf16[4,48,768]{2,1,0:T(8,128)(2,1)}), bf16[4,48,768]{2,1,0:T(8,128)(2,1)S(1)}, u32[]{:S(2)}, u32[]{:S(2)}) async-start(bf16[4,48,768]{2,1,0:T(8,128)(2,1)} %both_kernel.4.refs_6_), calls=%async_computation.2 | async-start | bytes 589824 | tf_op jit(solution)/shard_map/all_to_all | solution.py:994
  257.3 12.0 %collective-permute-done.48.refs_2_ = bf16[208,768]{1,0:T(8,128)(2,1)S(1)} collective-permute-done((bf16[208,768]{1,0:T(8,128)(2,1)S(1)}, bf16[208,768]{1,0:T(8,128)(2,1)S(1)}, u32[]{:S(2)}, u32[]{:S(2)}) %collective-permute-start.48) | collective-permute-done | bytes 319520 | tf_op jit(solution)/shard_map/ppermute | solution.py:403
  270.7 2.3 collective-permute-start.52
  273.7 3.4 %total_kernel.1 = (f32[192,2304]{1,0:T(8,128)}, f32[4,48,768]{2,1,0:T(8,128)}, f32[192,768]{1,0:T(8,128)}, f32[8,576]{1,0:T(8,128)}, f32[8,768]{1,0:T(8,128)}) custom-call(s32[3]{0:T(128)} %pad_add_fusion.refs_0_, bf16[288,576]{1,0:T(8,128)(2,1)} %both_kernel.5.refs_3_.refs_1_, bf16[288,576]{1,0:T(8,128)(2,1)} %copy-done.23, bf16[288,576]{1,0:T(8,128)(2,1)} %copy-done.24, ...), custom_call_target="tpu_custom_call" | custom-call | flops 3449999872 | bytes 1 | tf_op jit(solution)/shard_map/total_kernel/pallas_call | solution.py:433
  277.2 3.5 %collective-permute-done.50.refs_4_ = bf16[208,768]{1,0:T(8,128)(2,1)S(1)} collective-permute-done((bf16[208,768]{1,0:T(8,128)(2,1)S(1)}, bf16[208,768]{1,0:T(8,128)(2,1)S(1)}, u32[]{:S(2)}, u32[]{:S(2)}) %collective-permute-start.50) | collective-permute-done | bytes 319520 | tf_op jit(solution)/shard_map/ppermute | solution.py:407
  280.7 4.8 %collective-permute-done.51.refs_6_ = bf16[4,48,768]{2,1,0:T(8,128)(2,1)S(1)} collective-permute-done((bf16[4,48,768]{2,1,0:T(8,128)(2,1)S(1)}, bf16[4,48,768]{2,1,0:T(8,128)(2,1)S(1)}, u32[]{:S(2)}, u32[]{:S(2)}) %collective-permute-start.51) | collective-permute-done | bytes 294944 | tf_op jit(solution)/shard_map/ppermute | solution.py:403
  286.8 5.5 %collective-permute-done.53.refs_8_ = bf16[4,48,768]{2,1,0:T(8,128)(2,1)S(1)} collective-permute-done((bf16[4,48,768]{2,1,0:T(8,128)(2,1)S(1)}, bf16[4,48,768]{2,1,0:T(8,128)(2,1)S(1)}, u32[]{:S(2)}, u32[]{:S(2)}) %collective-permute-start.53) | collective-permute-done | bytes 294944 | tf_op jit(solution)/shard_map/ppermute | solution.py:407
  293.0 4.0 %feed_total_kernel.1 = (f32[4,192,768]{2,1,0:T(8,128)}, f32[4,48,3072]{2,1,0:T(8,128)}, f32[16,768]{1,0:T(8,128)}) custom-call(s32[3]{0:T(128)} %pad_add_fusion.refs_0_, bf16[208,768]{1,0:T(8,128)(2,1)} %both_kernel.3.refs_6_.refs_1_, bf16[208,768]{1,0:T(8,128)(2,1)} %copy-done.32, bf16[208,768]{1,0:T(8,128)(2,1)} %copy-done.36, ...), custom_call_target="tpu_custom_call" | custom-call | flops 4600000000 | bytes 1 | tf_op jit(solution)/shard_map/feed_total_kernel/pallas_call | solution.py:433
  (312 shorter events, 71.4 us)
Async XLA Ops:
  7.2 77.5 %all-gather.7.cloned.1.call-start = ((), (), s32[]{:S(2)}) async-start(), calls=%async_computation.3 | async-start | bytes 1474560 | tf_op jit(solution)/shard_map/all_gather | solution.py:891
  9.8 20.1 %collective-permute-start = (bf16[128,768]{1,0:T(8,128)(2,1)}, bf16[128,768]{1,0:T(8,128)(2,1)S(1)}, u32[]{:S(2)}, u32[]{:S(2)}) collective-permute-start(bf16[128,768]{1,0:T(8,128)(2,1)} %get-tuple-element.81.refs_2_.refs_1_.refs_3_.refs_6_), channel_id=1, source_target_pairs={{0,1},{1,0},{2,3},{3,2},{4,5},{5,4},{6,7},{7,6},{8,9},{9,8},{10,11... | collective-permute-start | bytes 589832 | tf_op jit(solution)/shard_map/ppermute | solution.py:403
  12.7 18.8 %collective-permute-start.1 = (bf16[128,768]{1,0:T(8,128)(2,1)}, bf16[128,768]{1,0:T(8,128)(2,1)S(1)}, u32[]{:S(2)}, u32[]{:S(2)}) collective-permute-start(bf16[128,768]{1,0:T(8,128)(2,1)} %get-tuple-element.81.refs_2_.refs_1_.refs_3_.refs_6_), channel_id=1, source_target_pairs={{0,2},{2,0},{1,3},{3,1},{4,6},{6,4},{5,7},{7,5},{8,10},{10,8},{9,1... | collective-permute-start | bytes 589832 | tf_op jit(solution)/shard_map/ppermute | solution.py:403
  14.3 15.1 %collective-permute-start.3 = (bf16[128,768]{1,0:T(8,128)(2,1)}, bf16[128,768]{1,0:T(8,128)(2,1)S(1)}, u32[]{:S(2)}, u32[]{:S(2)}) collective-permute-start(bf16[128,768]{1,0:T(8,128)(2,1)} %get-tuple-element.82), channel_id=1, source_target_pairs={{0,4},{4,0},{1,5},{5,1},{2,6},{6,2},{3,7},{7,3},{8,12},{12,8},{9,1... | collective-permute-start | bytes 589832 | tf_op jit(solution)/shard_map/ppermute | solution.py:403
  28.9 16.4 %collective-permute-start.12 = (bf16[192,768]{1,0:T(8,128)(2,1)}, bf16[192,768]{1,0:T(8,128)(2,1)S(1)}, u32[]{:S(2)}, u32[]{:S(2)}) collective-permute-start(bf16[192,768]{1,0:T(8,128)(2,1)} %get-tuple-element.84), channel_id=1, source_target_pairs={{0,16},{16,0},{1,17},{17,1},{2,18},{18,2},{3,19},{19,3},{4,20},{20... | collective-permute-start | bytes 884744 | tf_op jit(solution)/shard_map/ppermute | solution.py:403
  29.4 18.3 %collective-permute-start.13 = (bf16[192,768]{1,0:T(8,128)(2,1)}, bf16[192,768]{1,0:T(8,128)(2,1)S(1)}, u32[]{:S(2)}, u32[]{:S(2)}) collective-permute-start(bf16[192,768]{1,0:T(8,128)(2,1)} %get-tuple-element.85), channel_id=1, source_target_pairs={{0,8},{8,0},{1,9},{9,1},{2,10},{10,2},{3,11},{11,3},{4,12},{12,4},... | collective-permute-start | bytes 884744 | tf_op jit(solution)/shard_map/ppermute | solution.py:403
  29.9 14.3 %collective-permute-start.9 = (bf16[192,576]{1,0:T(8,128)(2,1)S(1)}, bf16[192,576]{1,0:T(8,128)(2,1)S(1)}, u32[]{:S(2)}, u32[]{:S(2)}) collective-permute-start(bf16[192,576]{1,0:T(8,128)(2,1)S(1)} %copy-done.51), channel_id=1, source_target_pairs={{0,16},{16,0},{1,17},{17,1},{2,18},{18,2},{3,19},{19,3},{4,20},{20... | collective-permute-start | bytes 663560 | tf_op jit(solution)/shard_map/ppermute | solution.py:403
  31.5 13.3 %collective-permute-start.10 = (bf16[192,576]{1,0:T(8,128)(2,1)S(1)}, bf16[192,576]{1,0:T(8,128)(2,1)S(1)}, u32[]{:S(2)}, u32[]{:S(2)}) collective-permute-start(bf16[192,576]{1,0:T(8,128)(2,1)S(1)} %copy-done.51), channel_id=1, source_target_pairs={{0,8},{8,0},{1,9},{9,1},{2,10},{10,2},{3,11},{11,3},{4,12},{12,4},... | collective-permute-start | bytes 663560 | tf_op jit(solution)/shard_map/ppermute | solution.py:403
  37.7 68.3 %all-gather.9.cloned.1.call-start = ((), (), s32[]{:S(2)}) async-start(), calls=%async_computation.4 | async-start | bytes 1966080 | tf_op jit(solution)/shard_map/all_gather | solution.py:931
  39.1 13.4 %collective-permute-start.14 = (bf16[192,768]{1,0:T(8,128)(2,1)S(1)}, bf16[192,768]{1,0:T(8,128)(2,1)S(1)}, u32[]{:S(2)}, u32[]{:S(2)}) collective-permute-start(bf16[192,768]{1,0:T(8,128)(2,1)S(1)} %copy-done.44), channel_id=1, source_target_pairs={{0,24},{8,16},{16,8},{24,0},{1,25},{9,17},{17,9},{25,1},{2,26},{10... | collective-permute-start | bytes 884744 | tf_op jit(solution)/shard_map/ppermute | solution.py:889
  44.2 8.3 %collective-permute-start.4 = (bf16[128,768]{1,0:T(8,128)(2,1)}, bf16[128,768]{1,0:T(8,128)(2,1)S(1)}, u32[]{:S(2)}, u32[]{:S(2)}) collective-permute-start(bf16[128,768]{1,0:T(8,128)(2,1)} %copy-done.58), channel_id=1, source_target_pairs={{0,1},{1,0},{2,3},{3,2},{4,5},{5,4},{6,7},{7,6},{8,9},{9,8},{10,11... | collective-permute-start | bytes 589832 | tf_op jit(solution)/shard_map/ppermute | solution.py:403
  45.2 9.7 %collective-permute-start.6 = (bf16[128,768]{1,0:T(8,128)(2,1)}, bf16[128,768]{1,0:T(8,128)(2,1)S(1)}, u32[]{:S(2)}, u32[]{:S(2)}) collective-permute-start(bf16[128,768]{1,0:T(8,128)(2,1)} %copy-done.58), channel_id=1, source_target_pairs={{0,3},{1,2},{2,1},{3,0},{4,7},{5,6},{6,5},{7,4},{8,11},{9,10},{10,... | collective-permute-start | bytes 589832 | tf_op jit(solution)/shard_map/ppermute | solution.py:407
  52.5 18.4 %collective-permute-start.15 = (bf16[128,768]{1,0:T(8,128)(2,1)}, bf16[128,768]{1,0:T(8,128)(2,1)S(1)}, u32[]{:S(2)}, u32[]{:S(2)}) collective-permute-start(bf16[128,768]{1,0:T(8,128)(2,1)} %pick_kernel.1.refs_20_), channel_id=1, source_target_pairs={{0,4},{4,0},{1,5},{5,1},{2,6},{6,2},{3,7},{7,3},{8,12},{12,8},{9,1... | collective-permute-start | bytes 589832 | tf_op jit(solution)/shard_map/ppermute | solution.py:403
  87.9 10.9 %collective-permute-start.16 = (bf16[256,768]{1,0:T(8,128)(2,1)}, bf16[256,768]{1,0:T(8,128)(2,1)S(1)}, u32[]{:S(2)}, u32[]{:S(2)}) collective-permute-start(bf16[256,768]{1,0:T(8,128)(2,1)} %get-tuple-element.90.refs_1_.refs_15_), channel_id=1, source_target_pairs={{0,16},{16,0},{1,17},{17,1},{2,18},{18,2},{3,19},{19,3},{4,20},{20... | collective-permute-start | bytes 1179656 | tf_op jit(solution)/shard_map/ppermute | solution.py:403
  87.9 18.0 %collective-permute-start.17 = (bf16[256,768]{1,0:T(8,128)(2,1)}, bf16[256,768]{1,0:T(8,128)(2,1)S(1)}, u32[]{:S(2)}, u32[]{:S(2)}) collective-permute-start(bf16[256,768]{1,0:T(8,128)(2,1)} %get-tuple-element.90.refs_1_.refs_15_), channel_id=1, source_target_pairs={{0,8},{8,0},{1,9},{9,1},{2,10},{10,2},{3,11},{11,3},{4,12},{12,4},... | collective-permute-start | bytes 1179656 | tf_op jit(solution)/shard_map/ppermute | solution.py:403
  116.8 31.1 %collective-permute-start.22 = (bf16[2,256,768]{2,1,0:T(8,128)(2,1)}, bf16[2,256,768]{2,1,0:T(8,128)(2,1)S(1)}, u32[]{:S(2)}, u32[]{:S(2)}) collective-permute-start(bf16[2,256,768]{2,1,0:T(8,128)(2,1)} %get-tuple-element.95), channel_id=1, source_target_pairs={{0,8},{8,0},{1,9},{9,1},{2,10},{10,2},{3,11},{11,3},{4,12},{12,4},... | collective-permute-start | bytes 2359304 | tf_op jit(solution)/shard_map/ppermute | solution.py:403
  122.2 11.4 %collective-permute-start.24 = (bf16[256,768]{1,0:T(8,128)(2,1)}, bf16[256,768]{1,0:T(8,128)(2,1)S(1)}, u32[]{:S(2)}, u32[]{:S(2)}) collective-permute-start(bf16[256,768]{1,0:T(8,128)(2,1)} %second_kernel.2.refs_8_), channel_id=1, source_target_pairs={{0,16},{16,0},{1,17},{17,1},{2,18},{18,2},{3,19},{19,3},{4,20},{20... | collective-permute-start | bytes 1179656 | tf_op jit(solution)/shard_map/ppermute | solution.py:403
  138.7 13.0 %all-to-all-start.1 = ((bf16[4,192,256]{2,1,0:T(8,128)(2,1)}), bf16[4,192,256]{2,1,0:T(8,128)(2,1)S(1)}, u32[]{:S(2)}, u32[]{:S(2)}) async-start(bf16[4,192,256]{2,1,0:T(8,128)(2,1)} %get-tuple-element.110), calls=%async_computation.1 | async-start | bytes 786432 | tf_op jit(solution)/shard_map/all_to_all | solution.py:880
  142.3 39.0 %all-gather.11.cloned.1.call-start = ((), (), s32[]{:S(2)}) async-start(), calls=%async_computation.5 | async-start | bytes 1966080 | tf_op jit(solution)/shard_map/all_gather | solution.py:961
  142.4 24.5 %collective-permute-start.26 = (bf16[208,768]{1,0:T(8,128)(2,1)S(1)}, bf16[208,768]{1,0:T(8,128)(2,1)S(1)}, u32[]{:S(2)}, u32[]{:S(2)}) collective-permute-start(bf16[208,768]{1,0:T(8,128)(2,1)S(1)} %copy-done.30), channel_id=1, source_target_pairs={{0,1},{1,0},{2,3},{3,2},{4,5},{5,4},{6,7},{7,6},{8,9},{9,8},{10,11... | collective-permute-start | bytes 958472 | tf_op jit(solution)/shard_map/ppermute | solution.py:403
  144.4 23.3 %collective-permute-start.27 = (bf16[208,768]{1,0:T(8,128)(2,1)S(1)}, bf16[208,768]{1,0:T(8,128)(2,1)S(1)}, u32[]{:S(2)}, u32[]{:S(2)}) collective-permute-start(bf16[208,768]{1,0:T(8,128)(2,1)S(1)} %copy-done.29), channel_id=1, source_target_pairs={{0,2},{2,0},{1,3},{3,1},{4,6},{6,4},{5,7},{7,5},{8,10},{10,8},{9,1... | collective-permute-start | bytes 958472 | tf_op jit(solution)/shard_map/ppermute | solution.py:403
  145.8 21.8 %collective-permute-start.28 = (bf16[208,768]{1,0:T(8,128)(2,1)S(1)}, bf16[208,768]{1,0:T(8,128)(2,1)S(1)}, u32[]{:S(2)}, u32[]{:S(2)}) collective-permute-start(bf16[208,768]{1,0:T(8,128)(2,1)S(1)} %copy-done.28), channel_id=1, source_target_pairs={{0,3},{1,2},{2,1},{3,0},{4,7},{5,6},{6,5},{7,4},{8,11},{9,10},{10,... | collective-permute-start | bytes 958472 | tf_op jit(solution)/shard_map/ppermute | solution.py:407
  146.0 30.1 %collective-permute-start.31 = (bf16[4,48,768]{2,1,0:T(8,128)(2,1)}, bf16[4,48,768]{2,1,0:T(8,128)(2,1)}, u32[]{:S(2)}, u32[]{:S(2)}) collective-permute-start(bf16[4,48,768]{2,1,0:T(8,128)(2,1)} %get-tuple-element.120), channel_id=1, source_target_pairs={{0,1},{1,0},{2,3},{3,2},{4,5},{5,4},{6,7},{7,6},{8,9},{9,8},{10,11... | collective-permute-start | bytes 884744 | tf_op jit(solution)/shard_map/ppermute | solution.py:403
  147.9 30.6 %collective-permute-start.32 = (bf16[4,48,768]{2,1,0:T(8,128)(2,1)}, bf16[4,48,768]{2,1,0:T(8,128)(2,1)}, u32[]{:S(2)}, u32[]{:S(2)}) collective-permute-start(bf16[4,48,768]{2,1,0:T(8,128)(2,1)} %get-tuple-element.121), channel_id=1, source_target_pairs={{0,2},{2,0},{1,3},{3,1},{4,6},{6,4},{5,7},{7,5},{8,10},{10,8},{9,1... | collective-permute-start | bytes 884744 | tf_op jit(solution)/shard_map/ppermute | solution.py:403
  167.0 11.5 %collective-permute-start.33 = (bf16[4,48,768]{2,1,0:T(8,128)(2,1)S(1)}, bf16[4,48,768]{2,1,0:T(8,128)(2,1)S(1)}, u32[]{:S(2)}, u32[]{:S(2)}) collective-permute-start(bf16[4,48,768]{2,1,0:T(8,128)(2,1)S(1)} %copy-done.42), channel_id=1, source_target_pairs={{0,3},{1,2},{2,1},{3,0},{4,7},{5,6},{6,5},{7,4},{8,11},{9,10},{10,... | collective-permute-start | bytes 884744 | tf_op jit(solution)/shard_map/ppermute | solution.py:407
  175.5 8.8 %collective-permute-start.30 = (bf16[2,224,576]{2,1,0:T(8,128)(2,1)}, bf16[2,224,576]{2,1,0:T(8,128)(2,1)S(1)}, u32[]{:S(2)}, u32[]{:S(2)}) collective-permute-start(bf16[2,224,576]{2,1,0:T(8,128)(2,1)} %get-tuple-element.116), channel_id=1, source_target_pairs={{0,8},{8,0},{1,9},{9,1},{2,10},{10,2},{3,11},{11,3},{4,12},{12,4},... | collective-permute-start | bytes 1548296 | tf_op jit(solution)/shard_map/ppermute | solution.py:403
  175.5 21.3 %collective-permute-start.25 = (bf16[256,768]{1,0:T(8,128)(2,1)S(1)}, bf16[256,768]{1,0:T(8,128)(2,1)S(1)}, u32[]{:S(2)}, u32[]{:S(2)}) collective-permute-start(bf16[256,768]{1,0:T(8,128)(2,1)S(1)} %copy-done.14), channel_id=1, source_target_pairs={{0,16},{16,0},{1,17},{17,1},{2,18},{18,2},{3,19},{19,3},{4,20},{20... | collective-permute-start | bytes 1179656 | tf_op jit(solution)/shard_map/ppermute | solution.py:403
  176.1 17.4 %collective-permute-start.29 = (bf16[208,768]{1,0:T(8,128)(2,1)S(1)}, bf16[208,768]{1,0:T(8,128)(2,1)S(1)}, u32[]{:S(2)}, u32[]{:S(2)}) collective-permute-start(bf16[208,768]{1,0:T(8,128)(2,1)S(1)} %copy-done.31), channel_id=1, source_target_pairs={{0,4},{4,0},{1,5},{5,1},{2,6},{6,2},{3,7},{7,3},{8,12},{12,8},{9,1... | collective-permute-start | bytes 958472 | tf_op jit(solution)/shard_map/ppermute | solution.py:403
  187.2 19.4 %collective-permute-start.35 = (bf16[224,576]{1,0:T(8,128)(2,1)}, bf16[224,576]{1,0:T(8,128)(2,1)S(1)}, u32[]{:S(2)}, u32[]{:S(2)}) collective-permute-start(bf16[224,576]{1,0:T(8,128)(2,1)} %get-tuple-element.127), channel_id=1, source_target_pairs={{0,16},{16,0},{1,17},{17,1},{2,18},{18,2},{3,19},{19,3},{4,20},{20... | collective-permute-start | bytes 774152 | tf_op jit(solution)/shard_map/ppermute | solution.py:403
  188.7 11.6 %collective-permute-start.36 = (bf16[64,576]{1,0:T(8,128)(2,1)S(1)}, bf16[64,576]{1,0:T(8,128)(2,1)S(1)}, u32[]{:S(2)}, u32[]{:S(2)}) collective-permute-start(bf16[64,576]{1,0:T(8,128)(2,1)S(1)} %copy-done.75), channel_id=1, source_target_pairs={{0,1},{1,0},{2,3},{3,2},{4,5},{5,4},{6,7},{7,6},{8,9},{9,8},{10,11... | collective-permute-start | bytes 221192 | tf_op jit(solution)/shard_map/ppermute | solution.py:403
  190.3 10.5 %collective-permute-start.37 = (bf16[64,576]{1,0:T(8,128)(2,1)S(1)}, bf16[64,576]{1,0:T(8,128)(2,1)S(1)}, u32[]{:S(2)}, u32[]{:S(2)}) collective-permute-start(bf16[64,576]{1,0:T(8,128)(2,1)S(1)} %copy-done.73), channel_id=1, source_target_pairs={{0,2},{2,0},{1,3},{3,1},{4,6},{6,4},{5,7},{7,5},{8,10},{10,8},{9,1... | collective-permute-start | bytes 221192 | tf_op jit(solution)/shard_map/ppermute | solution.py:403
  196.8 16.5 %collective-permute-start.43 = (bf16[4,48,768]{2,1,0:T(8,128)(2,1)S(1)}, bf16[4,48,768]{2,1,0:T(8,128)(2,1)S(1)}, u32[]{:S(2)}, u32[]{:S(2)}) collective-permute-start(bf16[4,48,768]{2,1,0:T(8,128)(2,1)S(1)} %copy-done.43), channel_id=1, source_target_pairs={{0,4},{4,0},{1,5},{5,1},{2,6},{6,2},{3,7},{7,3},{8,12},{12,8},{9,1... | collective-permute-start | bytes 884744 | tf_op jit(solution)/shard_map/ppermute | solution.py:403
  200.3 15.6 %collective-permute-start.40 = (bf16[256,768]{1,0:T(8,128)(2,1)S(1)}, bf16[256,768]{1,0:T(8,128)(2,1)S(1)}, u32[]{:S(2)}, u32[]{:S(2)}) collective-permute-start(bf16[256,768]{1,0:T(8,128)(2,1)S(1)} %copy-done.13), channel_id=1, source_target_pairs={{0,1},{1,0},{2,3},{3,2},{4,5},{5,4},{6,7},{7,6},{8,9},{9,8},{10,11... | collective-permute-start | bytes 1179656 | tf_op jit(solution)/shard_map/ppermute | solution.py:403
  200.8 29.0 %collective-permute-start.41 = (bf16[256,768]{1,0:T(8,128)(2,1)S(1)}, bf16[256,768]{1,0:T(8,128)(2,1)S(1)}, u32[]{:S(2)}, u32[]{:S(2)}) collective-permute-start(bf16[256,768]{1,0:T(8,128)(2,1)S(1)} %copy-done.12), channel_id=1, source_target_pairs={{0,2},{2,0},{1,3},{3,1},{4,6},{6,4},{5,7},{7,5},{8,10},{10,8},{9,1... | collective-permute-start | bytes 1179656 | tf_op jit(solution)/shard_map/ppermute | solution.py:403
  201.7 36.3 %collective-permute-start.42 = (bf16[256,768]{1,0:T(8,128)(2,1)S(1)}, bf16[256,768]{1,0:T(8,128)(2,1)S(1)}, u32[]{:S(2)}, u32[]{:S(2)}) collective-permute-start(bf16[256,768]{1,0:T(8,128)(2,1)S(1)} %copy-done.11), channel_id=1, source_target_pairs={{0,3},{1,2},{2,1},{3,0},{4,7},{5,6},{6,5},{7,4},{8,11},{9,10},{10,... | collective-permute-start | bytes 1179656 | tf_op jit(solution)/shard_map/ppermute | solution.py:407
  209.4 31.9 %collective-permute-start.39 = (bf16[288,576]{1,0:T(8,128)(2,1)}, bf16[288,576]{1,0:T(8,128)(2,1)S(1)}, u32[]{:S(2)}, u32[]{:S(2)}) collective-permute-start(bf16[288,576]{1,0:T(8,128)(2,1)} %join_kernel.1.refs_3_.refs_1_), channel_id=1, source_target_pairs={{0,4},{4,0},{1,5},{5,1},{2,6},{6,2},{3,7},{7,3},{8,12},{12,8},{9,1... | collective-permute-start | bytes 995336 | tf_op jit(solution)/shard_map/ppermute | solution.py:403
  213.3 38.3 %collective-permute-start.34 = (bf16[128,768]{1,0:T(8,128)(2,1)S(1)}, bf16[128,768]{1,0:T(8,128)(2,1)S(1)}, u32[]{:S(2)}, u32[]{:S(2)}) collective-permute-start(bf16[128,768]{1,0:T(8,128)(2,1)S(1)} %copy-done.63), channel_id=1, source_target_pairs={{0,4},{4,0},{1,5},{5,1},{2,6},{6,2},{3,7},{7,3},{8,12},{12,8},{9,1... | collective-permute-start | bytes 589832 | tf_op jit(solution)/shard_map/ppermute | solution.py:403
  241.3 13.3 %collective-permute-start.44 = (bf16[128,768]{1,0:T(8,128)(2,1)}, bf16[128,768]{1,0:T(8,128)(2,1)S(1)}, u32[]{:S(2)}, u32[]{:S(2)}) collective-permute-start(bf16[128,768]{1,0:T(8,128)(2,1)} %get-tuple-element.136), channel_id=1, source_target_pairs={{0,4},{4,0},{1,5},{5,1},{2,6},{6,2},{3,7},{7,3},{8,12},{12,8},{9,1... | collective-permute-start | bytes 589832 | tf_op jit(solution)/shard_map/ppermute | solution.py:403
  244.0 25.7 %collective-permute-start.45 = (bf16[288,576]{1,0:T(8,128)(2,1)}, bf16[288,576]{1,0:T(8,128)(2,1)S(1)}, u32[]{:S(2)}, u32[]{:S(2)}) collective-permute-start(bf16[288,576]{1,0:T(8,128)(2,1)} %both_kernel.5.refs_3_.refs_1_), channel_id=1, source_target_pairs={{0,1},{1,0},{2,3},{3,2},{4,5},{5,4},{6,7},{7,6},{8,9},{9,8},{10,11... | collective-permute-start | bytes 995336 | tf_op jit(solution)/shard_map/ppermute | solution.py:403
  245.0 25.7 %collective-permute-start.46 = (bf16[288,576]{1,0:T(8,128)(2,1)}, bf16[288,576]{1,0:T(8,128)(2,1)S(1)}, u32[]{:S(2)}, u32[]{:S(2)}) collective-permute-start(bf16[288,576]{1,0:T(8,128)(2,1)} %both_kernel.5.refs_3_.refs_1_), channel_id=1, source_target_pairs={{0,2},{2,0},{1,3},{3,1},{4,6},{6,4},{5,7},{7,5},{8,10},{10,8},{9,1... | collective-permute-start | bytes 995336 | tf_op jit(solution)/shard_map/ppermute | solution.py:403
  245.9 27.0 %collective-permute-start.47 = (bf16[288,576]{1,0:T(8,128)(2,1)}, bf16[288,576]{1,0:T(8,128)(2,1)S(1)}, u32[]{:S(2)}, u32[]{:S(2)}) collective-permute-start(bf16[288,576]{1,0:T(8,128)(2,1)} %both_kernel.5.refs_3_.refs_1_), channel_id=1, source_target_pairs={{0,3},{1,2},{2,1},{3,0},{4,7},{5,6},{6,5},{7,4},{8,11},{9,10},{10,... | collective-permute-start | bytes 995336 | tf_op jit(solution)/shard_map/ppermute | solution.py:407
  248.2 21.5 %all-to-all-start.2 = ((bf16[4,48,768]{2,1,0:T(8,128)(2,1)}), bf16[4,48,768]{2,1,0:T(8,128)(2,1)S(1)}, u32[]{:S(2)}, u32[]{:S(2)}) async-start(bf16[4,48,768]{2,1,0:T(8,128)(2,1)} %both_kernel.4.refs_6_), calls=%async_computation.2 | async-start | bytes 589824 | tf_op jit(solution)/shard_map/all_to_all | solution.py:994
  251.7 17.7 %collective-permute-start.48 = (bf16[208,768]{1,0:T(8,128)(2,1)S(1)}, bf16[208,768]{1,0:T(8,128)(2,1)S(1)}, u32[]{:S(2)}, u32[]{:S(2)}) collective-permute-start(bf16[208,768]{1,0:T(8,128)(2,1)S(1)} %copy-done.27), channel_id=1, source_target_pairs={{0,1},{1,0},{2,3},{3,2},{4,5},{5,4},{6,7},{7,6},{8,9},{9,8},{10,11... | collective-permute-start | bytes 958472 | tf_op jit(solution)/shard_map/ppermute | solution.py:403
  254.6 22.6 %collective-permute-start.49 = (bf16[208,768]{1,0:T(8,128)(2,1)S(1)}, bf16[208,768]{1,0:T(8,128)(2,1)S(1)}, u32[]{:S(2)}, u32[]{:S(2)}) collective-permute-start(bf16[208,768]{1,0:T(8,128)(2,1)S(1)} %copy-done.27), channel_id=1, source_target_pairs={{0,2},{2,0},{1,3},{3,1},{4,6},{6,4},{5,7},{7,5},{8,10},{10,8},{9,1... | collective-permute-start | bytes 958472 | tf_op jit(solution)/shard_map/ppermute | solution.py:403
  269.4 11.3 %collective-permute-start.50 = (bf16[208,768]{1,0:T(8,128)(2,1)S(1)}, bf16[208,768]{1,0:T(8,128)(2,1)S(1)}, u32[]{:S(2)}, u32[]{:S(2)}) collective-permute-start(bf16[208,768]{1,0:T(8,128)(2,1)S(1)} %copy-done.27), channel_id=1, source_target_pairs={{0,3},{1,2},{2,1},{3,0},{4,7},{5,6},{6,5},{7,4},{8,11},{9,10},{10,... | collective-permute-start | bytes 958472 | tf_op jit(solution)/shard_map/ppermute | solution.py:407
  269.7 15.7 %collective-permute-start.51 = (bf16[4,48,768]{2,1,0:T(8,128)(2,1)S(1)}, bf16[4,48,768]{2,1,0:T(8,128)(2,1)S(1)}, u32[]{:S(2)}, u32[]{:S(2)}) collective-permute-start(bf16[4,48,768]{2,1,0:T(8,128)(2,1)S(1)} %all-to-all-done.2.refs_5_), channel_id=1, source_target_pairs={{0,1},{1,0},{2,3},{3,2},{4,5},{5,4},{6,7},{7,6},{8,9},{9,8},{10,11... | collective-permute-start | bytes 884744 | tf_op jit(solution)/shard_map/ppermute | solution.py:403
  270.7 16.1 %collective-permute-start.52 = (bf16[4,48,768]{2,1,0:T(8,128)(2,1)S(1)}, bf16[4,48,768]{2,1,0:T(8,128)(2,1)S(1)}, u32[]{:S(2)}, u32[]{:S(2)}) collective-permute-start(bf16[4,48,768]{2,1,0:T(8,128)(2,1)S(1)} %all-to-all-done.2.refs_5_), channel_id=1, source_target_pairs={{0,2},{2,0},{1,3},{3,1},{4,6},{6,4},{5,7},{7,5},{8,10},{10,8},{9,1... | collective-permute-start | bytes 884744 | tf_op jit(solution)/shard_map/ppermute | solution.py:403
  273.0 19.3 %collective-permute-start.53 = (bf16[4,48,768]{2,1,0:T(8,128)(2,1)S(1)}, bf16[4,48,768]{2,1,0:T(8,128)(2,1)S(1)}, u32[]{:S(2)}, u32[]{:S(2)}) collective-permute-start(bf16[4,48,768]{2,1,0:T(8,128)(2,1)S(1)} %all-to-all-done.2.refs_5_), channel_id=1, source_target_pairs={{0,3},{1,2},{2,1},{3,0},{4,7},{5,6},{6,5},{7,4},{8,11},{9,10},{10,... | collective-permute-start | bytes 884744 | tf_op jit(solution)/shard_map/ppermute | solution.py:407
  (99 other events, 555.2 us)
Sparse Core Ops, SparseCore 0:
  37.8 19.5 all-gather.6
  73.6 18.3 all-gather.8
  148.0 18.7 all-gather.10

commit v2 on v1

--- a/solution.py
+++ b/solution.py
@@ -417,12 +417,16 @@
     )
 
 
+class Values:
+    pass
+
+
 class Steps:
     def __init__(self, ids):
         self.ids = ids
         self.last = None
 
-    def __call__(self, kernel, inputs, outputs, micros, scratch=(), behind=()):
+    def __call__(self, kernel, micros, inputs, outputs, scratch=(), behind=()):
         behind = [*behind] + ([self.last] if self.last is not None else [])
         shapes = [jax.ShapeDtypeStruct(shape, dtype) for shape, dtype in outputs]
         count = 1 + len(inputs)
@@ -461,12 +465,8 @@
     return r * (e - jnp.mean(e, -1, keepdims=True) - x * jnp.mean(e * x, -1, keepdims=True))
 
 
-def time_row(ids, te_a, te_b, vec):
-    at = pl.ds(2 * ids[SEQ] + ids[HALF], 1)
-    return te_a[at, :] + te_b[at, :] + vec[0:1, :]
-
-
-def token_kernel(ids, tokens, mine, far):
+def token_kernel(ids, tokens, mine, far, blank):
+    blank[...] = jnp.zeros(blank.shape, blank.dtype)
     mine[...] = tokens[ids[HALF]]
     far[...] = tokens[1 - ids[HALF]]
 
@@ -476,7 +476,7 @@
 
 
 def column_kernel(ids, w_qkv, out):
-    part = out.shape[1] // 3
+    part = w_qkv.shape[1] // 12
     width = w_qkv.shape[1] // 3
     for member in range(4):
 
@@ -484,7 +484,9 @@
         def _():
             for t in range(3):
                 at = t * width + member * part
-                out[:, t * part : (t + 1) * part] = w_qkv[:, at : at + part]
+                value = w_qkv[:, at : at + part]
+                for block in range(4):
+                    out[block, :, t * part : (t + 1) * part] = value
 
 
 def up_kernel(ids, w_up, own, y, c, yc):
@@ -493,23 +495,15 @@
         ref[...] = w_up[:, pl.ds(pl.multiple_of((ids[SEQ] ^ flip) * ff, ff), ff)]
 
 
-def add_kernel(ids, left, right, out):
-    out[...] = left[...] + right[...]
-
-
-def own_kernel(ids, grad_out, far, own):
+def own_kernel(ids, grad_out, far, w_out, own, copy):
+    copy[...] = w_out[...]
     half = far.shape[0]
     own[:half] = grad_out[ids[HALF]]
     own[half:] = far[...]
 
 
 def second_kernel(ids, keep, recv, out):
-    out[...] = (keep[...] + recv[1].astype(F32)).astype(BF16)
-
-
-def total4_kernel(ids, a, b, c, d, out):
-    total = a[...].astype(F32) + b[...].astype(F32) + c[...].astype(F32) + d[...].astype(F32)
-    out[...] = total.astype(BF16)
+    out[...] = (keep[...].astype(F32) + recv[1].astype(F32)).astype(BF16)
 
 
 def both_kernel(ids, left, right, out):
@@ -528,20 +522,29 @@
     out[rows:] = total.astype(BF16)
 
 
+def pieces_kernel(ids, a, b, c, d, down, up):
+    total = a[...].astype(F32) + b[...].astype(F32) + c[...].astype(F32) + d[...].astype(F32)
+    low = total.astype(BF16)
+    rows = down.shape[0]
+    fine = up.shape[1]
+    down[...] = low[:rows]
+    for s in range(4):
+        up[s] = low[rows + s * fine : rows + (s + 1) * fine]
+
+
 def attend_kernel(
-    ids, tok_own, tok_x, tok_z, tok_d, far_own, far_x, far_z, far_d, te_a, te_b, vec, small, wq_own, wq_y, wq_c, wq_yc,
-    attn_in, qkv_t, o_full, o_send, lse, w_t, w_rows,
+    ids, tok_own, tok_x, tok_z, tok_d, far_own, far_x, far_z, far_d, sinus, w_time, vec, small, wq,
+    attn_in, qkv_t, o_full, o_send, lse, w_t, te,
 ):
-    part = wq_own.shape[1] // 3
-    rows = wq_own.shape[0]
     piece, width = tok_own.shape
+    part = width // 4
+    rows = wq.shape[1]
     own = 2 * piece
-    si, gi = ids[SEQ], ids[MEMBER]
-    for ref, flip in ((wq_own, 0), (wq_y, 2), (wq_c, 1), (wq_yc, 3)):
-        w_rows[si ^ flip] = ref[...]
+    gi = ids[MEMBER]
     for block in range(4):
-        w_t[:, block * rows : (block + 1) * rows] = w_rows[block].T
-    te_row = time_row(ids, te_a, te_b, vec)
+        w_t[:, block * rows : (block + 1) * rows] = wq[block].T
+    te[...] = dot(sinus[...], w_time[...]) + vec[0:1, :]
+    te_row = te[0:1, :]
     gain, offset = vec[1:2, :], vec[2:3, :]
     bias = small[gi].astype(F32).T
     pairs = ((tok_own, far_own), (tok_x, far_x), (tok_z, far_z), (tok_d, far_d))
@@ -571,29 +574,43 @@
             lse[head * 4 + block] = jnp.broadcast_to(top + jnp.log(total), (8, own))
 
 
+def fold(value):
+    third = value.shape[0] // 3
+    return jnp.concatenate([value[i * third : (i + 1) * third] for i in range(3)], 1)
+
+
+def unfold(value):
+    wide = value.shape[1] // 3
+    return jnp.concatenate([value[:, i * wide : (i + 1) * wide] for i in range(3)], 0)
+
+
 def branch_kernel(
-    ids, attn, w_out, tok_own, far_own, te_a, te_b, vec, mlp_in, hidden_two, a_own, a_y, a_c, a_yc
+    ids, attn, w_out, tok_own, far_own, te, vec, mlp_in, hidden_two, folds
 ):
     rows = attn.shape[1]
-    te_row = time_row(ids, te_a, te_b, vec)
+    te_row = te[0:1, :]
     hidden = jnp.concatenate([tok_own[...], far_own[...]]).astype(F32) + te_row + vec[5:6, :]
     for block in range(4):
         hidden = hidden + dot(attn[block], w_out[block * rows : (block + 1) * rows, :], 0, 0)
     hidden_two[...] = hidden
     normed, _ = normalize(hidden)
     mlp_in[...] = (normed * vec[6:7, :] + vec[7:8, :]).astype(BF16)
-    for ref, flip in ((a_own, 0), (a_y, 2), (a_c, 1), (a_yc, 3)):
-        ref[...] = attn[ids[SEQ] ^ flip]
+    for block in range(4):
+        folds[block] = fold(attn[ids[SEQ] ^ block])
 
 
 def feed_kernel(
-    ids, m_own, m_y, m_c, m_yc, go_all, u_own, u_y, u_c, u_yc, w_down, b_up,
+    ids, m_own, m_y, m_c, m_yc, go_all, u_own, u_y, u_c, u_yc, w_down, b_up, folds,
     gm_own, gm_pair, gm_send, out_own, out_pair, out_send, act_all, gp_all, w_up,
 ):
     si = ids[SEQ]
     rows = u_own.shape[0]
+    own = m_own.shape[0]
     for ref, flip in ((u_own, 0), (u_y, 2), (u_c, 1), (u_yc, 3)):
         w_up[pl.ds(pl.multiple_of((si ^ flip) * rows, rows), rows), :] = ref[...]
+    fine = folds.shape[1]
+    out_send[2 * own : 2 * own + fine, :] = folds[1]
+    out_send[2 * own + fine :, :] = folds[3]
     for block, (ref, flip) in enumerate(((m_own, 0), (m_y, 2), (m_c, 1), (m_yc, 3))):
         grad_out = go_all[si ^ flip]
         pre = dot(ref[...], w_up[...]) + b_up[...]
@@ -607,15 +624,15 @@
         gm = dot(grad_pre, w_up[...], 1, 1)
         out = dot(act, w_down[...])
         if block < 2:
-            (gm_own, gm_pair)[block][...] = gm
-            (out_own, out_pair)[block][...] = out
+            (gm_own, gm_pair)[block][...] = gm.astype(gm_pair.dtype if block else F32)
+            (out_own, out_pair)[block][...] = out.astype(out_pair.dtype if block else F32)
         else:
             gm_send[block - 2] = gm.astype(BF16)
-            out_send[block - 2] = out.astype(BF16)
+            out_send[(block - 2) * own : (block - 1) * own, :] = out.astype(BF16)
 
 
 def feed_grad_kernel(
-    ids, m_own, m_y, m_c, m_yc, go_all, act_all, gp_all, d_own, d_x, d_z, d_d, u_own, u_x, u_z, u_d, grad
+    ids, m_own, m_y, m_c, m_yc, go_all, act_all, gp_all, p_own, p_x, p_z, p_d, grad
 ):
     si, gi = ids[SEQ], ids[MEMBER]
     width = m_own.shape[1]
@@ -623,6 +640,7 @@
     part = ff // 4
     rows = width // 4
     fine = rows // 4
+    pieces = ((p_own, 0), (p_x, 1), (p_z, 2), (p_d, 3))
     orders = ((m_own, 0), (m_y, 2), (m_c, 1), (m_yc, 3))
     for s in range(4):
         cols = slice(s * part, (s + 1) * part)
@@ -630,7 +648,7 @@
         for block, (_, flip) in enumerate(orders):
             total = total + dot(act_all[block, :, cols], go_all[si ^ flip], 0, 0)
         grad[cols, :] = total.astype(BF16)
-    for ref, flip in ((d_own, 0), (d_x, 1), (d_z, 2), (d_d, 3)):
+    for ref, flip in pieces:
         ref[:part, :] = grad[pl.ds(pl.multiple_of((gi ^ flip) * part, 16), part), :]
     for s in range(4):
         cols = slice(s * rows, (s + 1) * rows)
@@ -638,9 +656,10 @@
         for block, (ref, _) in enumerate(orders):
             total = total + dot(ref[:, cols], gp_all[block], 0, 0)
         grad[cols, :] = total.astype(BF16)
-    for ref, flip in ((u_own, 0), (u_x, 1), (u_z, 2), (u_d, 3)):
+    for ref, flip in pieces:
         for s in range(4):
-            ref[s] = grad[pl.ds(pl.multiple_of(s * rows + (gi ^ flip) * fine, 16), fine), :]
+            at = part + 16 + s * fine
+            ref[at : at + fine, :] = grad[pl.ds(pl.multiple_of(s * rows + (gi ^ flip) * fine, 16), fine), :]
     b_up = jnp.zeros((1, ff), F32)
     b_down = jnp.zeros((1, width), F32)
     for block in range(4):
@@ -648,13 +667,13 @@
         b_down = b_down + jnp.sum(go_all[block].astype(F32), 0, keepdims=True)
     line = lax.broadcasted_iota(jnp.int32, (16, width), 0)
     extra = jnp.where(line == 0, b_up, jnp.where(line == 1, b_down, 0.0))
-    for ref, flip in ((d_own, 0), (d_x, 1), (d_z, 2), (d_d, 3)):
-        ref[part:, :] = jnp.where(gi == flip, extra, 0.0).astype(BF16)
+    for ref, flip in pieces:
+        ref[part : part + 16, :] = jnp.where(gi == flip, extra, 0.0).astype(BF16)
 
 
 def back_kernel(
-    ids, gm_keep, gm_c, gm_y, hidden_two, go_own, w_out, vec,
-    grad_two, branch, ga_send, sums,
+    ids, gm_keep, gm_c, gm_y, hidden_two, go_own, w_out, vec, out_far, out_c, folds,
+    grad_two, branch, ga_send, sums, out_pair,
 ):
     rows = w_out.shape[0] // 4
     grad_mlp = gm_keep[...] + gm_c[0].astype(F32) + gm_y[...].astype(F32)
@@ -670,33 +689,16 @@
     sums[2:3, :] = jnp.sum(low.astype(F32), 0, keepdims=True)
     sums[3:4, :] = jnp.sum(grad, 0, keepdims=True)
     sums[4:8, :] = jnp.zeros((4, sums.shape[1]), F32)
-
-
-def out_grad_kernel(ids, a_own, a_y, a_c, a_yc, branch, w_own, w_x, w_z, w_d, grads):
-    si, gi = ids[SEQ], ids[MEMBER]
-    narrow = w_own.shape[1]
-    fine = a_own.shape[0] // 4
-    third = fine // 3
-    grad = jnp.zeros((a_own.shape[0], branch.shape[2]), F32)
-    for ref, flip in ((a_own, 0), (a_y, 2), (a_c, 1), (a_yc, 3)):
-        grad = grad + dot(ref[...], branch[si ^ flip])
-    grads[...] = grad.astype(BF16)
-    for ref, flip in ((w_own, 0), (w_x, 1), (w_z, 2), (w_d, 3)):
-        lines = grads[pl.ds(pl.multiple_of((gi ^ flip) * fine, 16), fine), :]
-        ref[:fine, :] = lines[:, :narrow]
-        ref[fine:, :] = jnp.concatenate([lines[i * third : (i + 1) * third, narrow:] for i in range(3)], 1)
-
-
-def out_kernel(ids, hidden_two, out_keep, out_c, out_y, vec, mine, other):
-    out = hidden_two[...] + vec[8:9, :] + out_keep[...] + out_c[0].astype(F32) + out_y[...].astype(F32)
-    half = mine.shape[0]
-    mine[...] = out[:half].astype(BF16)
-    other[...] = out[half:].astype(BF16)
+    own = out_far.shape[0]
+    fine = folds.shape[1]
+    out_pair[:own, :] = (out_far[...].astype(F32) + out_c[own : 2 * own, :].astype(F32)).astype(BF16)
+    out_pair[own : own + fine, :] = folds[2]
+    out_pair[own + fine :, :] = out_c[2 * own + fine :, :]
 
 
 def attend_back_kernel(
-    ids, qkv_t, lse, o_full, ga, w_t, tok_own, tok_x, tok_z, tok_d, far_own, far_x, far_z, far_d, te_a, te_b, vec,
-    dqkv_t, gh_own, gh_x, gh_z, gh_d, sums, dk, dv,
+    ids, qkv_t, lse, o_full, ga, w_t, tok_own, tok_x, tok_z, tok_d, far_own, far_x, far_z, far_d, te, vec,
+    dqkv_t, gh_send, sums, dk, dv,
 ):
     part = o_full.shape[1]
     own = 2 * tok_own.shape[0]
@@ -728,19 +730,17 @@
             dqkv_t[block, pl.ds(part + at, HEAD_DIM), :] = dk[:, lanes].astype(BF16)
             dqkv_t[block, pl.ds(2 * part + at, HEAD_DIM), :] = dv[:, lanes].astype(BF16)
 
-    te_row = time_row(ids, te_a, te_b, vec)
+    te_row = te[0:1, :]
     gain = vec[1:2, :]
     sum_gain = jnp.zeros_like(gain)
     sum_bias = jnp.zeros_like(gain)
     sum_hidden = jnp.zeros_like(gain)
-    pairs = (
-        (tok_own, far_own, gh_own), (tok_x, far_x, gh_x), (tok_z, far_z, gh_z), (tok_d, far_d, gh_d)
-    )
-    for block, (tok, far, to) in enumerate(pairs):
+    pairs = ((tok_own, far_own), (tok_x, far_x), (tok_z, far_z), (tok_d, far_d))
+    for block, (tok, far) in enumerate(pairs):
         normed, rstd = normalize(jnp.concatenate([tok[...], far[...]]).astype(F32) + te_row)
         grad_norm = dot(dqkv_t[block], w_t[...], 0, 0)
         grad = norm_back(grad_norm * gain, normed, rstd)
-        to[...] = grad.astype(BF16)
+        gh_send[gi ^ block] = grad.astype(BF16)
         sum_gain = sum_gain + jnp.sum(grad_norm * normed, 0, keepdims=True)
         sum_bias = sum_bias + jnp.sum(grad_norm, 0, keepdims=True)
         sum_hidden = sum_hidden + jnp.sum(grad, 0, keepdims=True)
@@ -793,33 +793,68 @@
             give[flip // 2, rows:, :] = extra.astype(BF16)
 
 
-def hidden_grad_kernel(ids, grad_two, a, b, c, d, mine, other):
+def out_grad_kernel(ids, folds, out_c, out_y, branch_s, w_own, w_x, w_z, w_d, low):
+    si, gi = ids[SEQ], ids[MEMBER]
+    rows = low.shape[0]
+    cols = w_own.shape[1]
+    fine = rows // 4
+    third = fine // 3
+    own = branch_s.shape[1]
+    third_rows = folds.shape[1]
+    grad = dot(unfold(folds[0]), branch_s[si])
+    grad = grad + dot(unfold(out_c[2 * own : 2 * own + third_rows, :]), branch_s[si ^ 1])
+    grad = grad + dot(unfold(out_y[own : own + third_rows, :]), branch_s[si ^ 2])
+    grad = grad + dot(unfold(out_y[own + third_rows :, :]), branch_s[si ^ 3])
+    low[...] = grad.astype(BF16)
+    for ref, flip in ((w_own, 0), (w_x, 1), (w_z, 2), (w_d, 3)):
+        lines = low[pl.ds(pl.multiple_of((gi ^ flip) * fine, 16), fine), :]
+        ref[:fine, :] = lines[:, :cols]
+        ref[fine:, :] = jnp.concatenate([lines[i * third : (i + 1) * third, cols:] for i in range(3)], 1)
+
+
+def out_kernel(ids, hidden_two, out_keep, out_c, out_y, vec, mine, other):
+    half = mine.shape[0]
+    out = hidden_two[...] + vec[8:9, :] + out_keep[...] + out_c[: 2 * half].astype(F32) + out_y[: 2 * half].astype(F32)
+    mine[...] = out[:half].astype(BF16)
+    other[...] = out[half:].astype(BF16)
+
+
+def hidden_grad_kernel(ids, grad_two, recv, mine, other):
     half = mine.shape[0]
     grad = grad_two[...]
-    for ref in (a, b, c, d):
-        grad = grad + ref[...].astype(F32)
+    for member in range(4):
+        grad = grad + recv[member].astype(F32)
     mine[...] = grad[:half].astype(BF16)
     other[...] = grad[half:].astype(BF16)
 
 
-def feed_total_kernel(ids, d_own, d_x, d_z, d_d, u_own, u_x, u_z, u_d, w_down, w_up, small):
+def down_total_kernel(ids, own, x, z, d, w_down, b_up, b_down):
     gi = ids[MEMBER]
     quarter = w_down.shape[1]
-    fine = w_up.shape[1]
-    ff = w_down.shape[2]
-    for ref, flip in ((d_own, 0), (d_x, 1), (d_z, 2), (d_d, 3)):
+    for ref, flip in ((own, 0), (x, 1), (z, 2), (d, 3)):
         w_down[gi ^ flip] = ref[:quarter, :].astype(F32)
 
         @pl.when(gi == flip)
         def _():
-            small[...] = ref[quarter:, :].astype(F32)
-
-    for ref, flip in ((u_own, 0), (u_x, 1), (u_z, 2), (u_d, 3)):
+            b_up[...] = ref[quarter : quarter + 1, :].astype(F32)
+            full = ref[quarter : quarter + 2, :].astype(F32)
+            rows = b_down.shape[1]
+            for s in range(4):
+
+                @pl.when(ids[SEQ] == s)
+                def _():
+                    b_down[...] = full[1:2, s * rows : (s + 1) * rows]
+
+
+def up_total_kernel(ids, own, x, z, d, w_up):
+    gi = ids[MEMBER]
+    ff = own.shape[2]
+    for ref, flip in ((own, 0), (x, 1), (z, 2), (d, 3)):
         for s in range(4):
             w_up[gi ^ flip, :, s * ff : (s + 1) * ff] = ref[s].astype(F32)
 
 
-def total_kernel(ids, g_own, g_x, g_z, g_d, sinus, w_qkv, w_out, w_time, vectors, embeds, totals):
+def total_kernel(ids, g_own, g_x, g_z, g_d, sinus, w_qkv, w_out, w_time, vectors, b_time, totals, embeds):
     si, gi = ids[SEQ], ids[MEMBER]
     rows = w_qkv.shape[0]
     cols = g_own.shape[1]
@@ -849,15 +884,24 @@
     for b in range(8):
         embeds[b : b + 1, :half] = totals[8 + 2 * b : 9 + 2 * b, :half]
         embeds[b : b + 1, half:] = totals[9 + 2 * b : 10 + 2 * b, :half]
+    full = jnp.sum(embeds[...], 0, keepdims=True)
+    for s in range(4):
+
+        @pl.when(si == s)
+        def _():
+            b_time[...] = full[:, s * rows : (s + 1) * rows]
+
     w_time[...] = lax.dot_general(
         sinus[...], embeds[...], (((0,), (0,)), ((), ())), precision=lax.Precision.HIGHEST,
         preferred_element_type=F32,
     )
 
 
-def pair_kernel(ids, mine, other, out):
-    out[ids[HALF]] = mine[...]
-    out[1 - ids[HALF]] = other[...]
+def pair_kernel(ids, grad_mine, out_mine, grad_other, out_other, grad_tokens, output):
+    grad_tokens[ids[HALF]] = grad_mine[...]
+    grad_tokens[1 - ids[HALF]] = grad_other[...]
+    output[ids[HALF]] = out_mine[...]
+    output[1 - ids[HALF]] = out_other[...]
 
 
 def group_body(
@@ -879,6 +923,9 @@
     def members(value):
         return lax.all_to_all(value, ("zl", "x"), split_axis=0, concat_axis=0, tiled=True)
 
+    def shards(value):
+        return lax.all_to_all(value, ("y", "c"), split_axis=0, concat_axis=0, tiled=True)
+
     def gather4(value):
         return [value, swap(value, "x"), swap(value, "zl"), across(value)]
 
@@ -888,135 +935,186 @@
     def across_seq(value):
         return lax.ppermute(value, ("y", "c"), [(i, i ^ 3) for i in range(4)])
 
-    w_out_f = lax.all_gather(w_out, ("y", "c"), axis=0, tiled=True)
-    tok_own, tok_far = step(token_kernel, [tokens], [((piece, width), BF16)] * 2, 1)
-    far_own = swap(tok_far, "h")
-    toks = gather4(tok_own)
-    fars = gather4(far_own)
-    (wq_own,) = step(column_kernel, [w_qkv], [((rows, 3 * part), BF16)], 2)
-    wq_y = swap(wq_own, "y")
-    wq_c = swap(wq_own, "c")
-    wq_yc = swap(wq_y, "c")
-    low_bits = (timestep % 64).astype(BF16)
-    high_bits = (timestep // 64).astype(BF16)
-    steps_row = jnp.concatenate([high_bits, low_bits, jnp.zeros((rows - 2 * seqs,), BF16)])
-    blank = jnp.zeros((rows,), BF16)
-    small = jnp.stack(
-        [b_time, ln1_gain, ln1_bias, b_query, b_value, b_out, ln2_gain, ln2_bias, b_down, steps_row] + [blank] * 6
-    )
-    small_all = lax.all_gather(small, ("y", "c"))
-    vec = jnp.transpose(small_all, (1, 0, 2)).reshape(16, width).astype(F32)
-    steps = (small_all[:, 9, :seqs].astype(F32) * 64 + small_all[:, 9, seqs : 2 * seqs].astype(F32)).reshape(-1)
     half = width // 2
-    place = si * rows + jnp.arange(rows)
-    freq = jnp.exp(-math.log(10000.0) * (place % half).astype(F32) / half)
-    angles = steps[:, None] * freq[None, :]
-    sinus_rows = jnp.where(place < half, jnp.sin(angles), jnp.cos(angles)).astype(BF16)
-    te = dot(sinus_rows, w_time)
-    up_own, up_y, up_c, up_yc = step(up_kernel, [w_up], [((rows, ff), BF16)] * 4, 2)
-    ups = [up_own, swap(up_y, "y"), swap(up_c, "c"), across_seq(up_yc)]
-    (te_a,) = step(add_kernel, [te, swap(te, "y")], [((4 * seqs, width), F32)], 1, behind=[far_own])
-    te_b = swap(te_a, "c")
-    (go_send,) = step(pick_kernel, [grad_out], [((piece, width), BF16)], 1)
-    go_far = swap(go_send, "h")
-
-    attn_in, qkv_t, o_full, o_send, lse, w_t = step(
-        attend_kernel, [*toks, *fars, te_a, te_b, vec, small_all, wq_own, wq_y, wq_c, wq_yc],
-        [((4, own, width), BF16), ((4, 3 * part, own), BF16), ((4, part, own), F32), ((4, part, own), BF16),
-         ((4 * heads, 8, own), F32), ((3 * part, width), BF16)],
-        15, [pltpu.VMEM((4, rows, 3 * part), BF16)], ups[1:],
-    )
-    attn = members(o_send)
-    (go_own,) = step(own_kernel, [grad_out, go_far], [((own, width), BF16)], 1)
-    go_all = lax.all_gather(go_own, ("y", "c"))
-    mlp_own, hidden_two, a_own, a_y, a_c, a_yc = step(
-        branch_kernel, [attn, w_out_f, tok_own, far_own, te_a, te_b, vec],
-        [((own, width), BF16), ((own, width), F32)] + [((part, own), BF16)] * 4, 3,
-    )
-    mlp_y = swap(mlp_own, "y")
-    mlp_c = swap(mlp_own, "c")
-    mlp_yc = swap(mlp_y, "c")
-    mlps = [mlp_own, mlp_y, mlp_c, mlp_yc]
-    a_s = [a_own, swap(a_y, "y"), swap(a_c, "c"), across_seq(a_yc)]
-    two = (2, own, width)
-    gm_own, gm_far, gm_send, out_own, out_far, out_send, act_all, gp_all = step(
-        feed_kernel, [*mlps, go_all, *ups, w_down, b_up.astype(F32).reshape(1, ff)],
-        [*[((own, width), F32)] * 2, (two, BF16), *[((own, width), F32)] * 2, (two, BF16), *[((4, own, ff), BF16)] * 2], 10,
-        [pltpu.VMEM((width, ff), BF16)], a_s[1:],
-    )
-    gm_c = swap(gm_send, "c")
-    out_c = swap(out_send, "c")
-    (gm_pair,) = step(second_kernel, [gm_far, gm_c], [((own, width), BF16)], 1)
-    gm_y = swap(gm_pair, "y")
-    quarters = [((ff // 4 + 16, width), BF16)] * 4 + [((4, rows // 4, ff), BF16)] * 4
-    *gd, gu_own, gu_x, gu_z, gu_d = step(
-        feed_grad_kernel, [*mlps, go_all, act_all, gp_all], quarters, 7, [pltpu.VMEM((width, width), BF16)]
-    )
-    gds = trade4(*gd)
-    grad_two, branch, ga_send, sums_two = step(
-        back_kernel, [gm_own, gm_c, gm_y, hidden_two, go_own, w_out_f, vec],
-        [((own, width), F32), ((own, width), BF16), ((4, part, own), BF16), ((8, width), F32)], 4,
-    )
-    ga = members(ga_send)
-    branch_s = lax.all_gather(branch, ("y", "c"))
-    (out_pair,) = step(second_kernel, [out_far, out_c], [((own, width), BF16)], 1)
-    out_y = swap(out_pair, "y")
-    gus = trade4(gu_own, gu_x, gu_z, gu_d)
-
-    dqkv_t, gh_own, gh_x, gh_z, gh_d, sums_one = step(
-        attend_back_kernel, [qkv_t, lse, o_full, ga, w_t, *toks, *fars, te_a, te_b, vec],
-        [((4, 3 * part, own), BF16)] + [((own, width), BF16)] * 4 + [((8, width), F32)],
-        15, [pltpu.VMEM((HEAD_DIM, 4 * own), F32)] * 2,
-    )
-    ghs = trade4(gh_own, gh_x, gh_z, gh_d)
-    (gd_sum,) = step(total4_kernel, gds, [((ff // 4 + 16, width), BF16)], 1)
-    gd_h = swap(gd_sum, "h")
+    hidden_low = ((own, width), BF16)
+    hidden_full = ((own, width), F32)
+    down = ((ff // 4 + 16, width), BF16)
+    up = ((4, rows // 4, ff), BF16)
+    packed = ((ff // 4 + 16 + rows, width), BF16)
     chain = (2, rows + 32, 3 * part)
-    ch_keep, ch_give = step(qkv_grad_kernel, [attn_in, dqkv_t, sums_two, sums_one], [(chain, BF16), (chain, BF16)], 5)
-    ch_c = swap(ch_give, "c")
-    (gu_sum,) = step(total4_kernel, gus, [((4, rows // 4, ff), BF16)], 1)
-    gu_h = swap(gu_sum, "h")
-    folded = ((rows // 4 + rows // 12, 3 * part), BF16)
-    wo = step(out_grad_kernel, [*a_s, branch_s], [folded] * 4, 2, [pltpu.VMEM((rows, width), BF16)])
-    wos = trade4(*wo)
-    first, second = step(chain_kernel, [ch_keep, ch_c], [(chain[1:], BF16)] * 2, 1)
-    ch_y = swap(second, "y")
-    (gd_sum,) = step(both_kernel, [gd_sum, gd_h], [((ff // 4 + 16, width), BF16)], 1)
-    gds = gather4(gd_sum)
-    out_mine, out_other = step(
-        out_kernel, [hidden_two, out_own, out_c, out_y, vec], [((piece, width), BF16), ((piece, width), BF16)], 2
-    )
-    out_recv = swap(out_other, "h")
     joined = ((rows + 32 + rows // 3, 3 * part), BF16)
-    (now,) = step(join_kernel, [first, ch_y, *wos], [joined], 1)
-    ch_h = swap(now, "h")
-    (gu_sum,) = step(both_kernel, [gu_sum, gu_h], [((4, rows // 4, ff), BF16)], 1)
-    gu_s = lax.all_to_all(gu_sum, ("y", "c"), split_axis=0, concat_axis=0, tiled=True)
-    gt_mine, gt_other = step(
-        hidden_grad_kernel, [grad_two, *ghs], [((piece, width), BF16), ((piece, width), BF16)], 2
-    )
-    gt_recv = swap(gt_other, "h")
-    (now,) = step(both_kernel, [now, ch_h], [joined], 1)
-    gqs = gather4(now)
-    gus = gather4(gu_s)
-    (output,) = step(pair_kernel, [out_mine, out_recv], [((seqs, piece, width), BF16)], 1.5)
-    (grad_tokens,) = step(pair_kernel, [gt_mine, gt_recv], [((seqs, piece, width), BF16)], 1.5)
-    t_qkv, t_out, total_w_time, tv, embeds = step(
-        total_kernel, [*gqs, sinus_rows.astype(F32)],
-        [((rows, 3 * width), F32), ((4, rows // 4, width), F32), ((rows, width), F32), ((8, 3 * part), F32),
-         ((8, width), F32)],
-        3, [pltpu.VMEM((32, 3 * part), F32)],
-    )
-    t_down, t_up, t_small = step(
-        feed_total_kernel, [*gds, *gus],
-        [((4, ff // 4, width), F32), ((4, rows // 4, 4 * ff), F32), ((16, width), F32)], 4,
-    )
-    total_b_time = lax.dynamic_slice_in_dim(jnp.sum(embeds, 0), si * rows, rows, 0)
-    total_b_down = lax.dynamic_slice_in_dim(t_small[1], si * rows, rows, 0)
+    v = Values()
+
+    def sinusoid_at(steps, place):
+        freq = jnp.exp(-math.log(10000.0) * (place % half).astype(F32) / half)
+        angles = steps[:, None] * freq[None, :]
+        return jnp.where(place < half, jnp.sin(angles), jnp.cos(angles)).astype(BF16)
+
+    w_time_f = lax.all_gather(w_time, ("y", "c"), axis=0, tiled=True)
+    here = jnp.broadcast_to(pick(timestep, hi).astype(F32), (8,))
+    sinus_here = sinusoid_at(here, jnp.arange(width))
+
+    def token():
+        tok_own, tok_far, blank = step(token_kernel, 2, [tokens], [((piece, width), BF16)] * 2 + [((1, rows), BF16)])
+        v.blank = blank.reshape(rows)
+        v.far_own = swap(tok_far, "h")
+        v.toks = gather4(tok_own)
+        v.fars = gather4(v.far_own)
+
+    def small_parameters():
+        low_bits = (timestep % 64).astype(BF16)
+        high_bits = (timestep // 64).astype(BF16)
+        steps_row = jnp.concatenate([high_bits, low_bits, jnp.zeros((rows - 2 * seqs,), BF16)])
+        small = jnp.stack(
+            [b_time, ln1_gain, ln1_bias, b_query, b_value, b_out, ln2_gain, ln2_bias, b_down, steps_row] + [v.blank] * 6
+        )
+        v.small = lax.all_gather(small, ("y", "c"))
+        v.vec = jnp.transpose(v.small, (1, 0, 2)).reshape(16, width).astype(F32)
+
+    def column():
+        (blocks,) = step(column_kernel, 2, [w_qkv], [((4, rows, 3 * part), BF16)], behind=[v.small])
+        v.wq = shards(blocks)
+
+    def up_weights():
+        pieces = step(up_kernel, 2, [w_up], [((rows, ff), BF16)] * 4)
+        v.ups = [pieces[0], swap(pieces[1], "y"), swap(pieces[2], "c"), across_seq(pieces[3])]
+
+    def pick_grad():
+        (send,) = step(pick_kernel, 2, [grad_out], [((piece, width), BF16)])
+        v.go_far = swap(send, "h")
+
+    def attend():
+        v.attn_in, v.qkv_t, v.o_full, send, v.lse, v.w_t, v.te = step(attend_kernel, 15, [*v.toks, *v.fars, sinus_here, w_time_f, v.vec, v.small, v.wq],
+            [((4, own, width), BF16), ((4, 3 * part, own), BF16), ((4, part, own), F32), ((4, part, own), BF16),
+             ((4 * heads, 8, own), F32), ((3 * part, width), BF16), ((8, width), F32)], behind=[v.wq])
+        v.attn = members(send)
+
+    def own_grad():
+        v.go_own, copy = step(own_kernel, 2, [grad_out, v.go_far, w_out], [hidden_low, ((rows, width), BF16)])
+        v.w_out = lax.all_gather(copy, ("y", "c"), axis=0, tiled=True)
+        v.go_all = lax.all_gather(v.go_own, ("y", "c"))
+
+    def branch():
+        mlp, v.hidden_two, v.folds = step(branch_kernel, 30, [v.attn, v.w_out, v.toks[0], v.far_own, v.te, v.vec],
+            [hidden_low, hidden_full, ((4, part // 3, width), BF16)], behind=[*v.ups[1:]])
+        y = swap(mlp, "y")
+        v.mlps = [mlp, y, swap(mlp, "c"), swap(y, "c")]
+
+    def feed():
+        v.gm_own, v.gm_far, gm_send, v.out_own, v.out_far, out_send, v.act, v.gp = step(feed_kernel, 10,
+            [*v.mlps, v.go_all, *v.ups, w_down, b_up.astype(F32).reshape(1, ff), v.folds],
+            [hidden_full, hidden_low, ((2, own, width), BF16), hidden_full, hidden_low,
+             ((2 * own + 2 * part // 3, width), BF16), *[((4, own, ff), BF16)] * 2],
+            [pltpu.VMEM((width, ff), BF16)],
+        )
+        v.gm_c = swap(gm_send, "c")
+        v.out_c = swap(out_send, "c")
+
+    def gm_add():
+        (pair,) = step(second_kernel, 2, [v.gm_far, v.gm_c], [hidden_low])
+        v.gm_y = swap(pair, "y")
+
+    def feed_grad():
+        v.ps = trade4(*step(feed_grad_kernel, 7, [*v.mlps, v.go_all, v.act, v.gp], [packed] * 4,
+            [pltpu.VMEM((width, width), BF16)],
+        ))
+
+    def back():
+        v.grad_two, branch_low, send, v.sums_two, pair = step(back_kernel, 5,
+            [v.gm_own, v.gm_c, v.gm_y, v.hidden_two, v.go_own, v.w_out, v.vec, v.out_far, v.out_c,
+             v.folds],
+            [hidden_full, hidden_low, ((4, part, own), BF16), ((8, width), F32), ((own + 2 * part // 3, width), BF16)],
+        )
+        v.ga = members(send)
+        v.branch_s = lax.all_gather(branch_low, ("y", "c"))
+        v.out_y = swap(pair, "y")
+
+    def attend_back():
+        v.dqkv, gh, v.sums_one = step(attend_back_kernel, 15,
+            [v.qkv_t, v.lse, v.o_full, v.ga, v.w_t, *v.toks, *v.fars, v.te, v.vec],
+            [((4, 3 * part, own), BF16), ((4, own, width), BF16), ((8, width), F32)],
+            [pltpu.VMEM((HEAD_DIM, 4 * own), F32)] * 2,
+        )
+        v.gh = members(gh)
+
+    def p_sum():
+        v.d_low, v.u_low = step(pieces_kernel, 2, v.ps, [down, up])
+        v.d_h = swap(v.d_low, "h")
+        v.u_h = swap(v.u_low, "h")
+
+    def qkv_grad():
+        v.ch_keep, give = step(qkv_grad_kernel, 5, [v.attn_in, v.dqkv, v.sums_two, v.sums_one], [(chain, BF16)] * 2
+        )
+        v.ch_c = swap(give, "c")
+
+    def out_grad():
+        pieces = step(out_grad_kernel, 3, [v.folds, v.out_c, v.out_y, v.branch_s],
+            [((rows // 3, 3 * part), BF16)] * 4, [pltpu.VMEM((rows, width), BF16)],
+        )
+        v.wos = trade4(*pieces)
+
+    def chain_add():
+        v.first, second = step(chain_kernel, 2, [v.ch_keep, v.ch_c], [(chain[1:], BF16)] * 2)
+        v.ch_y = swap(second, "y")
+
+    def join():
+        (v.now,) = step(join_kernel, 2, [v.first, v.ch_y, *v.wos], [joined])
+        v.ch_h = swap(v.now, "h")
+
+    def out():
+        v.out_mine, other = step(out_kernel, 2, [v.hidden_two, v.out_own, v.out_c, v.out_y, v.vec],
+            [((piece, width), BF16)] * 2,
+        )
+        v.out_h = swap(other, "h")
+
+    def hidden():
+        v.gt_mine, other = step(hidden_grad_kernel, 3, [v.grad_two, v.gh], [((piece, width), BF16)] * 2)
+        v.gt_h = swap(other, "h")
+
+    def d_add():
+        (value,) = step(both_kernel, 2, [v.d_low, v.d_h], [down])
+        v.dg = gather4(value)
+
+    def u_add():
+        (value,) = step(both_kernel, 2, [v.u_low, v.u_h], [up])
+        v.gu_s = shards(value)
+        v.ug = gather4(v.gu_s)
+
+    def now_add():
+        (value,) = step(both_kernel, 2, [v.now, v.ch_h], [joined])
+        v.qg = gather4(value)
+
+    def pair():
+        v.grad_tokens, v.output = step(pair_kernel, 2, [v.gt_mine, v.out_mine, v.gt_h, v.out_h], [((seqs, piece, width), BF16)] * 2
+        )
+
+    def total():
+        steps = (v.small[:, 9, :seqs].astype(F32) * 64 + v.small[:, 9, seqs : 2 * seqs].astype(F32)).reshape(-1)
+        sinus_rows = sinusoid_at(steps, si * rows + jnp.arange(rows)).astype(F32)
+        v.w_qkv, v.t_out, v.w_time, v.tv, v.b_time = step(total_kernel, 3, [*v.qg, sinus_rows],
+            [((rows, 3 * width), F32), ((4, rows // 4, width), F32), ((rows, width), F32), ((8, 3 * part), F32),
+             ((1, rows), F32)],
+            [pltpu.VMEM((32, 3 * part), F32), pltpu.VMEM((8, width), F32)],
+        )
+
+    def down_total():
+        v.w_down, v.b_up, v.b_down = step(down_total_kernel, 3, v.dg, [((4, ff // 4, width), F32), ((1, ff), F32), ((1, rows), F32)]
+        )
+
+    def up_total():
+        (v.w_up,) = step(up_total_kernel, 3, v.ug, [((4, rows // 4, 4 * ff), F32)])
+
+    for run in (
+        token, small_parameters, pick_grad, column, up_weights, own_grad, attend, branch, feed, gm_add, feed_grad,
+        back, attend_back, out, p_sum, qkv_grad, chain_add, out_grad, join, d_add, hidden, u_add, now_add, down_total,
+        total, pair, up_total,
+    ):
+        run()
+    tv = v.tv
     return (
-        output, grad_tokens, total_w_time, total_b_time, tv[3, :rows], tv[4, :rows], t_qkv,
-        tv[5, :part], tv[5, 2 * part :], t_out.reshape(rows, width), tv[2, :rows], tv[0, :rows], tv[1, :rows],
-        t_up.reshape(rows, 4 * ff), t_small[0], t_down.reshape(ff, width), total_b_down,
+        v.output, v.grad_tokens, v.w_time, v.b_time.reshape(rows), tv[3, :rows], tv[4, :rows], v.w_qkv,
+        tv[5, :part], tv[5, 2 * part :], v.t_out.reshape(rows, width), tv[2, :rows], tv[0, :rows], tv[1, :rows],
+        v.w_up.reshape(rows, 4 * ff), v.b_up.reshape(ff), v.w_down.reshape(ff, width), v.b_down.reshape(rows),
     )
 
 

time: 309 us -> 290 us (0.939)
  waiting for transfers between devices: 90.4 us -> 76.6 us
  blocking collectives: 16.3 us -> 5.64 us
  starting transfers between devices: 59.7 us -> 65.8 us
    ppermute x9 -> x7, waiting for transfers between devices: 24.3 us -> 10.2 us  [across(): return lax.ppermute(value, ('zl', 'x'), [(i, i ^ 3) for i in range(4)])]
    all_to_all x1 -> x0, blocking collectives: 11.2 us -> none  [members(): lax.all_to_all(value, ('zl', 'x'), split_axis=0, concat_axis=0, tiled=True)]
    ppermute x43 -> x32, starting transfers between devices: 39.7 us -> 29.8 us  [swap(): return lax.ppermute(value, axis, [(0, 1), (1, 0)])]
    all_to_all x1 -> x3, starting transfers between devices: 3.65 us -> 11.4 us  [members(): lax.all_to_all(value, ('zl', 'x'), split_axis=0, concat_axis=0, tiled=True)]
    ppermute x43 -> x32, waiting for transfers between devices: 62.4 us -> 54.8 us  [swap(): return lax.ppermute(value, axis, [(0, 1), (1, 0)])]
    ppermute x9 -> x7, starting transfers between devices: 9.87 us -> 17 us  [across(): return lax.ppermute(value, ('zl', 'x'), [(i, i ^ 3) for i in range(4)])]
    all_to_all x1 -> x3, waiting for transfers between devices: 0.01 us -> 4.16 us  [members(): lax.all_to_all(value, ('zl', 'x'), split_axis=0, concat_axis=0, tiled=True)]
    ppermute x2 -> x1, waiting for transfers between devices: 3.59 us -> 7.26 us  [across_seq(): return lax.ppermute(value, ('y', 'c'), [(i, i ^ 3) for i in range(4)])]
  transfers between devices with their start and end apart: 59 -> 49, of which waited for: 19 -> 16; matrix products, arithmetic and copies ran while one was open for 1% -> 3% of each run, Pallas kernels for 30% -> 30%
where the time goes in v2:
time: 290 us; the launch traced here: 289 us
  Pallas kernels  106 us (37%)
  waiting for transfers between devices  76.6 us (26%)
  starting transfers between devices  65.8 us (23%)
  local copies, waits for them, and re-layouts  15.1 us (5%)
  between operations  15.1 us (5%)
  blocking collectives  5.64 us (2%)
  other arithmetic  4.2 us (1%)
    pallas_call x26, Pallas kernels, __call__(): pl.pallas_call(run, out_shape=shapes, in_specs=[pl.BlockSpec(memory_space...  106 us
    ppermute x32, waiting for transfers between devices, swap(): return lax.ppermute(value, axis, [(0, 1), (1, 0)])  54.8 us
    ppermute x32, starting transfers between devices, swap(): return lax.ppermute(value, axis, [(0, 1), (1, 0)])  29.8 us
    ppermute x7, starting transfers between devices, across(): return lax.ppermute(value, ('zl', 'x'), [(i, i ^ 3) for i in range(4)])  17 us
    unnamed x126, local copies, waits for them, and re-layouts  11.5 us
    all_to_all x3, starting transfers between devices, members(): lax.all_to_all(value, ('zl', 'x'), split_axis=0, concat_axis=0, tiled=True)  11.4 us
    ppermute x7, waiting for transfers between devices, across(): return lax.ppermute(value, ('zl', 'x'), [(i, i ^ 3) for i in range(4)])  10.2 us
    ppermute x1, waiting for transfers between devices, across_seq(): return lax.ppermute(value, ('y', 'c'), [(i, i ^ 3) for i in range(4)])  7.26 us
  transfers between devices with their start and end apart: 49, of which 16 were waited for; matrix products, arithmetic and copies ran while one was open for 3% of the time, Pallas kernels for 30%

profile of v2, /device:TPU:0, one launch (start us, length us, event | category | flops | bytes accessed | tf_op | source)
XLA Modules:
  0.0 288.6 jit_solution(17872493330406272067)
XLA Ops:
  9.6 4.0 %collective-permute-start.2 = (bf16[128,768]{1,0:T(8,128)(2,1)}, bf16[128,768]{1,0:T(8,128)(2,1)S(1)}, u32[]{:S(2)}, u32[]{:S(2)}) collective-permute-start(bf16[128,768]{1,0:T(8,128)(2,1)} %get-tuple-element.80.refs_2_.refs_1_.refs_3_.refs_6_), channel_id=1, source_target_pairs={{0,3},{1,2},{2,1},{3,0},{4,7},{5,6},{6,5},{7,4},{8,11},{9,10},{10,... | collective-permute-start | bytes 589832 | tf_op jit(solution)/shard_map/ppermute | solution.py:407
  16.1 3.0 %collective-permute-start.7 = (bf16[128,768]{1,0:T(8,128)(2,1)}, bf16[128,768]{1,0:T(8,128)(2,1)S(1)}, u32[]{:S(2)}, u32[]{:S(2)}) collective-permute-start(bf16[128,768]{1,0:T(8,128)(2,1)} %pick_kernel.1.refs_3_), channel_id=1, source_target_pairs={{0,4},{4,0},{1,5},{5,1},{2,6},{6,2},{3,7},{7,3},{8,12},{12,8},{9,1... | collective-permute-start | bytes 589832 | tf_op jit(solution)/shard_map/ppermute | solution.py:403
  19.5 5.6 %all-gather = bf16[64,192]{1,0:T(8,128)(2,1)} all-gather(bf16[16,192]{1,0:T(8,128)(2,1)S(1)} %stack.59), channel_id=2, replica_groups=mesh['y'=2,'c'=2,'h'=2,'zl'=2,'x'=2] {'y','c'}, dimensions={0}, use_global_device_ids=true | all-gather | bytes 30720 | tf_op jit(solution)/shard_map/all_gather | solution.py:971
  25.1 2.2 column_kernel.1.refs_2_
  27.3 3.7 %all-to-all-start = ((bf16[4,192,576]{2,1,0:T(8,128)(2,1)}), bf16[4,192,576]{2,1,0:T(8,128)(2,1)S(1)}, u32[]{:S(2)}, u32[]{:S(2)}) async-start(bf16[4,192,576]{2,1,0:T(8,128)(2,1)} %column_kernel.1.refs_2_), calls=%async_computation | async-start | bytes 1966080 | tf_op jit(solution)/shard_map/all_to_all | solution.py:927
  33.8 2.4 up_kernel.1
  36.1 2.9 %collective-permute-start.6 = (bf16[128,768]{1,0:T(8,128)(2,1)S(1)}, bf16[128,768]{1,0:T(8,128)(2,1)S(1)}, u32[]{:S(2)}, u32[]{:S(2)}) collective-permute-start(bf16[128,768]{1,0:T(8,128)(2,1)S(1)} %collective-permute-done.3.refs_5_.refs_4_.refs_10_), channel_id=1, source_target_pairs={{0,3},{1,2},{2,1},{3,0},{4,7},{5,6},{6,5},{7,4},{8,11},{9,10},{10,... | collective-permute-start | bytes 589832 | tf_op jit(solution)/shard_map/ppermute | solution.py:407
  41.8 3.0 %collective-permute-done.6.refs_8_.refs_13_ = bf16[128,768]{1,0:T(8,128)(2,1)S(1)} collective-permute-done((bf16[128,768]{1,0:T(8,128)(2,1)S(1)}, bf16[128,768]{1,0:T(8,128)(2,1)S(1)}, u32[]{:S(2)}, u32[]{:S(2)}) %collective-permute-start.6) | collective-permute-done | bytes 196640 | tf_op jit(solution)/shard_map/ppermute | solution.py:407
  44.9 4.0 %collective-permute-done.5.refs_7_.refs_12_ = bf16[128,768]{1,0:T(8,128)(2,1)S(1)} collective-permute-done((bf16[128,768]{1,0:T(8,128)(2,1)S(1)}, bf16[128,768]{1,0:T(8,128)(2,1)S(1)}, u32[]{:S(2)}, u32[]{:S(2)}) %collective-permute-start.5) | collective-permute-done | bytes 196640 | tf_op jit(solution)/shard_map/ppermute | solution.py:403
  50.0 16.0 %attend_kernel.1 = (bf16[4,256,768]{2,1,0:T(8,128)(2,1)}, bf16[4,576,256]{2,1,0:T(8,128)(2,1)}, f32[4,192,256]{2,1,0:T(8,128)}, bf16[4,192,256]{2,1,0:T(8,128)(2...) custom-call(s32[3]{0:T(128)} %pad_add_fusion.refs_0_, ...), custom_call_target="tpu_custom_call" | custom-call | flops 17250000896 | bytes 1 | tf_op jit(solution)/shard_map/attend_kernel/pallas_call | solution.py:437
  66.0 3.7 %all-to-all-start.1 = ((bf16[4,192,256]{2,1,0:T(8,128)(2,1)}), bf16[4,192,256]{2,1,0:T(8,128)(2,1)S(1)}, u32[]{:S(2)}, u32[]{:S(2)}) async-start(bf16[4,192,256]{2,1,0:T(8,128)(2,1)} %get-tuple-element.85), calls=%async_computation.1 | async-start | bytes 786432 | tf_op jit(solution)/shard_map/all_to_all | solution.py:924
  71.9 7.8 %collective-permute-done.8.refs_7_ = bf16[192,768]{1,0:T(8,128)(2,1)S(1)} collective-permute-done((bf16[192,768]{1,0:T(8,128)(2,1)S(1)}, bf16[192,768]{1,0:T(8,128)(2,1)S(1)}, u32[]{:S(2)}, u32[]{:S(2)}) %collective-permute-start.8) | collective-permute-done | bytes 294944 | tf_op jit(solution)/shard_map/ppermute | solution.py:403
  79.7 7.3 %collective-permute-done.10.refs_9_ = bf16[192,768]{1,0:T(8,128)(2,1)S(1)} collective-permute-done((bf16[192,768]{1,0:T(8,128)(2,1)S(1)}, bf16[192,768]{1,0:T(8,128)(2,1)S(1)}, u32[]{:S(2)}, u32[]{:S(2)}) %collective-permute-start.10) | collective-permute-done | bytes 294944 | tf_op jit(solution)/shard_map/ppermute | solution.py:936
  87.8 3.2 %branch_kernel.1 = (bf16[256,768]{1,0:T(8,128)(2,1)}, f32[256,768]{1,0:T(8,128)}, bf16[4,64,768]{2,1,0:T(8,128)(2,1)}) custom-call(s32[3]{0:T(128)} %pad_add_fusion.refs_0_, bf16[4,192,256]{2,1,0:T(8,128)(2,1)} %copy-done.3, bf16[768,768]{1,0:T(8,128)(2,1)} %all-gather.10.cloned.1.call-done.refs_2_.refs_6_, ...), custom_call_target="tpu_custom_call" | custom-call | flops 34500001792 | bytes 1 | tf_op jit(solution)/shard_map/branch_kernel/pallas_call | solution.py:437
  91.1 2.4 collective-permute-start.12
  93.5 9.8 %collective-permute-done.11.refs_2_ = bf16[256,768]{1,0:T(8,128)(2,1)S(1)} collective-permute-done((bf16[256,768]{1,0:T(8,128)(2,1)}, bf16[256,768]{1,0:T(8,128)(2,1)S(1)}, u32[]{:S(2)}, u32[]{:S(2)}) %collective-permute-start.11) | collective-permute-done | bytes 393248 | tf_op jit(solution)/shard_map/ppermute | solution.py:403
  105.7 9.9 %feed_kernel.1 = (f32[256,768]{1,0:T(8,128)}, bf16[256,768]{1,0:T(8,128)(2,1)}, bf16[2,256,768]{2,1,0:T(8,128)(2,1)}, f32[256,768]{1,0:T(8,128)}, bf16[256,768]{...) custom-call(s32[3]{0:T(128)} %pad_add_fusion.refs_0_, ...), custom_call_target="tpu_custom_call" | custom-call | flops 11500000256 | bytes 1 | tf_op jit(solution)/shard_map/feed_kernel/pallas_call | solution.py:437
  119.0 2.1 second_kernel.1.refs_8_
  121.1 7.6 %feed_grad_kernel.1 = (bf16[400,768]{1,0:T(8,128)(2,1)}, bf16[400,768]{1,0:T(8,128)(2,1)}, bf16[400,768]{1,0:T(8,128)(2,1)}, bf16[400,768]{1,0:T(8,128)(2,1)}) custom-call(s32[3]{0:T(128)} %pad_add_fusion.refs_0_, bf16[256,768]{1,0:T(8,128)(2,1)} %get-tuple-element.92.refs_1_.refs_13_, bf16[256,768]{1,0:T(8,128)(2,1)} %copy-done.13, ...), custom_call_target="tpu_custom_call" | custom-call | flops 8049999872 | bytes 1 | tf_op jit(solution)/shard_map/feed_grad_kernel/pallas_call | solution.py:437
  128.7 3.8 %collective-permute-done.15.refs_3_ = bf16[256,768]{1,0:T(8,128)(2,1)S(1)} collective-permute-done((bf16[256,768]{1,0:T(8,128)(2,1)}, bf16[256,768]{1,0:T(8,128)(2,1)S(1)}, u32[]{:S(2)}, u32[]{:S(2)}) %collective-permute-start.15) | collective-permute-done | bytes 393248 | tf_op jit(solution)/shard_map/ppermute | solution.py:403
  133.2 5.1 %back_kernel.1 = (f32[256,768]{1,0:T(8,128)}, bf16[256,768]{1,0:T(8,128)(2,1)}, bf16[4,192,256]{2,1,0:T(8,128)(2,1)}, f32[8,768]{1,0:T(8,128)}, bf16[384,768]{1,0:T(8,128)(2,1)}) custom-call(s32[3]{0:T(128)} %pad_add_fusion.refs_0_, f32[256,768]{1,0:T(8,128)} %get-tuple-element.94.refs_3_.refs_1_, bf16[2,256,768]{2,1,0:T(8,128)(2,1)} %copy-done.9, ...), custom_call_target="tpu_custom_call" | custom-call | flops 5750000128 | bytes 1 | tf_op jit(solution)/shard_map/back_kernel/pallas_call | solution.py:437
  138.3 4.2 %all-to-all-start.2 = ((bf16[4,192,256]{2,1,0:T(8,128)(2,1)}), bf16[4,192,256]{2,1,0:T(8,128)(2,1)S(1)}, u32[]{:S(2)}, u32[]{:S(2)}) async-start(bf16[4,192,256]{2,1,0:T(8,128)(2,1)} %get-tuple-element.107), calls=%async_computation.2 | async-start | bytes 786432 | tf_op jit(solution)/shard_map/all_to_all | solution.py:924
  146.4 4.2 %all-to-all-done.2.refs_4_ = bf16[4,192,256]{2,1,0:T(8,128)(2,1)S(1)} async-done(((bf16[4,192,256]{2,1,0:T(8,128)(2,1)}), bf16[4,192,256]{2,1,0:T(8,128)(2,1)S(1)}, u32[]{:S(2)}, u32[]{:S(2)}) %all-to-all-start.2) | async-done | bytes 393248 | tf_op jit(solution)/shard_map/all_to_all | solution.py:924
  151.3 14.8 %attend_back_kernel.1 = (bf16[4,576,256]{2,1,0:T(8,128)(2,1)}, bf16[4,256,768]{2,1,0:T(8,128)(2,1)}, f32[8,768]{1,0:T(8,128)}) custom-call(s32[3]{0:T(128)} %pad_add_fusion.refs_0_, bf16[4,576,256]{2,1,0:T(8,128)(2,1)} %get-tuple-element.104.refs_1_, f32[12,8,256]{2,1,0:T(8,128)} %get-tuple-element.105.refs_2_, f32[4,192,256]{2,1,0:T(8,128)} %get-tuple-element.106.refs_3_, ...), custom_call_target="tpu_custom_call" | custom-call | flops 17250000896 | bytes 1 | tf_op jit(solution)/shard_map/attend_back_kernel/pallas_call | solution.py:437
  166.1 3.6 %all-to-all-start.3 = ((bf16[4,256,768]{2,1,0:T(8,128)(2,1)}), bf16[4,256,768]{2,1,0:T(8,128)(2,1)S(1)}, u32[]{:S(2)}, u32[]{:S(2)}) async-start(bf16[4,256,768]{2,1,0:T(8,128)(2,1)} %get-tuple-element.109), calls=%async_computation.3 | async-start | bytes 3145728 | tf_op jit(solution)/shard_map/all_to_all | solution.py:924
  169.7 2.7 out_kernel.1
  172.4 5.6 %collective-permute-done.19.refs_4_ = bf16[400,768]{1,0:T(8,128)(2,1)} collective-permute-done((bf16[400,768]{1,0:T(8,128)(2,1)S(1)}, bf16[400,768]{1,0:T(8,128)(2,1)}, u32[]{:S(2)}, u32[]{:S(2)}) %collective-permute-start.19) | collective-permute-done | bytes 614432 | tf_op jit(solution)/shard_map/ppermute | solution.py:407
  178.0 2.7 pieces_kernel.1
  180.6 4.9 %qkv_grad_kernel.1 = (bf16[2,224,576]{2,1,0:T(8,128)(2,1)}, bf16[2,224,576]{2,1,0:T(8,128)(2,1)}) custom-call(s32[3]{0:T(128)} %pad_add_fusion.refs_0_, bf16[4,256,768]{2,1,0:T(8,128)(2,1)} %get-tuple-element.91.refs_10_.refs_1_, bf16[4,576,256]{2,1,0:T(8,128)(2,1)} %get-tuple-element.115.refs_6_.refs_2_, f32[8,768]{1,0:T(8,128)} %get-tuple-element.118.refs_3_, ...), custom_call_target="tpu_custom_call" | custom-call | flops 5750000128 | bytes 1 | tf_op jit(solution)/shard_map/qkv_grad_kernel/pallas_call | solution.py:437
  186.5 2.8 collective-permute-start.21
  190.1 2.1 chain_kernel.1
  192.5 3.3 %out_grad_kernel.1 = (bf16[64,576]{1,0:T(8,128)(2,1)}, bf16[64,576]{1,0:T(8,128)(2,1)}, bf16[64,576]{1,0:T(8,128)(2,1)}, bf16[64,576]{1,0:T(8,128)(2,1)}) custom-call(s32[3]{0:T(128)} %pad_add_fusion.refs_0_, bf16[4,64,768]{2,1,0:T(8,128)(2,1)} %get-tuple-element.93.refs_12_.refs_10_.refs_1_, bf16[640,768]{1,0:T(8,128)(2,1)} %copy-done.8, ...), custom_call_target="tpu_custom_call" | custom-call | flops 3449999872 | bytes 1 | tf_op jit(solution)/shard_map/out_grad_kernel/pallas_call | solution.py:437
  196.4 2.9 %collective-permute-start.26 = (bf16[64,576]{1,0:T(8,128)(2,1)}, bf16[64,576]{1,0:T(8,128)(2,1)S(1)}, u32[]{:S(2)}, u32[]{:S(2)}) collective-permute-start(bf16[64,576]{1,0:T(8,128)(2,1)} %get-tuple-element.128), channel_id=1, source_target_pairs={{0,3},{1,2},{2,1},{3,0},{4,7},{5,6},{6,5},{7,4},{8,11},{9,10},{10,... | collective-permute-start | bytes 221192 | tf_op jit(solution)/shard_map/ppermute | solution.py:407
  199.3 2.1 collective-permute-done.23.refs_2_
  202.5 2.6 collective-permute-done.25.refs_5_
  211.9 2.3 collective-permute-start.35
  215.4 3.0 %collective-permute-start.29 = (bf16[288,576]{1,0:T(8,128)(2,1)S(1)}, bf16[288,576]{1,0:T(8,128)(2,1)S(1)}, u32[]{:S(2)}, u32[]{:S(2)}) collective-permute-start(bf16[288,576]{1,0:T(8,128)(2,1)S(1)} %copy-done.20), channel_id=1, source_target_pairs={{0,4},{4,0},{1,5},{5,1},{2,6},{6,2},{3,7},{7,3},{8,12},{12,8},{9,1... | collective-permute-start | bytes 995336 | tf_op jit(solution)/shard_map/ppermute | solution.py:403
  219.5 2.6 hidden_grad_kernel.1
  223.9 8.2 %collective-permute-done.29.refs_2_ = bf16[288,576]{1,0:T(8,128)(2,1)S(1)} collective-permute-done((bf16[288,576]{1,0:T(8,128)(2,1)S(1)}, bf16[288,576]{1,0:T(8,128)(2,1)S(1)}, u32[]{:S(2)}, u32[]{:S(2)}) %collective-permute-start.29) | collective-permute-done | bytes 331808 | tf_op jit(solution)/shard_map/ppermute | solution.py:403
  234.8 5.7 %collective-permute-start.33 = (bf16[288,576]{1,0:T(8,128)(2,1)}, bf16[288,576]{1,0:T(8,128)(2,1)S(1)}, u32[]{:S(2)}, u32[]{:S(2)}) collective-permute-start(bf16[288,576]{1,0:T(8,128)(2,1)} %both_kernel.5.refs_5_.refs_1_), channel_id=1, source_target_pairs={{0,3},{1,2},{2,1},{3,0},{4,7},{5,6},{6,5},{7,4},{8,11},{9,10},{10,... | collective-permute-start | bytes 995336 | tf_op jit(solution)/shard_map/ppermute | solution.py:407
  243.9 3.5 %all-to-all-start.4 = ((bf16[4,48,768]{2,1,0:T(8,128)(2,1)}), bf16[4,48,768]{2,1,0:T(8,128)(2,1)S(1)}, u32[]{:S(2)}, u32[]{:S(2)}) async-start(bf16[4,48,768]{2,1,0:T(8,128)(2,1)} %both_kernel.4.refs_3_), calls=%async_computation.4 | async-start | bytes 589824 | tf_op jit(solution)/shard_map/all_to_all | solution.py:927
  247.5 2.9 %collective-permute-start.27 = (bf16[128,768]{1,0:T(8,128)(2,1)S(1)}, bf16[128,768]{1,0:T(8,128)(2,1)S(1)}, u32[]{:S(2)}, u32[]{:S(2)}) collective-permute-start(bf16[128,768]{1,0:T(8,128)(2,1)S(1)} %copy-done.45), channel_id=1, source_target_pairs={{0,4},{4,0},{1,5},{5,1},{2,6},{6,2},{3,7},{7,3},{8,12},{12,8},{9,1... | collective-permute-start | bytes 589832 | tf_op jit(solution)/shard_map/ppermute | solution.py:403
  250.4 2.9 down_total_kernel.1
  256.1 9.7 %collective-permute-done.32.refs_3_ = bf16[288,576]{1,0:T(8,128)(2,1)S(1)} collective-permute-done((bf16[288,576]{1,0:T(8,128)(2,1)}, bf16[288,576]{1,0:T(8,128)(2,1)S(1)}, u32[]{:S(2)}, u32[]{:S(2)}) %collective-permute-start.32) | collective-permute-done | bytes 331808 | tf_op jit(solution)/shard_map/ppermute | solution.py:403
  266.7 3.5 %total_kernel.1 = (f32[192,2304]{1,0:T(8,128)}, f32[4,48,768]{2,1,0:T(8,128)}, f32[192,768]{1,0:T(8,128)}, f32[8,576]{1,0:T(8,128)}, f32[1,192]{1,0:T(1,128)}) custom-call(s32[3]{0:T(128)} %pad_add_fusion.refs_0_, bf16[288,576]{1,0:T(8,128)(2,1)} %both_kernel.5.refs_5_.refs_1_, bf16[288,576]{1,0:T(8,128)(2,1)} %copy-done.19, bf16[288,576]{1,0:T(8,128)(2,1)} %copy-done.18, ...), custom_call_target="tpu_custom_call" | custom-call | flops 3449999872 | bytes 1 | tf_op jit(solution)/shard_map/total_kernel/pallas_call | solution.py:437
  270.9 2.1 pair_kernel.1
  274.5 3.8 %collective-permute-done.38.refs_3_ = bf16[4,48,768]{2,1,0:T(8,128)(2,1)S(1)} collective-permute-done((bf16[4,48,768]{2,1,0:T(8,128)(2,1)S(1)}, bf16[4,48,768]{2,1,0:T(8,128)(2,1)S(1)}, u32[]{:S(2)}, u32[]{:S(2)}) %collective-permute-start.38) | collective-permute-done | bytes 294944 | tf_op jit(solution)/shard_map/ppermute | solution.py:403
  279.2 2.8 up_total_kernel.1
  (237 shorter events, 52.9 us)
Async XLA Ops:
  7.2 41.8 %all-gather.8.cloned.1.call-start = ((), (), s32[]{:S(2)}) async-start(), calls=%async_computation.5 | async-start | bytes 1474560 | tf_op jit(solution)/shard_map/all_gather | solution.py:953
  9.6 29.9 %collective-permute-start.2 = (bf16[128,768]{1,0:T(8,128)(2,1)}, bf16[128,768]{1,0:T(8,128)(2,1)S(1)}, u32[]{:S(2)}, u32[]{:S(2)}) collective-permute-start(bf16[128,768]{1,0:T(8,128)(2,1)} %get-tuple-element.80.refs_2_.refs_1_.refs_3_.refs_6_), channel_id=1, source_target_pairs={{0,3},{1,2},{2,1},{3,0},{4,7},{5,6},{6,5},{7,4},{8,11},{9,10},{10,... | collective-permute-start | bytes 589832 | tf_op jit(solution)/shard_map/ppermute | solution.py:407
  13.5 28.3 %collective-permute-start.1 = (bf16[128,768]{1,0:T(8,128)(2,1)}, bf16[128,768]{1,0:T(8,128)(2,1)S(1)}, u32[]{:S(2)}, u32[]{:S(2)}) collective-permute-start(bf16[128,768]{1,0:T(8,128)(2,1)} %get-tuple-element.80.refs_2_.refs_1_.refs_3_.refs_6_), channel_id=1, source_target_pairs={{0,2},{2,0},{1,3},{3,1},{4,6},{6,4},{5,7},{7,5},{8,10},{10,8},{9,1... | collective-permute-start | bytes 589832 | tf_op jit(solution)/shard_map/ppermute | solution.py:403
  14.0 27.8 %collective-permute-start = (bf16[128,768]{1,0:T(8,128)(2,1)}, bf16[128,768]{1,0:T(8,128)(2,1)S(1)}, u32[]{:S(2)}, u32[]{:S(2)}) collective-permute-start(bf16[128,768]{1,0:T(8,128)(2,1)} %get-tuple-element.80.refs_2_.refs_1_.refs_3_.refs_6_), channel_id=1, source_target_pairs={{0,1},{1,0},{2,3},{3,2},{4,5},{5,4},{6,7},{7,6},{8,9},{9,8},{10,11... | collective-permute-start | bytes 589832 | tf_op jit(solution)/shard_map/ppermute | solution.py:403
  16.1 23.0 %collective-permute-start.7 = (bf16[128,768]{1,0:T(8,128)(2,1)}, bf16[128,768]{1,0:T(8,128)(2,1)S(1)}, u32[]{:S(2)}, u32[]{:S(2)}) collective-permute-start(bf16[128,768]{1,0:T(8,128)(2,1)} %pick_kernel.1.refs_3_), channel_id=1, source_target_pairs={{0,4},{4,0},{1,5},{5,1},{2,6},{6,2},{3,7},{7,3},{8,12},{12,8},{9,1... | collective-permute-start | bytes 589832 | tf_op jit(solution)/shard_map/ppermute | solution.py:403
  19.1 17.1 %collective-permute-start.3 = (bf16[128,768]{1,0:T(8,128)(2,1)S(1)}, bf16[128,768]{1,0:T(8,128)(2,1)S(1)}, u32[]{:S(2)}, u32[]{:S(2)}) collective-permute-start(bf16[128,768]{1,0:T(8,128)(2,1)S(1)} %copy-done.47), channel_id=1, source_target_pairs={{0,4},{4,0},{1,5},{5,1},{2,6},{6,2},{3,7},{7,3},{8,12},{12,8},{9,1... | collective-permute-start | bytes 589832 | tf_op jit(solution)/shard_map/ppermute | solution.py:403
  27.3 21.6 %all-to-all-start = ((bf16[4,192,576]{2,1,0:T(8,128)(2,1)}), bf16[4,192,576]{2,1,0:T(8,128)(2,1)S(1)}, u32[]{:S(2)}, u32[]{:S(2)}) async-start(bf16[4,192,576]{2,1,0:T(8,128)(2,1)} %column_kernel.1.refs_2_), calls=%async_computation | async-start | bytes 1966080 | tf_op jit(solution)/shard_map/all_to_all | solution.py:927
  31.0 56.0 %all-gather.10.cloned.1.call-start = ((), (), s32[]{:S(2)}) async-start(), calls=%async_computation.6 | async-start | bytes 1474560 | tf_op jit(solution)/shard_map/all_gather | solution.py:994
  36.1 8.8 %collective-permute-start.6 = (bf16[128,768]{1,0:T(8,128)(2,1)S(1)}, bf16[128,768]{1,0:T(8,128)(2,1)S(1)}, u32[]{:S(2)}, u32[]{:S(2)}) collective-permute-start(bf16[128,768]{1,0:T(8,128)(2,1)S(1)} %collective-permute-done.3.refs_5_.refs_4_.refs_10_), channel_id=1, source_target_pairs={{0,3},{1,2},{2,1},{3,0},{4,7},{5,6},{6,5},{7,4},{8,11},{9,10},{10,... | collective-permute-start | bytes 589832 | tf_op jit(solution)/shard_map/ppermute | solution.py:407
  39.0 9.9 %collective-permute-start.5 = (bf16[128,768]{1,0:T(8,128)(2,1)S(1)}, bf16[128,768]{1,0:T(8,128)(2,1)S(1)}, u32[]{:S(2)}, u32[]{:S(2)}) collective-permute-start(bf16[128,768]{1,0:T(8,128)(2,1)S(1)} %collective-permute-done.3.refs_5_.refs_4_.refs_10_), channel_id=1, source_target_pairs={{0,2},{2,0},{1,3},{3,1},{4,6},{6,4},{5,7},{7,5},{8,10},{10,8},{9,1... | collective-permute-start | bytes 589832 | tf_op jit(solution)/shard_map/ppermute | solution.py:403
  39.5 9.5 %collective-permute-start.4 = (bf16[128,768]{1,0:T(8,128)(2,1)S(1)}, bf16[128,768]{1,0:T(8,128)(2,1)S(1)}, u32[]{:S(2)}, u32[]{:S(2)}) collective-permute-start(bf16[128,768]{1,0:T(8,128)(2,1)S(1)} %collective-permute-done.3.refs_5_.refs_4_.refs_10_), channel_id=1, source_target_pairs={{0,1},{1,0},{2,3},{3,2},{4,5},{5,4},{6,7},{7,6},{8,9},{9,8},{10,11... | collective-permute-start | bytes 589832 | tf_op jit(solution)/shard_map/ppermute | solution.py:403
  66.0 21.0 %all-to-all-start.1 = ((bf16[4,192,256]{2,1,0:T(8,128)(2,1)}), bf16[4,192,256]{2,1,0:T(8,128)(2,1)S(1)}, u32[]{:S(2)}, u32[]{:S(2)}) async-start(bf16[4,192,256]{2,1,0:T(8,128)(2,1)} %get-tuple-element.85), calls=%async_computation.1 | async-start | bytes 786432 | tf_op jit(solution)/shard_map/all_to_all | solution.py:924
  69.7 34.3 %all-gather.12.cloned.1.call-start = ((), (), s32[]{:S(2)}) async-start(), calls=%async_computation.7 | async-start | bytes 1966080 | tf_op jit(solution)/shard_map/all_gather | solution.py:995
  69.7 10.0 %collective-permute-start.8 = (bf16[192,768]{1,0:T(8,128)(2,1)S(1)}, bf16[192,768]{1,0:T(8,128)(2,1)S(1)}, u32[]{:S(2)}, u32[]{:S(2)}) collective-permute-start(bf16[192,768]{1,0:T(8,128)(2,1)S(1)} %copy-done.29), channel_id=1, source_target_pairs={{0,16},{16,0},{1,17},{17,1},{2,18},{18,2},{3,19},{19,3},{4,20},{20... | collective-permute-start | bytes 884744 | tf_op jit(solution)/shard_map/ppermute | solution.py:403
  71.5 8.2 %collective-permute-start.9 = (bf16[192,768]{1,0:T(8,128)(2,1)S(1)}, bf16[192,768]{1,0:T(8,128)(2,1)S(1)}, u32[]{:S(2)}, u32[]{:S(2)}) collective-permute-start(bf16[192,768]{1,0:T(8,128)(2,1)S(1)} %copy-done.28), channel_id=1, source_target_pairs={{0,8},{8,0},{1,9},{9,1},{2,10},{10,2},{3,11},{11,3},{4,12},{12,4},... | collective-permute-start | bytes 884744 | tf_op jit(solution)/shard_map/ppermute | solution.py:403
  71.5 15.5 %collective-permute-start.10 = (bf16[192,768]{1,0:T(8,128)(2,1)S(1)}, bf16[192,768]{1,0:T(8,128)(2,1)S(1)}, u32[]{:S(2)}, u32[]{:S(2)}) collective-permute-start(bf16[192,768]{1,0:T(8,128)(2,1)S(1)} %copy-done.27), channel_id=1, source_target_pairs={{0,24},{8,16},{16,8},{24,0},{1,25},{9,17},{17,9},{25,1},{2,26},{10... | collective-permute-start | bytes 884744 | tf_op jit(solution)/shard_map/ppermute | solution.py:936
  91.1 12.2 %collective-permute-start.11 = (bf16[256,768]{1,0:T(8,128)(2,1)}, bf16[256,768]{1,0:T(8,128)(2,1)S(1)}, u32[]{:S(2)}, u32[]{:S(2)}) collective-permute-start(bf16[256,768]{1,0:T(8,128)(2,1)} %get-tuple-element.92.refs_1_.refs_13_), channel_id=1, source_target_pairs={{0,16},{16,0},{1,17},{17,1},{2,18},{18,2},{3,19},{19,3},{4,20},{20... | collective-permute-start | bytes 1179656 | tf_op jit(solution)/shard_map/ppermute | solution.py:403
  91.1 12.9 %collective-permute-start.12 = (bf16[256,768]{1,0:T(8,128)(2,1)}, bf16[256,768]{1,0:T(8,128)(2,1)S(1)}, u32[]{:S(2)}, u32[]{:S(2)}) collective-permute-start(bf16[256,768]{1,0:T(8,128)(2,1)} %get-tuple-element.92.refs_1_.refs_13_), channel_id=1, source_target_pairs={{0,8},{8,0},{1,9},{9,1},{2,10},{10,2},{3,11},{11,3},{4,12},{12,4},... | collective-permute-start | bytes 1179656 | tf_op jit(solution)/shard_map/ppermute | solution.py:403
  115.6 2.5 collective-permute-start.14
  115.7 13.0 %collective-permute-start.16 = (bf16[640,768]{1,0:T(8,128)(2,1)}, bf16[640,768]{1,0:T(8,128)(2,1)S(1)}, u32[]{:S(2)}, u32[]{:S(2)}) collective-permute-start(bf16[640,768]{1,0:T(8,128)(2,1)} %get-tuple-element.99), channel_id=1, source_target_pairs={{0,8},{8,0},{1,9},{9,1},{2,10},{10,2},{3,11},{11,3},{4,12},{12,4},... | collective-permute-start | bytes 2949128 | tf_op jit(solution)/shard_map/ppermute | solution.py:403
  121.1 11.4 %collective-permute-start.15 = (bf16[256,768]{1,0:T(8,128)(2,1)}, bf16[256,768]{1,0:T(8,128)(2,1)S(1)}, u32[]{:S(2)}, u32[]{:S(2)}) collective-permute-start(bf16[256,768]{1,0:T(8,128)(2,1)} %second_kernel.1.refs_8_), channel_id=1, source_target_pairs={{0,16},{16,0},{1,17},{17,1},{2,18},{18,2},{3,19},{19,3},{4,20},{20... | collective-permute-start | bytes 1179656 | tf_op jit(solution)/shard_map/ppermute | solution.py:403
  138.3 12.2 %all-to-all-start.2 = ((bf16[4,192,256]{2,1,0:T(8,128)(2,1)}), bf16[4,192,256]{2,1,0:T(8,128)(2,1)S(1)}, u32[]{:S(2)}, u32[]{:S(2)}) async-start(bf16[4,192,256]{2,1,0:T(8,128)(2,1)} %get-tuple-element.107), calls=%async_computation.2 | async-start | bytes 786432 | tf_op jit(solution)/shard_map/all_to_all | solution.py:924
  142.5 50.0 %all-gather.14.cloned.1.call-start = ((), (), s32[]{:S(2)}) async-start(), calls=%async_computation.8 | async-start | bytes 1966080 | tf_op jit(solution)/shard_map/all_gather | solution.py:1029
  142.5 29.9 %collective-permute-start.17 = (bf16[400,768]{1,0:T(8,128)(2,1)}, bf16[400,768]{1,0:T(8,128)(2,1)S(1)}, u32[]{:S(2)}, u32[]{:S(2)}) collective-permute-start(bf16[400,768]{1,0:T(8,128)(2,1)} %get-tuple-element.110), channel_id=1, source_target_pairs={{0,1},{1,0},{2,3},{3,2},{4,5},{5,4},{6,7},{7,6},{8,9},{9,8},{10,11... | collective-permute-start | bytes 1843208 | tf_op jit(solution)/shard_map/ppermute | solution.py:403
  144.5 27.9 %collective-permute-start.18 = (bf16[400,768]{1,0:T(8,128)(2,1)}, bf16[400,768]{1,0:T(8,128)(2,1)}, u32[]{:S(2)}, u32[]{:S(2)}) collective-permute-start(bf16[400,768]{1,0:T(8,128)(2,1)} %get-tuple-element.111), channel_id=1, source_target_pairs={{0,2},{2,0},{1,3},{3,1},{4,6},{6,4},{5,7},{7,5},{8,10},{10,8},{9,1... | collective-permute-start | bytes 1843208 | tf_op jit(solution)/shard_map/ppermute | solution.py:403
  146.0 32.0 %collective-permute-start.19 = (bf16[400,768]{1,0:T(8,128)(2,1)S(1)}, bf16[400,768]{1,0:T(8,128)(2,1)}, u32[]{:S(2)}, u32[]{:S(2)}) collective-permute-start(bf16[400,768]{1,0:T(8,128)(2,1)S(1)} %copy-done.10), channel_id=1, source_target_pairs={{0,3},{1,2},{2,1},{3,0},{4,7},{5,6},{6,5},{7,4},{8,11},{9,10},{10,... | collective-permute-start | bytes 1843208 | tf_op jit(solution)/shard_map/ppermute | solution.py:407
  146.0 23.6 %collective-permute-start.20 = (bf16[384,768]{1,0:T(8,128)(2,1)}, bf16[384,768]{1,0:T(8,128)(2,1)}, u32[]{:S(2)}, u32[]{:S(2)}) collective-permute-start(bf16[384,768]{1,0:T(8,128)(2,1)} %get-tuple-element.114), channel_id=1, source_target_pairs={{0,16},{16,0},{1,17},{17,1},{2,18},{18,2},{3,19},{19,3},{4,20},{20... | collective-permute-start | bytes 1769480 | tf_op jit(solution)/shard_map/ppermute | solution.py:403
  166.1 52.3 %all-to-all-start.3 = ((bf16[4,256,768]{2,1,0:T(8,128)(2,1)}), bf16[4,256,768]{2,1,0:T(8,128)(2,1)S(1)}, u32[]{:S(2)}, u32[]{:S(2)}) async-start(bf16[4,256,768]{2,1,0:T(8,128)(2,1)} %get-tuple-element.109), calls=%async_computation.3 | async-start | bytes 3145728 | tf_op jit(solution)/shard_map/all_to_all | solution.py:924
  185.5 3.8 %collective-permute-start.22 = (bf16[2,224,576]{2,1,0:T(8,128)(2,1)}, bf16[2,224,576]{2,1,0:T(8,128)(2,1)S(1)}, u32[]{:S(2)}, u32[]{:S(2)}) collective-permute-start(bf16[2,224,576]{2,1,0:T(8,128)(2,1)} %get-tuple-element.121), channel_id=1, source_target_pairs={{0,8},{8,0},{1,9},{9,1},{2,10},{10,2},{3,11},{11,3},{4,12},{12,4},... | collective-permute-start | bytes 1548296 | tf_op jit(solution)/shard_map/ppermute | solution.py:403
  186.5 22.8 %collective-permute-start.21 = (bf16[208,768]{1,0:T(8,128)(2,1)S(1)}, bf16[208,768]{1,0:T(8,128)(2,1)S(1)}, u32[]{:S(2)}, u32[]{:S(2)}) collective-permute-start(bf16[208,768]{1,0:T(8,128)(2,1)S(1)} %copy-done.22), channel_id=1, source_target_pairs={{0,4},{4,0},{1,5},{5,1},{2,6},{6,2},{3,7},{7,3},{8,12},{12,8},{9,1... | collective-permute-start | bytes 958472 | tf_op jit(solution)/shard_map/ppermute | solution.py:403
  192.2 9.2 %collective-permute-start.23 = (bf16[224,576]{1,0:T(8,128)(2,1)}, bf16[224,576]{1,0:T(8,128)(2,1)S(1)}, u32[]{:S(2)}, u32[]{:S(2)}) collective-permute-start(bf16[224,576]{1,0:T(8,128)(2,1)} %get-tuple-element.123), channel_id=1, source_target_pairs={{0,16},{16,0},{1,17},{17,1},{2,18},{18,2},{3,19},{19,3},{4,20},{20... | collective-permute-start | bytes 774152 | tf_op jit(solution)/shard_map/ppermute | solution.py:403
  195.8 6.6 %collective-permute-start.24 = (bf16[64,576]{1,0:T(8,128)(2,1)}, bf16[64,576]{1,0:T(8,128)(2,1)S(1)}, u32[]{:S(2)}, u32[]{:S(2)}) collective-permute-start(bf16[64,576]{1,0:T(8,128)(2,1)} %get-tuple-element.126), channel_id=1, source_target_pairs={{0,1},{1,0},{2,3},{3,2},{4,5},{5,4},{6,7},{7,6},{8,9},{9,8},{10,11... | collective-permute-start | bytes 221192 | tf_op jit(solution)/shard_map/ppermute | solution.py:403
  196.4 8.7 %collective-permute-start.25 = (bf16[64,576]{1,0:T(8,128)(2,1)}, bf16[64,576]{1,0:T(8,128)(2,1)S(1)}, u32[]{:S(2)}, u32[]{:S(2)}) collective-permute-start(bf16[64,576]{1,0:T(8,128)(2,1)} %get-tuple-element.127), channel_id=1, source_target_pairs={{0,2},{2,0},{1,3},{3,1},{4,6},{6,4},{5,7},{7,5},{8,10},{10,8},{9,1... | collective-permute-start | bytes 221192 | tf_op jit(solution)/shard_map/ppermute | solution.py:403
  196.4 10.3 %collective-permute-start.26 = (bf16[64,576]{1,0:T(8,128)(2,1)}, bf16[64,576]{1,0:T(8,128)(2,1)S(1)}, u32[]{:S(2)}, u32[]{:S(2)}) collective-permute-start(bf16[64,576]{1,0:T(8,128)(2,1)} %get-tuple-element.128), channel_id=1, source_target_pairs={{0,3},{1,2},{2,1},{3,0},{4,7},{5,6},{6,5},{7,4},{8,11},{9,10},{10,... | collective-permute-start | bytes 221192 | tf_op jit(solution)/shard_map/ppermute | solution.py:407
  201.4 20.7 %collective-permute-start.30 = (bf16[4,48,768]{2,1,0:T(8,128)(2,1)}, bf16[4,48,768]{2,1,0:T(8,128)(2,1)}, u32[]{:S(2)}, u32[]{:S(2)}) collective-permute-start(bf16[4,48,768]{2,1,0:T(8,128)(2,1)} %get-tuple-element.132.refs_1_), channel_id=1, source_target_pairs={{0,4},{4,0},{1,5},{5,1},{2,6},{6,2},{3,7},{7,3},{8,12},{12,8},{9,1... | collective-permute-start | bytes 884744 | tf_op jit(solution)/shard_map/ppermute | solution.py:403
  211.9 29.7 %collective-permute-start.36 = (bf16[208,768]{1,0:T(8,128)(2,1)}, bf16[208,768]{1,0:T(8,128)(2,1)S(1)}, u32[]{:S(2)}, u32[]{:S(2)}) collective-permute-start(bf16[208,768]{1,0:T(8,128)(2,1)} %both_kernel.3.refs_3_.refs_1_), channel_id=1, source_target_pairs={{0,3},{1,2},{2,1},{3,0},{4,7},{5,6},{6,5},{7,4},{8,11},{9,10},{10,... | collective-permute-start | bytes 958472 | tf_op jit(solution)/shard_map/ppermute | solution.py:407
  211.9 35.4 %collective-permute-start.35 = (bf16[208,768]{1,0:T(8,128)(2,1)}, bf16[208,768]{1,0:T(8,128)(2,1)S(1)}, u32[]{:S(2)}, u32[]{:S(2)}) collective-permute-start(bf16[208,768]{1,0:T(8,128)(2,1)} %both_kernel.3.refs_3_.refs_1_), channel_id=1, source_target_pairs={{0,2},{2,0},{1,3},{3,1},{4,6},{6,4},{5,7},{7,5},{8,10},{10,8},{9,1... | collective-permute-start | bytes 958472 | tf_op jit(solution)/shard_map/ppermute | solution.py:403
  214.2 33.3 %collective-permute-start.34 = (bf16[208,768]{1,0:T(8,128)(2,1)}, bf16[208,768]{1,0:T(8,128)(2,1)S(1)}, u32[]{:S(2)}, u32[]{:S(2)}) collective-permute-start(bf16[208,768]{1,0:T(8,128)(2,1)} %both_kernel.3.refs_3_.refs_1_), channel_id=1, source_target_pairs={{0,1},{1,0},{2,3},{3,2},{4,5},{5,4},{6,7},{7,6},{8,9},{9,8},{10,11... | collective-permute-start | bytes 958472 | tf_op jit(solution)/shard_map/ppermute | solution.py:403
  215.4 16.7 %collective-permute-start.29 = (bf16[288,576]{1,0:T(8,128)(2,1)S(1)}, bf16[288,576]{1,0:T(8,128)(2,1)S(1)}, u32[]{:S(2)}, u32[]{:S(2)}) collective-permute-start(bf16[288,576]{1,0:T(8,128)(2,1)S(1)} %copy-done.20), channel_id=1, source_target_pairs={{0,4},{4,0},{1,5},{5,1},{2,6},{6,2},{3,7},{7,3},{8,12},{12,8},{9,1... | collective-permute-start | bytes 995336 | tf_op jit(solution)/shard_map/ppermute | solution.py:403
  234.8 19.8 %collective-permute-start.33 = (bf16[288,576]{1,0:T(8,128)(2,1)}, bf16[288,576]{1,0:T(8,128)(2,1)S(1)}, u32[]{:S(2)}, u32[]{:S(2)}) collective-permute-start(bf16[288,576]{1,0:T(8,128)(2,1)} %both_kernel.5.refs_5_.refs_1_), channel_id=1, source_target_pairs={{0,3},{1,2},{2,1},{3,0},{4,7},{5,6},{6,5},{7,4},{8,11},{9,10},{10,... | collective-permute-start | bytes 995336 | tf_op jit(solution)/shard_map/ppermute | solution.py:407
  240.5 25.3 %collective-permute-start.32 = (bf16[288,576]{1,0:T(8,128)(2,1)}, bf16[288,576]{1,0:T(8,128)(2,1)S(1)}, u32[]{:S(2)}, u32[]{:S(2)}) collective-permute-start(bf16[288,576]{1,0:T(8,128)(2,1)} %both_kernel.5.refs_5_.refs_1_), channel_id=1, source_target_pairs={{0,2},{2,0},{1,3},{3,1},{4,6},{6,4},{5,7},{7,5},{8,10},{10,8},{9,1... | collective-permute-start | bytes 995336 | tf_op jit(solution)/shard_map/ppermute | solution.py:403
  241.7 24.1 %collective-permute-start.31 = (bf16[288,576]{1,0:T(8,128)(2,1)}, bf16[288,576]{1,0:T(8,128)(2,1)S(1)}, u32[]{:S(2)}, u32[]{:S(2)}) collective-permute-start(bf16[288,576]{1,0:T(8,128)(2,1)} %both_kernel.5.refs_5_.refs_1_), channel_id=1, source_target_pairs={{0,1},{1,0},{2,3},{3,2},{4,5},{5,4},{6,7},{7,6},{8,9},{9,8},{10,11... | collective-permute-start | bytes 995336 | tf_op jit(solution)/shard_map/ppermute | solution.py:403
  243.9 10.7 %all-to-all-start.4 = ((bf16[4,48,768]{2,1,0:T(8,128)(2,1)}), bf16[4,48,768]{2,1,0:T(8,128)(2,1)S(1)}, u32[]{:S(2)}, u32[]{:S(2)}) async-start(bf16[4,48,768]{2,1,0:T(8,128)(2,1)} %both_kernel.4.refs_3_), calls=%async_computation.4 | async-start | bytes 589824 | tf_op jit(solution)/shard_map/all_to_all | solution.py:927
  247.4 22.8 %collective-permute-start.28 = (bf16[128,768]{1,0:T(8,128)(2,1)S(1)}, bf16[128,768]{1,0:T(8,128)(2,1)S(1)}, u32[]{:S(2)}, u32[]{:S(2)}) collective-permute-start(bf16[128,768]{1,0:T(8,128)(2,1)S(1)} %copy-done.42), channel_id=1, source_target_pairs={{0,4},{4,0},{1,5},{5,1},{2,6},{6,2},{3,7},{7,3},{8,12},{12,8},{9,1... | collective-permute-start | bytes 589832 | tf_op jit(solution)/shard_map/ppermute | solution.py:403
  247.5 22.7 %collective-permute-start.27 = (bf16[128,768]{1,0:T(8,128)(2,1)S(1)}, bf16[128,768]{1,0:T(8,128)(2,1)S(1)}, u32[]{:S(2)}, u32[]{:S(2)}) collective-permute-start(bf16[128,768]{1,0:T(8,128)(2,1)S(1)} %copy-done.45), channel_id=1, source_target_pairs={{0,4},{4,0},{1,5},{5,1},{2,6},{6,2},{3,7},{7,3},{8,12},{12,8},{9,1... | collective-permute-start | bytes 589832 | tf_op jit(solution)/shard_map/ppermute | solution.py:403
  254.6 19.9 %collective-permute-start.39 = (bf16[4,48,768]{2,1,0:T(8,128)(2,1)S(1)}, bf16[4,48,768]{2,1,0:T(8,128)(2,1)S(1)}, u32[]{:S(2)}, u32[]{:S(2)}) collective-permute-start(bf16[4,48,768]{2,1,0:T(8,128)(2,1)S(1)} %all-to-all-done.4.refs_1_), channel_id=1, source_target_pairs={{0,3},{1,2},{2,1},{3,0},{4,7},{5,6},{6,5},{7,4},{8,11},{9,10},{10,... | collective-permute-start | bytes 884744 | tf_op jit(solution)/shard_map/ppermute | solution.py:407
  265.8 12.6 %collective-permute-start.38 = (bf16[4,48,768]{2,1,0:T(8,128)(2,1)S(1)}, bf16[4,48,768]{2,1,0:T(8,128)(2,1)S(1)}, u32[]{:S(2)}, u32[]{:S(2)}) collective-permute-start(bf16[4,48,768]{2,1,0:T(8,128)(2,1)S(1)} %all-to-all-done.4.refs_1_), channel_id=1, source_target_pairs={{0,2},{2,0},{1,3},{3,1},{4,6},{6,4},{5,7},{7,5},{8,10},{10,8},{9,1... | collective-permute-start | bytes 884744 | tf_op jit(solution)/shard_map/ppermute | solution.py:403
  265.8 12.6 %collective-permute-start.37 = (bf16[4,48,768]{2,1,0:T(8,128)(2,1)S(1)}, bf16[4,48,768]{2,1,0:T(8,128)(2,1)S(1)}, u32[]{:S(2)}, u32[]{:S(2)}) collective-permute-start(bf16[4,48,768]{2,1,0:T(8,128)(2,1)S(1)} %all-to-all-done.4.refs_1_), channel_id=1, source_target_pairs={{0,1},{1,0},{2,3},{3,2},{4,5},{5,4},{6,7},{7,6},{8,9},{9,8},{10,11... | collective-permute-start | bytes 884744 | tf_op jit(solution)/shard_map/ppermute | solution.py:403
  (64 other events, 333.9 us)
Sparse Core Ops, SparseCore 0:
  14.2 19.1 all-gather.7
  41.9 19.4 all-gather.9
  72.6 22.0 all-gather.11
  146.2 23.5 all-gather.13

commit v3 on v2

--- a/solution.py
+++ b/solution.py
@@ -986,7 +986,7 @@
     def attend():
         v.attn_in, v.qkv_t, v.o_full, send, v.lse, v.w_t, v.te = step(attend_kernel, 15, [*v.toks, *v.fars, sinus_here, w_time_f, v.vec, v.small, v.wq],
             [((4, own, width), BF16), ((4, 3 * part, own), BF16), ((4, part, own), F32), ((4, part, own), BF16),
-             ((4 * heads, 8, own), F32), ((3 * part, width), BF16), ((8, width), F32)], behind=[v.wq])
+             ((4 * heads, 8, own), F32), ((3 * part, width), BF16), ((8, width), F32)], behind=[v.ups[1], v.ups[2]])
         v.attn = members(send)
 
     def own_grad():
@@ -996,7 +996,7 @@
 
     def branch():
         mlp, v.hidden_two, v.folds = step(branch_kernel, 30, [v.attn, v.w_out, v.toks[0], v.far_own, v.te, v.vec],
-            [hidden_low, hidden_full, ((4, part // 3, width), BF16)], behind=[*v.ups[1:]])
+            [hidden_low, hidden_full, ((4, part // 3, width), BF16)], behind=[v.ups[3]])
         y = swap(mlp, "y")
         v.mlps = [mlp, y, swap(mlp, "c"), swap(y, "c")]
 

time: 290 us -> 288 us (level)
  starting transfers between devices: 65.8 us -> 62 us
    ppermute x32, waiting for transfers between devices: 54.8 us -> 58.7 us  [swap(): return lax.ppermute(value, axis, [(0, 1), (1, 0)])]
    ppermute x7, waiting for transfers between devices: 10.2 us -> 7.06 us  [across(): return lax.ppermute(value, ('zl', 'x'), [(i, i ^ 3) for i in range(4)])]
    unnamed x126 -> x122, local copies, waits for them, and re-layouts: 11.5 us -> 11.7 us
  transfers between devices with their start and end apart: 49 -> 49, of which waited for: 16 -> 15; matrix products, arithmetic and copies ran while one was open for 3% -> 3% of each run, Pallas kernels for 30% -> 30%
where the time goes in v3:
time: 288 us; the launch traced here: 287 us
  Pallas kernels  106 us (37%)
  waiting for transfers between devices  78.6 us (27%)
  starting transfers between devices  62 us (22%)
  local copies, waits for them, and re-layouts  15.4 us (5%)
  between operations  15.1 us (5%)
  blocking collectives  5.64 us (2%)
  other arithmetic  4.34 us (2%)
    pallas_call x26, Pallas kernels, __call__(): pl.pallas_call(run, out_shape=shapes, in_specs=[pl.BlockSpec(memory_space...  106 us
    ppermute x32, waiting for transfers between devices, swap(): return lax.ppermute(value, axis, [(0, 1), (1, 0)])  58.7 us
    ppermute x32, starting transfers between devices, swap(): return lax.ppermute(value, axis, [(0, 1), (1, 0)])  27.1 us
    ppermute x7, starting transfers between devices, across(): return lax.ppermute(value, ('zl', 'x'), [(i, i ^ 3) for i in range(4)])  16.2 us
    unnamed x122, local copies, waits for them, and re-layouts  11.7 us
    all_to_all x3, starting transfers between devices, members(): lax.all_to_all(value, ('zl', 'x'), split_axis=0, concat_axis=0, tiled=True)  11.3 us
    ppermute x1, waiting for transfers between devices, across_seq(): return lax.ppermute(value, ('y', 'c'), [(i, i ^ 3) for i in range(4)])  8.2 us
    all_to_all x2, starting transfers between devices, shards(): lax.all_to_all(value, ('y', 'c'), split_axis=0, concat_axis=0, tiled=True)  7.1 us
  transfers between devices with their start and end apart: 49, of which 15 were waited for; matrix products, arithmetic and copies ran while one was open for 3% of the time, Pallas kernels for 30%

profile of v3, /device:TPU:0, one launch (start us, length us, event | category | flops | bytes accessed | tf_op | source)
XLA Modules:
  0.0 287.0 jit_solution(10601771822099477348)
XLA Ops:
  9.6 4.0 %collective-permute-start.2 = (bf16[128,768]{1,0:T(8,128)(2,1)}, bf16[128,768]{1,0:T(8,128)(2,1)S(1)}, u32[]{:S(2)}, u32[]{:S(2)}) collective-permute-start(bf16[128,768]{1,0:T(8,128)(2,1)} %get-tuple-element.80.refs_2_.refs_1_.refs_3_.refs_6_), channel_id=1, source_target_pairs={{0,3},{1,2},{2,1},{3,0},{4,7},{5,6},{6,5},{7,4},{8,11},{9,10},{10,... | collective-permute-start | bytes 589832 | tf_op jit(solution)/shard_map/ppermute | solution.py:407
  16.1 3.0 %collective-permute-start.9 = (bf16[128,768]{1,0:T(8,128)(2,1)}, bf16[128,768]{1,0:T(8,128)(2,1)S(1)}, u32[]{:S(2)}, u32[]{:S(2)}) collective-permute-start(bf16[128,768]{1,0:T(8,128)(2,1)} %pick_kernel.1.refs_3_), channel_id=1, source_target_pairs={{0,4},{4,0},{1,5},{5,1},{2,6},{6,2},{3,7},{7,3},{8,12},{12,8},{9,1... | collective-permute-start | bytes 589832 | tf_op jit(solution)/shard_map/ppermute | solution.py:403
  19.5 5.6 %all-gather = bf16[64,192]{1,0:T(8,128)(2,1)} all-gather(bf16[16,192]{1,0:T(8,128)(2,1)S(1)} %stack.59), channel_id=2, replica_groups=mesh['y'=2,'c'=2,'h'=2,'zl'=2,'x'=2] {'y','c'}, dimensions={0}, use_global_device_ids=true | all-gather | bytes 30720 | tf_op jit(solution)/shard_map/all_gather | solution.py:971
  25.2 2.2 column_kernel.1.refs_2_
  27.4 3.7 %all-to-all-start = ((bf16[4,192,576]{2,1,0:T(8,128)(2,1)}), bf16[4,192,576]{2,1,0:T(8,128)(2,1)S(1)}, u32[]{:S(2)}, u32[]{:S(2)}) async-start(bf16[4,192,576]{2,1,0:T(8,128)(2,1)} %column_kernel.1.refs_2_), calls=%async_computation | async-start | bytes 1966080 | tf_op jit(solution)/shard_map/all_to_all | solution.py:927
  32.4 2.4 up_kernel.1
  34.8 2.0 collective-permute-start.7
  38.3 2.9 collective-permute-start.6
  41.8 2.1 own_kernel.1
  43.9 7.2 %collective-permute-done.7.refs_14_.refs_7_ = bf16[192,768]{1,0:T(8,128)(2,1)S(1)} collective-permute-done((bf16[192,768]{1,0:T(8,128)(2,1)}, bf16[192,768]{1,0:T(8,128)(2,1)S(1)}, u32[]{:S(2)}, u32[]{:S(2)}) %collective-permute-start.7) | collective-permute-done | bytes 294944 | tf_op jit(solution)/shard_map/ppermute | solution.py:403
  52.4 15.7 %attend_kernel.1 = (bf16[4,256,768]{2,1,0:T(8,128)(2,1)}, bf16[4,576,256]{2,1,0:T(8,128)(2,1)}, f32[4,192,256]{2,1,0:T(8,128)}, bf16[4,192,256]{2,1,0:T(8,128)(2...) custom-call(s32[3]{0:T(128)} %pad_add_fusion.refs_0_, ...), custom_call_target="tpu_custom_call" | custom-call | flops 17250000896 | bytes 1 | tf_op jit(solution)/shard_map/attend_kernel/pallas_call | solution.py:437
  68.2 4.1 %all-to-all-start.1 = ((bf16[4,192,256]{2,1,0:T(8,128)(2,1)}), bf16[4,192,256]{2,1,0:T(8,128)(2,1)S(1)}, u32[]{:S(2)}, u32[]{:S(2)}) async-start(bf16[4,192,256]{2,1,0:T(8,128)(2,1)} %get-tuple-element.87), calls=%async_computation.1 | async-start | bytes 786432 | tf_op jit(solution)/shard_map/all_to_all | solution.py:924
  73.0 8.2 %collective-permute-done.10.refs_7_.refs_9_ = bf16[192,768]{1,0:T(8,128)(2,1)S(1)} collective-permute-done((bf16[192,768]{1,0:T(8,128)(2,1)S(1)}, bf16[192,768]{1,0:T(8,128)(2,1)S(1)}, u32[]{:S(2)}, u32[]{:S(2)}) %collective-permute-start.10) | collective-permute-done | bytes 294944 | tf_op jit(solution)/shard_map/ppermute | solution.py:936
  82.1 3.3 %branch_kernel.1 = (bf16[256,768]{1,0:T(8,128)(2,1)}, f32[256,768]{1,0:T(8,128)}, bf16[4,64,768]{2,1,0:T(8,128)(2,1)}) custom-call(s32[3]{0:T(128)} %pad_add_fusion.refs_0_, bf16[4,192,256]{2,1,0:T(8,128)(2,1)} %copy-done.3, bf16[768,768]{1,0:T(8,128)(2,1)} %all-gather.10.cloned.1.call-done.refs_2_.refs_6_, ...), custom_call_target="tpu_custom_call" | custom-call | flops 34500001792 | bytes 1 | tf_op jit(solution)/shard_map/branch_kernel/pallas_call | solution.py:437
  86.4 16.2 %collective-permute-done.11.refs_2_ = bf16[256,768]{1,0:T(8,128)(2,1)S(1)} collective-permute-done((bf16[256,768]{1,0:T(8,128)(2,1)}, bf16[256,768]{1,0:T(8,128)(2,1)S(1)}, u32[]{:S(2)}, u32[]{:S(2)}) %collective-permute-start.11) | collective-permute-done | bytes 393248 | tf_op jit(solution)/shard_map/ppermute | solution.py:403
  105.1 9.9 %feed_kernel.1 = (f32[256,768]{1,0:T(8,128)}, bf16[256,768]{1,0:T(8,128)(2,1)}, bf16[2,256,768]{2,1,0:T(8,128)(2,1)}, f32[256,768]{1,0:T(8,128)}, bf16[256,768]{...) custom-call(s32[3]{0:T(128)} %pad_add_fusion.refs_0_, ...), custom_call_target="tpu_custom_call" | custom-call | flops 11500000256 | bytes 1 | tf_op jit(solution)/shard_map/feed_kernel/pallas_call | solution.py:437
  115.5 2.0 collective-permute-done.14.refs_2_
  118.3 2.1 second_kernel.1.refs_8_
  120.8 7.6 %feed_grad_kernel.1 = (bf16[400,768]{1,0:T(8,128)(2,1)}, bf16[400,768]{1,0:T(8,128)(2,1)}, bf16[400,768]{1,0:T(8,128)(2,1)}, bf16[400,768]{1,0:T(8,128)(2,1)}) custom-call(s32[3]{0:T(128)} %pad_add_fusion.refs_0_, bf16[256,768]{1,0:T(8,128)(2,1)} %get-tuple-element.92.refs_1_.refs_13_, bf16[256,768]{1,0:T(8,128)(2,1)} %copy-done.13, ...), custom_call_target="tpu_custom_call" | custom-call | flops 8049999872 | bytes 1 | tf_op jit(solution)/shard_map/feed_grad_kernel/pallas_call | solution.py:437
  128.3 3.5 %collective-permute-done.15.refs_3_ = bf16[256,768]{1,0:T(8,128)(2,1)S(1)} collective-permute-done((bf16[256,768]{1,0:T(8,128)(2,1)}, bf16[256,768]{1,0:T(8,128)(2,1)S(1)}, u32[]{:S(2)}, u32[]{:S(2)}) %collective-permute-start.15) | collective-permute-done | bytes 393248 | tf_op jit(solution)/shard_map/ppermute | solution.py:403
  132.6 5.1 %back_kernel.1 = (f32[256,768]{1,0:T(8,128)}, bf16[256,768]{1,0:T(8,128)(2,1)}, bf16[4,192,256]{2,1,0:T(8,128)(2,1)}, f32[8,768]{1,0:T(8,128)}, bf16[384,768]{1,0:T(8,128)(2,1)}) custom-call(s32[3]{0:T(128)} %pad_add_fusion.refs_0_, f32[256,768]{1,0:T(8,128)} %get-tuple-element.94.refs_3_.refs_1_, bf16[2,256,768]{2,1,0:T(8,128)(2,1)} %copy-done.9, ...), custom_call_target="tpu_custom_call" | custom-call | flops 5750000128 | bytes 1 | tf_op jit(solution)/shard_map/back_kernel/pallas_call | solution.py:437
  137.7 3.7 %all-to-all-start.2 = ((bf16[4,192,256]{2,1,0:T(8,128)(2,1)}), bf16[4,192,256]{2,1,0:T(8,128)(2,1)S(1)}, u32[]{:S(2)}, u32[]{:S(2)}) async-start(bf16[4,192,256]{2,1,0:T(8,128)(2,1)} %get-tuple-element.107), calls=%async_computation.2 | async-start | bytes 786432 | tf_op jit(solution)/shard_map/all_to_all | solution.py:924
  145.5 3.9 %all-to-all-done.2.refs_4_ = bf16[4,192,256]{2,1,0:T(8,128)(2,1)S(1)} async-done(((bf16[4,192,256]{2,1,0:T(8,128)(2,1)}), bf16[4,192,256]{2,1,0:T(8,128)(2,1)S(1)}, u32[]{:S(2)}, u32[]{:S(2)}) %all-to-all-start.2) | async-done | bytes 393248 | tf_op jit(solution)/shard_map/all_to_all | solution.py:924
  150.1 14.8 %attend_back_kernel.1 = (bf16[4,576,256]{2,1,0:T(8,128)(2,1)}, bf16[4,256,768]{2,1,0:T(8,128)(2,1)}, f32[8,768]{1,0:T(8,128)}) custom-call(s32[3]{0:T(128)} %pad_add_fusion.refs_0_, bf16[4,576,256]{2,1,0:T(8,128)(2,1)} %get-tuple-element.104.refs_1_, f32[12,8,256]{2,1,0:T(8,128)} %get-tuple-element.105.refs_2_, f32[4,192,256]{2,1,0:T(8,128)} %get-tuple-element.106.refs_3_, ...), custom_call_target="tpu_custom_call" | custom-call | flops 17250000896 | bytes 1 | tf_op jit(solution)/shard_map/attend_back_kernel/pallas_call | solution.py:437
  165.0 3.6 %all-to-all-start.3 = ((bf16[4,256,768]{2,1,0:T(8,128)(2,1)}), bf16[4,256,768]{2,1,0:T(8,128)(2,1)S(1)}, u32[]{:S(2)}, u32[]{:S(2)}) async-start(bf16[4,256,768]{2,1,0:T(8,128)(2,1)} %get-tuple-element.109), calls=%async_computation.3 | async-start | bytes 3145728 | tf_op jit(solution)/shard_map/all_to_all | solution.py:924
  168.5 2.7 out_kernel.1
  171.3 5.5 %collective-permute-done.19.refs_4_ = bf16[400,768]{1,0:T(8,128)(2,1)} collective-permute-done((bf16[400,768]{1,0:T(8,128)(2,1)S(1)}, bf16[400,768]{1,0:T(8,128)(2,1)}, u32[]{:S(2)}, u32[]{:S(2)}) %collective-permute-start.19) | collective-permute-done | bytes 614432 | tf_op jit(solution)/shard_map/ppermute | solution.py:407
  176.8 2.7 pieces_kernel.1
  179.5 4.9 %qkv_grad_kernel.1 = (bf16[2,224,576]{2,1,0:T(8,128)(2,1)}, bf16[2,224,576]{2,1,0:T(8,128)(2,1)}) custom-call(s32[3]{0:T(128)} %pad_add_fusion.refs_0_, bf16[4,256,768]{2,1,0:T(8,128)(2,1)} %get-tuple-element.91.refs_8_.refs_1_, bf16[4,576,256]{2,1,0:T(8,128)(2,1)} %get-tuple-element.115.refs_6_.refs_2_, f32[8,768]{1,0:T(8,128)} %get-tuple-element.118.refs_3_, ...), custom_call_target="tpu_custom_call" | custom-call | flops 5750000128 | bytes 1 | tf_op jit(solution)/shard_map/qkv_grad_kernel/pallas_call | solution.py:437
  185.3 2.5 collective-permute-start.21
  188.6 2.1 chain_kernel.1
  191.3 3.3 %out_grad_kernel.1 = (bf16[64,576]{1,0:T(8,128)(2,1)}, bf16[64,576]{1,0:T(8,128)(2,1)}, bf16[64,576]{1,0:T(8,128)(2,1)}, bf16[64,576]{1,0:T(8,128)(2,1)}) custom-call(s32[3]{0:T(128)} %pad_add_fusion.refs_0_, bf16[4,64,768]{2,1,0:T(8,128)(2,1)} %get-tuple-element.93.refs_12_.refs_10_.refs_1_, bf16[640,768]{1,0:T(8,128)(2,1)} %copy-done.8, ...), custom_call_target="tpu_custom_call" | custom-call | flops 3449999872 | bytes 1 | tf_op jit(solution)/shard_map/out_grad_kernel/pallas_call | solution.py:437
  195.2 2.9 %collective-permute-start.26 = (bf16[64,576]{1,0:T(8,128)(2,1)}, bf16[64,576]{1,0:T(8,128)(2,1)S(1)}, u32[]{:S(2)}, u32[]{:S(2)}) collective-permute-start(bf16[64,576]{1,0:T(8,128)(2,1)} %get-tuple-element.128), channel_id=1, source_target_pairs={{0,3},{1,2},{2,1},{3,0},{4,7},{5,6},{6,5},{7,4},{8,11},{9,10},{10,... | collective-permute-start | bytes 221192 | tf_op jit(solution)/shard_map/ppermute | solution.py:407
  201.0 3.0 %collective-permute-done.25.refs_5_ = bf16[64,576]{1,0:T(8,128)(2,1)S(1)} collective-permute-done((bf16[64,576]{1,0:T(8,128)(2,1)}, bf16[64,576]{1,0:T(8,128)(2,1)S(1)}, u32[]{:S(2)}, u32[]{:S(2)}) %collective-permute-start.25) | collective-permute-done | bytes 73760 | tf_op jit(solution)/shard_map/ppermute | solution.py:403
  206.1 2.0 join_kernel.1.refs_3_.refs_1_
  213.0 2.7 collective-permute-start.34
  218.0 2.6 hidden_grad_kernel.1
  222.4 8.9 %collective-permute-done.29.refs_2_ = bf16[288,576]{1,0:T(8,128)(2,1)S(1)} collective-permute-done((bf16[288,576]{1,0:T(8,128)(2,1)S(1)}, bf16[288,576]{1,0:T(8,128)(2,1)S(1)}, u32[]{:S(2)}, u32[]{:S(2)}) %collective-permute-start.29) | collective-permute-done | bytes 331808 | tf_op jit(solution)/shard_map/ppermute | solution.py:403
  232.1 2.0 both_kernel.5.refs_5_.refs_1_
  234.1 4.9 %collective-permute-start.33 = (bf16[288,576]{1,0:T(8,128)(2,1)}, bf16[288,576]{1,0:T(8,128)(2,1)S(1)}, u32[]{:S(2)}, u32[]{:S(2)}) collective-permute-start(bf16[288,576]{1,0:T(8,128)(2,1)} %both_kernel.5.refs_5_.refs_1_), channel_id=1, source_target_pairs={{0,3},{1,2},{2,1},{3,0},{4,7},{5,6},{6,5},{7,4},{8,11},{9,10},{10,... | collective-permute-start | bytes 995336 | tf_op jit(solution)/shard_map/ppermute | solution.py:407
  242.4 3.5 %all-to-all-start.4 = ((bf16[4,48,768]{2,1,0:T(8,128)(2,1)}), bf16[4,48,768]{2,1,0:T(8,128)(2,1)S(1)}, u32[]{:S(2)}, u32[]{:S(2)}) async-start(bf16[4,48,768]{2,1,0:T(8,128)(2,1)} %both_kernel.4.refs_3_), calls=%async_computation.4 | async-start | bytes 589824 | tf_op jit(solution)/shard_map/all_to_all | solution.py:927
  246.0 2.9 %collective-permute-start.27 = (bf16[128,768]{1,0:T(8,128)(2,1)S(1)}, bf16[128,768]{1,0:T(8,128)(2,1)S(1)}, u32[]{:S(2)}, u32[]{:S(2)}) collective-permute-start(bf16[128,768]{1,0:T(8,128)(2,1)S(1)} %copy-done.44), channel_id=1, source_target_pairs={{0,4},{4,0},{1,5},{5,1},{2,6},{6,2},{3,7},{7,3},{8,12},{12,8},{9,1... | collective-permute-start | bytes 589832 | tf_op jit(solution)/shard_map/ppermute | solution.py:403
  249.0 2.9 %down_total_kernel.1 = (f32[4,192,768]{2,1,0:T(8,128)}, f32[1,768]{1,0:T(1,128)}, f32[1,192]{1,0:T(1,128)}) custom-call(s32[3]{0:T(128)} %pad_add_fusion.refs_0_, bf16[208,768]{1,0:T(8,128)(2,1)} %both_kernel.3.refs_3_.refs_1_, bf16[208,768]{1,0:T(8,128)(2,1)} %copy-done.26, bf16[208,768]{1,0:T(8,128)(2,1)} %copy-done.25, bf16[208,768]{1,0:T(8,128)(2,1)} %copy-done.23, ...), custom_call_target="tpu_custom_call" | custom-call | flops 3449999872 | bytes 1 | tf_op jit(solution)/shard_map/down_total_kernel/pallas_call | solution.py:437
  254.6 10.4 %collective-permute-done.32.refs_3_ = bf16[288,576]{1,0:T(8,128)(2,1)S(1)} collective-permute-done((bf16[288,576]{1,0:T(8,128)(2,1)}, bf16[288,576]{1,0:T(8,128)(2,1)S(1)}, u32[]{:S(2)}, u32[]{:S(2)}) %collective-permute-start.32) | collective-permute-done | bytes 331808 | tf_op jit(solution)/shard_map/ppermute | solution.py:403
  265.9 3.5 %total_kernel.1 = (f32[192,2304]{1,0:T(8,128)}, f32[4,48,768]{2,1,0:T(8,128)}, f32[192,768]{1,0:T(8,128)}, f32[8,576]{1,0:T(8,128)}, f32[1,192]{1,0:T(1,128)}) custom-call(s32[3]{0:T(128)} %pad_add_fusion.refs_0_, bf16[288,576]{1,0:T(8,128)(2,1)} %both_kernel.5.refs_5_.refs_1_, bf16[288,576]{1,0:T(8,128)(2,1)} %copy-done.19, bf16[288,576]{1,0:T(8,128)(2,1)} %copy-done.18, ...), custom_call_target="tpu_custom_call" | custom-call | flops 3449999872 | bytes 1 | tf_op jit(solution)/shard_map/total_kernel/pallas_call | solution.py:437
  270.1 2.1 pair_kernel.1
  273.7 3.1 %collective-permute-done.38.refs_3_ = bf16[4,48,768]{2,1,0:T(8,128)(2,1)S(1)} collective-permute-done((bf16[4,48,768]{2,1,0:T(8,128)(2,1)S(1)}, bf16[4,48,768]{2,1,0:T(8,128)(2,1)S(1)}, u32[]{:S(2)}, u32[]{:S(2)}) %collective-permute-start.38) | collective-permute-done | bytes 294944 | tf_op jit(solution)/shard_map/ppermute | solution.py:403
  277.7 2.8 up_total_kernel.1
  (233 shorter events, 49.5 us)
Async XLA Ops:
  7.2 44.0 %all-gather.8.cloned.1.call-start = ((), (), s32[]{:S(2)}) async-start(), calls=%async_computation.5 | async-start | bytes 1474560 | tf_op jit(solution)/shard_map/all_gather | solution.py:953
  9.6 28.6 %collective-permute-start.2 = (bf16[128,768]{1,0:T(8,128)(2,1)}, bf16[128,768]{1,0:T(8,128)(2,1)S(1)}, u32[]{:S(2)}, u32[]{:S(2)}) collective-permute-start(bf16[128,768]{1,0:T(8,128)(2,1)} %get-tuple-element.80.refs_2_.refs_1_.refs_3_.refs_6_), channel_id=1, source_target_pairs={{0,3},{1,2},{2,1},{3,0},{4,7},{5,6},{6,5},{7,4},{8,11},{9,10},{10,... | collective-permute-start | bytes 589832 | tf_op jit(solution)/shard_map/ppermute | solution.py:407
  13.6 27.5 %collective-permute-start.1 = (bf16[128,768]{1,0:T(8,128)(2,1)}, bf16[128,768]{1,0:T(8,128)(2,1)S(1)}, u32[]{:S(2)}, u32[]{:S(2)}) collective-permute-start(bf16[128,768]{1,0:T(8,128)(2,1)} %get-tuple-element.80.refs_2_.refs_1_.refs_3_.refs_6_), channel_id=1, source_target_pairs={{0,2},{2,0},{1,3},{3,1},{4,6},{6,4},{5,7},{7,5},{8,10},{10,8},{9,1... | collective-permute-start | bytes 589832 | tf_op jit(solution)/shard_map/ppermute | solution.py:403
  14.0 27.5 %collective-permute-start = (bf16[128,768]{1,0:T(8,128)(2,1)}, bf16[128,768]{1,0:T(8,128)(2,1)S(1)}, u32[]{:S(2)}, u32[]{:S(2)}) collective-permute-start(bf16[128,768]{1,0:T(8,128)(2,1)} %get-tuple-element.80.refs_2_.refs_1_.refs_3_.refs_6_), channel_id=1, source_target_pairs={{0,1},{1,0},{2,3},{3,2},{4,5},{5,4},{6,7},{7,6},{8,9},{9,8},{10,11... | collective-permute-start | bytes 589832 | tf_op jit(solution)/shard_map/ppermute | solution.py:403
  16.1 18.7 %collective-permute-start.9 = (bf16[128,768]{1,0:T(8,128)(2,1)}, bf16[128,768]{1,0:T(8,128)(2,1)S(1)}, u32[]{:S(2)}, u32[]{:S(2)}) collective-permute-start(bf16[128,768]{1,0:T(8,128)(2,1)} %pick_kernel.1.refs_3_), channel_id=1, source_target_pairs={{0,4},{4,0},{1,5},{5,1},{2,6},{6,2},{3,7},{7,3},{8,12},{12,8},{9,1... | collective-permute-start | bytes 589832 | tf_op jit(solution)/shard_map/ppermute | solution.py:403
  19.1 17.7 %collective-permute-start.3 = (bf16[128,768]{1,0:T(8,128)(2,1)S(1)}, bf16[128,768]{1,0:T(8,128)(2,1)S(1)}, u32[]{:S(2)}, u32[]{:S(2)}) collective-permute-start(bf16[128,768]{1,0:T(8,128)(2,1)S(1)} %copy-done.45), channel_id=1, source_target_pairs={{0,4},{4,0},{1,5},{5,1},{2,6},{6,2},{3,7},{7,3},{8,12},{12,8},{9,1... | collective-permute-start | bytes 589832 | tf_op jit(solution)/shard_map/ppermute | solution.py:403
  27.4 23.8 %all-to-all-start = ((bf16[4,192,576]{2,1,0:T(8,128)(2,1)}), bf16[4,192,576]{2,1,0:T(8,128)(2,1)S(1)}, u32[]{:S(2)}, u32[]{:S(2)}) async-start(bf16[4,192,576]{2,1,0:T(8,128)(2,1)} %column_kernel.1.refs_2_), calls=%async_computation | async-start | bytes 1966080 | tf_op jit(solution)/shard_map/all_to_all | solution.py:927
  31.1 50.2 %all-gather.10.cloned.1.call-start = ((), (), s32[]{:S(2)}) async-start(), calls=%async_computation.6 | async-start | bytes 1474560 | tf_op jit(solution)/shard_map/all_gather | solution.py:994
  34.8 16.3 %collective-permute-start.7 = (bf16[192,768]{1,0:T(8,128)(2,1)}, bf16[192,768]{1,0:T(8,128)(2,1)S(1)}, u32[]{:S(2)}, u32[]{:S(2)}) collective-permute-start(bf16[192,768]{1,0:T(8,128)(2,1)} %get-tuple-element.83), channel_id=1, source_target_pairs={{0,16},{16,0},{1,17},{17,1},{2,18},{18,2},{3,19},{19,3},{4,20},{20... | collective-permute-start | bytes 884744 | tf_op jit(solution)/shard_map/ppermute | solution.py:403
  36.8 14.3 %collective-permute-start.8 = (bf16[192,768]{1,0:T(8,128)(2,1)}, bf16[192,768]{1,0:T(8,128)(2,1)S(1)}, u32[]{:S(2)}, u32[]{:S(2)}) collective-permute-start(bf16[192,768]{1,0:T(8,128)(2,1)} %get-tuple-element.84), channel_id=1, source_target_pairs={{0,8},{8,0},{1,9},{9,1},{2,10},{10,2},{3,11},{11,3},{4,12},{12,4},... | collective-permute-start | bytes 884744 | tf_op jit(solution)/shard_map/ppermute | solution.py:403
  38.3 12.9 %collective-permute-start.6 = (bf16[128,768]{1,0:T(8,128)(2,1)S(1)}, bf16[128,768]{1,0:T(8,128)(2,1)S(1)}, u32[]{:S(2)}, u32[]{:S(2)}) collective-permute-start(bf16[128,768]{1,0:T(8,128)(2,1)S(1)} %collective-permute-done.3.refs_5_.refs_4_.refs_10_), channel_id=1, source_target_pairs={{0,3},{1,2},{2,1},{3,0},{4,7},{5,6},{6,5},{7,4},{8,11},{9,10},{10,... | collective-permute-start | bytes 589832 | tf_op jit(solution)/shard_map/ppermute | solution.py:407
  41.1 10.0 %collective-permute-start.5 = (bf16[128,768]{1,0:T(8,128)(2,1)S(1)}, bf16[128,768]{1,0:T(8,128)(2,1)S(1)}, u32[]{:S(2)}, u32[]{:S(2)}) collective-permute-start(bf16[128,768]{1,0:T(8,128)(2,1)S(1)} %collective-permute-done.3.refs_5_.refs_4_.refs_10_), channel_id=1, source_target_pairs={{0,2},{2,0},{1,3},{3,1},{4,6},{6,4},{5,7},{7,5},{8,10},{10,8},{9,1... | collective-permute-start | bytes 589832 | tf_op jit(solution)/shard_map/ppermute | solution.py:403
  41.6 9.6 %collective-permute-start.4 = (bf16[128,768]{1,0:T(8,128)(2,1)S(1)}, bf16[128,768]{1,0:T(8,128)(2,1)S(1)}, u32[]{:S(2)}, u32[]{:S(2)}) collective-permute-start(bf16[128,768]{1,0:T(8,128)(2,1)S(1)} %collective-permute-done.3.refs_5_.refs_4_.refs_10_), channel_id=1, source_target_pairs={{0,1},{1,0},{2,3},{3,2},{4,5},{5,4},{6,7},{7,6},{8,9},{9,8},{10,11... | collective-permute-start | bytes 589832 | tf_op jit(solution)/shard_map/ppermute | solution.py:403
  68.2 13.1 %all-to-all-start.1 = ((bf16[4,192,256]{2,1,0:T(8,128)(2,1)}), bf16[4,192,256]{2,1,0:T(8,128)(2,1)S(1)}, u32[]{:S(2)}, u32[]{:S(2)}) async-start(bf16[4,192,256]{2,1,0:T(8,128)(2,1)} %get-tuple-element.87), calls=%async_computation.1 | async-start | bytes 786432 | tf_op jit(solution)/shard_map/all_to_all | solution.py:924
  72.3 30.9 %all-gather.12.cloned.1.call-start = ((), (), s32[]{:S(2)}) async-start(), calls=%async_computation.7 | async-start | bytes 1966080 | tf_op jit(solution)/shard_map/all_gather | solution.py:995
  72.3 8.9 %collective-permute-start.10 = (bf16[192,768]{1,0:T(8,128)(2,1)S(1)}, bf16[192,768]{1,0:T(8,128)(2,1)S(1)}, u32[]{:S(2)}, u32[]{:S(2)}) collective-permute-start(bf16[192,768]{1,0:T(8,128)(2,1)S(1)} %copy-done.29), channel_id=1, source_target_pairs={{0,24},{8,16},{16,8},{24,0},{1,25},{9,17},{17,9},{25,1},{2,26},{10... | collective-permute-start | bytes 884744 | tf_op jit(solution)/shard_map/ppermute | solution.py:936
  85.4 17.2 %collective-permute-start.11 = (bf16[256,768]{1,0:T(8,128)(2,1)}, bf16[256,768]{1,0:T(8,128)(2,1)S(1)}, u32[]{:S(2)}, u32[]{:S(2)}) collective-permute-start(bf16[256,768]{1,0:T(8,128)(2,1)} %get-tuple-element.92.refs_1_.refs_13_), channel_id=1, source_target_pairs={{0,16},{16,0},{1,17},{17,1},{2,18},{18,2},{3,19},{19,3},{4,20},{20... | collective-permute-start | bytes 1179656 | tf_op jit(solution)/shard_map/ppermute | solution.py:403
  86.4 16.9 %collective-permute-start.12 = (bf16[256,768]{1,0:T(8,128)(2,1)}, bf16[256,768]{1,0:T(8,128)(2,1)S(1)}, u32[]{:S(2)}, u32[]{:S(2)}) collective-permute-start(bf16[256,768]{1,0:T(8,128)(2,1)} %get-tuple-element.92.refs_1_.refs_13_), channel_id=1, source_target_pairs={{0,8},{8,0},{1,9},{9,1},{2,10},{10,2},{3,11},{11,3},{4,12},{12,4},... | collective-permute-start | bytes 1179656 | tf_op jit(solution)/shard_map/ppermute | solution.py:403
  114.9 2.5 collective-permute-start.14
  115.1 13.2 %collective-permute-start.16 = (bf16[640,768]{1,0:T(8,128)(2,1)}, bf16[640,768]{1,0:T(8,128)(2,1)S(1)}, u32[]{:S(2)}, u32[]{:S(2)}) collective-permute-start(bf16[640,768]{1,0:T(8,128)(2,1)} %get-tuple-element.99), channel_id=1, source_target_pairs={{0,8},{8,0},{1,9},{9,1},{2,10},{10,2},{3,11},{11,3},{4,12},{12,4},... | collective-permute-start | bytes 2949128 | tf_op jit(solution)/shard_map/ppermute | solution.py:403
  120.4 11.4 %collective-permute-start.15 = (bf16[256,768]{1,0:T(8,128)(2,1)}, bf16[256,768]{1,0:T(8,128)(2,1)S(1)}, u32[]{:S(2)}, u32[]{:S(2)}) collective-permute-start(bf16[256,768]{1,0:T(8,128)(2,1)} %second_kernel.1.refs_8_), channel_id=1, source_target_pairs={{0,16},{16,0},{1,17},{17,1},{2,18},{18,2},{3,19},{19,3},{4,20},{20... | collective-permute-start | bytes 1179656 | tf_op jit(solution)/shard_map/ppermute | solution.py:403
  137.7 11.7 %all-to-all-start.2 = ((bf16[4,192,256]{2,1,0:T(8,128)(2,1)}), bf16[4,192,256]{2,1,0:T(8,128)(2,1)S(1)}, u32[]{:S(2)}, u32[]{:S(2)}) async-start(bf16[4,192,256]{2,1,0:T(8,128)(2,1)} %get-tuple-element.107), calls=%async_computation.2 | async-start | bytes 786432 | tf_op jit(solution)/shard_map/all_to_all | solution.py:924
  141.3 49.9 %all-gather.14.cloned.1.call-start = ((), (), s32[]{:S(2)}) async-start(), calls=%async_computation.8 | async-start | bytes 1966080 | tf_op jit(solution)/shard_map/all_gather | solution.py:1029
  141.4 29.9 %collective-permute-start.17 = (bf16[400,768]{1,0:T(8,128)(2,1)}, bf16[400,768]{1,0:T(8,128)(2,1)S(1)}, u32[]{:S(2)}, u32[]{:S(2)}) collective-permute-start(bf16[400,768]{1,0:T(8,128)(2,1)} %get-tuple-element.110), channel_id=1, source_target_pairs={{0,1},{1,0},{2,3},{3,2},{4,5},{5,4},{6,7},{7,6},{8,9},{9,8},{10,11... | collective-permute-start | bytes 1843208 | tf_op jit(solution)/shard_map/ppermute | solution.py:403
  143.4 27.9 %collective-permute-start.18 = (bf16[400,768]{1,0:T(8,128)(2,1)}, bf16[400,768]{1,0:T(8,128)(2,1)}, u32[]{:S(2)}, u32[]{:S(2)}) collective-permute-start(bf16[400,768]{1,0:T(8,128)(2,1)} %get-tuple-element.111), channel_id=1, source_target_pairs={{0,2},{2,0},{1,3},{3,1},{4,6},{6,4},{5,7},{7,5},{8,10},{10,8},{9,1... | collective-permute-start | bytes 1843208 | tf_op jit(solution)/shard_map/ppermute | solution.py:403
  144.8 32.0 %collective-permute-start.19 = (bf16[400,768]{1,0:T(8,128)(2,1)S(1)}, bf16[400,768]{1,0:T(8,128)(2,1)}, u32[]{:S(2)}, u32[]{:S(2)}) collective-permute-start(bf16[400,768]{1,0:T(8,128)(2,1)S(1)} %copy-done.10), channel_id=1, source_target_pairs={{0,3},{1,2},{2,1},{3,0},{4,7},{5,6},{6,5},{7,4},{8,11},{9,10},{10,... | collective-permute-start | bytes 1843208 | tf_op jit(solution)/shard_map/ppermute | solution.py:407
  145.0 23.6 %collective-permute-start.20 = (bf16[384,768]{1,0:T(8,128)(2,1)}, bf16[384,768]{1,0:T(8,128)(2,1)}, u32[]{:S(2)}, u32[]{:S(2)}) collective-permute-start(bf16[384,768]{1,0:T(8,128)(2,1)} %get-tuple-element.114), channel_id=1, source_target_pairs={{0,16},{16,0},{1,17},{17,1},{2,18},{18,2},{3,19},{19,3},{4,20},{20... | collective-permute-start | bytes 1769480 | tf_op jit(solution)/shard_map/ppermute | solution.py:403
  165.0 51.9 %all-to-all-start.3 = ((bf16[4,256,768]{2,1,0:T(8,128)(2,1)}), bf16[4,256,768]{2,1,0:T(8,128)(2,1)S(1)}, u32[]{:S(2)}, u32[]{:S(2)}) async-start(bf16[4,256,768]{2,1,0:T(8,128)(2,1)} %get-tuple-element.109), calls=%async_computation.3 | async-start | bytes 3145728 | tf_op jit(solution)/shard_map/all_to_all | solution.py:924
  184.3 3.5 %collective-permute-start.22 = (bf16[2,224,576]{2,1,0:T(8,128)(2,1)}, bf16[2,224,576]{2,1,0:T(8,128)(2,1)S(1)}, u32[]{:S(2)}, u32[]{:S(2)}) collective-permute-start(bf16[2,224,576]{2,1,0:T(8,128)(2,1)} %get-tuple-element.121), channel_id=1, source_target_pairs={{0,8},{8,0},{1,9},{9,1},{2,10},{10,2},{3,11},{11,3},{4,12},{12,4},... | collective-permute-start | bytes 1548296 | tf_op jit(solution)/shard_map/ppermute | solution.py:403
  185.3 24.3 %collective-permute-start.21 = (bf16[208,768]{1,0:T(8,128)(2,1)S(1)}, bf16[208,768]{1,0:T(8,128)(2,1)S(1)}, u32[]{:S(2)}, u32[]{:S(2)}) collective-permute-start(bf16[208,768]{1,0:T(8,128)(2,1)S(1)} %copy-done.22), channel_id=1, source_target_pairs={{0,4},{4,0},{1,5},{5,1},{2,6},{6,2},{3,7},{7,3},{8,12},{12,8},{9,1... | collective-permute-start | bytes 958472 | tf_op jit(solution)/shard_map/ppermute | solution.py:403
  190.7 9.2 %collective-permute-start.23 = (bf16[224,576]{1,0:T(8,128)(2,1)}, bf16[224,576]{1,0:T(8,128)(2,1)S(1)}, u32[]{:S(2)}, u32[]{:S(2)}) collective-permute-start(bf16[224,576]{1,0:T(8,128)(2,1)} %get-tuple-element.123), channel_id=1, source_target_pairs={{0,16},{16,0},{1,17},{17,1},{2,18},{18,2},{3,19},{19,3},{4,20},{20... | collective-permute-start | bytes 774152 | tf_op jit(solution)/shard_map/ppermute | solution.py:403
  194.6 6.4 %collective-permute-start.24 = (bf16[64,576]{1,0:T(8,128)(2,1)}, bf16[64,576]{1,0:T(8,128)(2,1)S(1)}, u32[]{:S(2)}, u32[]{:S(2)}) collective-permute-start(bf16[64,576]{1,0:T(8,128)(2,1)} %get-tuple-element.126), channel_id=1, source_target_pairs={{0,1},{1,0},{2,3},{3,2},{4,5},{5,4},{6,7},{7,6},{8,9},{9,8},{10,11... | collective-permute-start | bytes 221192 | tf_op jit(solution)/shard_map/ppermute | solution.py:403
  195.1 8.8 %collective-permute-start.25 = (bf16[64,576]{1,0:T(8,128)(2,1)}, bf16[64,576]{1,0:T(8,128)(2,1)S(1)}, u32[]{:S(2)}, u32[]{:S(2)}) collective-permute-start(bf16[64,576]{1,0:T(8,128)(2,1)} %get-tuple-element.127), channel_id=1, source_target_pairs={{0,2},{2,0},{1,3},{3,1},{4,6},{6,4},{5,7},{7,5},{8,10},{10,8},{9,1... | collective-permute-start | bytes 221192 | tf_op jit(solution)/shard_map/ppermute | solution.py:403
  195.2 10.3 %collective-permute-start.26 = (bf16[64,576]{1,0:T(8,128)(2,1)}, bf16[64,576]{1,0:T(8,128)(2,1)S(1)}, u32[]{:S(2)}, u32[]{:S(2)}) collective-permute-start(bf16[64,576]{1,0:T(8,128)(2,1)} %get-tuple-element.128), channel_id=1, source_target_pairs={{0,3},{1,2},{2,1},{3,0},{4,7},{5,6},{6,5},{7,4},{8,11},{9,10},{10,... | collective-permute-start | bytes 221192 | tf_op jit(solution)/shard_map/ppermute | solution.py:407
  199.9 20.7 %collective-permute-start.30 = (bf16[4,48,768]{2,1,0:T(8,128)(2,1)}, bf16[4,48,768]{2,1,0:T(8,128)(2,1)}, u32[]{:S(2)}, u32[]{:S(2)}) collective-permute-start(bf16[4,48,768]{2,1,0:T(8,128)(2,1)} %get-tuple-element.132.refs_1_), channel_id=1, source_target_pairs={{0,4},{4,0},{1,5},{5,1},{2,6},{6,2},{3,7},{7,3},{8,12},{12,8},{9,1... | collective-permute-start | bytes 884744 | tf_op jit(solution)/shard_map/ppermute | solution.py:403
  212.2 28.0 %collective-permute-start.36 = (bf16[208,768]{1,0:T(8,128)(2,1)}, bf16[208,768]{1,0:T(8,128)(2,1)S(1)}, u32[]{:S(2)}, u32[]{:S(2)}) collective-permute-start(bf16[208,768]{1,0:T(8,128)(2,1)} %both_kernel.3.refs_3_.refs_1_), channel_id=1, source_target_pairs={{0,3},{1,2},{2,1},{3,0},{4,7},{5,6},{6,5},{7,4},{8,11},{9,10},{10,... | collective-permute-start | bytes 958472 | tf_op jit(solution)/shard_map/ppermute | solution.py:407
  212.2 33.7 %collective-permute-start.35 = (bf16[208,768]{1,0:T(8,128)(2,1)}, bf16[208,768]{1,0:T(8,128)(2,1)S(1)}, u32[]{:S(2)}, u32[]{:S(2)}) collective-permute-start(bf16[208,768]{1,0:T(8,128)(2,1)} %both_kernel.3.refs_3_.refs_1_), channel_id=1, source_target_pairs={{0,2},{2,0},{1,3},{3,1},{4,6},{6,4},{5,7},{7,5},{8,10},{10,8},{9,1... | collective-permute-start | bytes 958472 | tf_op jit(solution)/shard_map/ppermute | solution.py:403
  213.0 33.0 %collective-permute-start.34 = (bf16[208,768]{1,0:T(8,128)(2,1)}, bf16[208,768]{1,0:T(8,128)(2,1)S(1)}, u32[]{:S(2)}, u32[]{:S(2)}) collective-permute-start(bf16[208,768]{1,0:T(8,128)(2,1)} %both_kernel.3.refs_3_.refs_1_), channel_id=1, source_target_pairs={{0,1},{1,0},{2,3},{3,2},{4,5},{5,4},{6,7},{7,6},{8,9},{9,8},{10,11... | collective-permute-start | bytes 958472 | tf_op jit(solution)/shard_map/ppermute | solution.py:403
  215.7 15.7 %collective-permute-start.29 = (bf16[288,576]{1,0:T(8,128)(2,1)S(1)}, bf16[288,576]{1,0:T(8,128)(2,1)S(1)}, u32[]{:S(2)}, u32[]{:S(2)}) collective-permute-start(bf16[288,576]{1,0:T(8,128)(2,1)S(1)} %copy-done.20), channel_id=1, source_target_pairs={{0,4},{4,0},{1,5},{5,1},{2,6},{6,2},{3,7},{7,3},{8,12},{12,8},{9,1... | collective-permute-start | bytes 995336 | tf_op jit(solution)/shard_map/ppermute | solution.py:403
  234.1 19.1 %collective-permute-start.33 = (bf16[288,576]{1,0:T(8,128)(2,1)}, bf16[288,576]{1,0:T(8,128)(2,1)S(1)}, u32[]{:S(2)}, u32[]{:S(2)}) collective-permute-start(bf16[288,576]{1,0:T(8,128)(2,1)} %both_kernel.5.refs_5_.refs_1_), channel_id=1, source_target_pairs={{0,3},{1,2},{2,1},{3,0},{4,7},{5,6},{6,5},{7,4},{8,11},{9,10},{10,... | collective-permute-start | bytes 995336 | tf_op jit(solution)/shard_map/ppermute | solution.py:407
  239.0 26.0 %collective-permute-start.32 = (bf16[288,576]{1,0:T(8,128)(2,1)}, bf16[288,576]{1,0:T(8,128)(2,1)S(1)}, u32[]{:S(2)}, u32[]{:S(2)}) collective-permute-start(bf16[288,576]{1,0:T(8,128)(2,1)} %both_kernel.5.refs_5_.refs_1_), channel_id=1, source_target_pairs={{0,2},{2,0},{1,3},{3,1},{4,6},{6,4},{5,7},{7,5},{8,10},{10,8},{9,1... | collective-permute-start | bytes 995336 | tf_op jit(solution)/shard_map/ppermute | solution.py:403
  240.1 24.9 %collective-permute-start.31 = (bf16[288,576]{1,0:T(8,128)(2,1)}, bf16[288,576]{1,0:T(8,128)(2,1)S(1)}, u32[]{:S(2)}, u32[]{:S(2)}) collective-permute-start(bf16[288,576]{1,0:T(8,128)(2,1)} %both_kernel.5.refs_5_.refs_1_), channel_id=1, source_target_pairs={{0,1},{1,0},{2,3},{3,2},{4,5},{5,4},{6,7},{7,6},{8,9},{9,8},{10,11... | collective-permute-start | bytes 995336 | tf_op jit(solution)/shard_map/ppermute | solution.py:403
  242.4 10.7 %all-to-all-start.4 = ((bf16[4,48,768]{2,1,0:T(8,128)(2,1)}), bf16[4,48,768]{2,1,0:T(8,128)(2,1)S(1)}, u32[]{:S(2)}, u32[]{:S(2)}) async-start(bf16[4,48,768]{2,1,0:T(8,128)(2,1)} %both_kernel.4.refs_3_), calls=%async_computation.4 | async-start | bytes 589824 | tf_op jit(solution)/shard_map/all_to_all | solution.py:927
  245.9 23.5 %collective-permute-start.28 = (bf16[128,768]{1,0:T(8,128)(2,1)S(1)}, bf16[128,768]{1,0:T(8,128)(2,1)S(1)}, u32[]{:S(2)}, u32[]{:S(2)}) collective-permute-start(bf16[128,768]{1,0:T(8,128)(2,1)S(1)} %copy-done.39), channel_id=1, source_target_pairs={{0,4},{4,0},{1,5},{5,1},{2,6},{6,2},{3,7},{7,3},{8,12},{12,8},{9,1... | collective-permute-start | bytes 589832 | tf_op jit(solution)/shard_map/ppermute | solution.py:403
  246.0 23.4 %collective-permute-start.27 = (bf16[128,768]{1,0:T(8,128)(2,1)S(1)}, bf16[128,768]{1,0:T(8,128)(2,1)S(1)}, u32[]{:S(2)}, u32[]{:S(2)}) collective-permute-start(bf16[128,768]{1,0:T(8,128)(2,1)S(1)} %copy-done.44), channel_id=1, source_target_pairs={{0,4},{4,0},{1,5},{5,1},{2,6},{6,2},{3,7},{7,3},{8,12},{12,8},{9,1... | collective-permute-start | bytes 589832 | tf_op jit(solution)/shard_map/ppermute | solution.py:403
  253.1 20.6 %collective-permute-start.39 = (bf16[4,48,768]{2,1,0:T(8,128)(2,1)S(1)}, bf16[4,48,768]{2,1,0:T(8,128)(2,1)S(1)}, u32[]{:S(2)}, u32[]{:S(2)}) collective-permute-start(bf16[4,48,768]{2,1,0:T(8,128)(2,1)S(1)} %all-to-all-done.4.refs_1_), channel_id=1, source_target_pairs={{0,3},{1,2},{2,1},{3,0},{4,7},{5,6},{6,5},{7,4},{8,11},{9,10},{10,... | collective-permute-start | bytes 884744 | tf_op jit(solution)/shard_map/ppermute | solution.py:407
  265.0 11.8 %collective-permute-start.38 = (bf16[4,48,768]{2,1,0:T(8,128)(2,1)S(1)}, bf16[4,48,768]{2,1,0:T(8,128)(2,1)S(1)}, u32[]{:S(2)}, u32[]{:S(2)}) collective-permute-start(bf16[4,48,768]{2,1,0:T(8,128)(2,1)S(1)} %all-to-all-done.4.refs_1_), channel_id=1, source_target_pairs={{0,2},{2,0},{1,3},{3,1},{4,6},{6,4},{5,7},{7,5},{8,10},{10,8},{9,1... | collective-permute-start | bytes 884744 | tf_op jit(solution)/shard_map/ppermute | solution.py:403
  265.0 11.8 %collective-permute-start.37 = (bf16[4,48,768]{2,1,0:T(8,128)(2,1)S(1)}, bf16[4,48,768]{2,1,0:T(8,128)(2,1)S(1)}, u32[]{:S(2)}, u32[]{:S(2)}) collective-permute-start(bf16[4,48,768]{2,1,0:T(8,128)(2,1)S(1)} %all-to-all-done.4.refs_1_), channel_id=1, source_target_pairs={{0,1},{1,0},{2,3},{3,2},{4,5},{5,4},{6,7},{7,6},{8,9},{9,8},{10,11... | collective-permute-start | bytes 884744 | tf_op jit(solution)/shard_map/ppermute | solution.py:403
  (62 other events, 283.4 us)
Sparse Core Ops, SparseCore 0:
  14.3 19.1 all-gather.7
  44.0 18.1 all-gather.9
  75.3 26.4 all-gather.11
  145.1 23.7 all-gather.13

commit v4 on v3

--- a/solution.py
+++ b/solution.py
@@ -836,14 +836,14 @@
 
         @pl.when(gi == flip)
         def _():
-            b_up[...] = ref[quarter : quarter + 1, :].astype(F32)
+            b_up[...] = ref[quarter : quarter + 1, :].astype(F32)[0]
             full = ref[quarter : quarter + 2, :].astype(F32)
-            rows = b_down.shape[1]
+            rows = b_down.shape[0]
             for s in range(4):
 
                 @pl.when(ids[SEQ] == s)
                 def _():
-                    b_down[...] = full[1:2, s * rows : (s + 1) * rows]
+                    b_down[...] = full[1, s * rows : (s + 1) * rows]
 
 
 def up_total_kernel(ids, own, x, z, d, w_up):
@@ -1098,7 +1098,7 @@
         )
 
     def down_total():
-        v.w_down, v.b_up, v.b_down = step(down_total_kernel, 3, v.dg, [((4, ff // 4, width), F32), ((1, ff), F32), ((1, rows), F32)]
+        v.w_down, v.b_up, v.b_down = step(down_total_kernel, 3, v.dg, [((4, ff // 4, width), F32), ((ff,), F32), ((rows,), F32)]
         )
 
     def up_total():
@@ -1114,7 +1114,7 @@
     return (
         v.output, v.grad_tokens, v.w_time, v.b_time.reshape(rows), tv[3, :rows], tv[4, :rows], v.w_qkv,
         tv[5, :part], tv[5, 2 * part :], v.t_out.reshape(rows, width), tv[2, :rows], tv[0, :rows], tv[1, :rows],
-        v.w_up.reshape(rows, 4 * ff), v.b_up.reshape(ff), v.w_down.reshape(ff, width), v.b_down.reshape(rows),
+        v.w_up.reshape(rows, 4 * ff), v.b_up, v.w_down.reshape(ff, width), v.b_down,
     )
 
 

time: 288 us -> 288 us (level)
  transfers between devices with their start and end apart: 49 -> 49, of which waited for: 15 -> 16; matrix products, arithmetic and copies ran while one was open for 3% -> 2% of each run, Pallas kernels for 30% -> 30%
where the time goes in v4:
time: 288 us; the launch traced here: 287 us
  Pallas kernels  106 us (37%)
  waiting for transfers between devices  79.9 us (28%)
  starting transfers between devices  62 us (22%)
  local copies, waits for them, and re-layouts  15.4 us (5%)
  between operations  15.1 us (5%)
  blocking collectives  5.64 us (2%)
  other arithmetic  3 us (1%)
    pallas_call x26, Pallas kernels, __call__(): pl.pallas_call(run, out_shape=shapes, in_specs=[pl.BlockSpec(memory_space...  106 us
    ppermute x32, waiting for transfers between devices, swap(): return lax.ppermute(value, axis, [(0, 1), (1, 0)])  59.6 us
    ppermute x32, starting transfers between devices, swap(): return lax.ppermute(value, axis, [(0, 1), (1, 0)])  27.1 us
    ppermute x7, starting transfers between devices, across(): return lax.ppermute(value, ('zl', 'x'), [(i, i ^ 3) for i in range(4)])  16.3 us
    unnamed x122, local copies, waits for them, and re-layouts  11.7 us
    all_to_all x3, starting transfers between devices, members(): lax.all_to_all(value, ('zl', 'x'), split_axis=0, concat_axis=0, tiled=True)  11.3 us
    ppermute x1, waiting for transfers between devices, across_seq(): return lax.ppermute(value, ('y', 'c'), [(i, i ^ 3) for i in range(4)])  8.2 us
    all_to_all x2, starting transfers between devices, shards(): lax.all_to_all(value, ('y', 'c'), split_axis=0, concat_axis=0, tiled=True)  7.1 us
  transfers between devices with their start and end apart: 49, of which 16 were waited for; matrix products, arithmetic and copies ran while one was open for 2% of the time, Pallas kernels for 30%

profile of v4, /device:TPU:0, one launch (start us, length us, event | category | flops | bytes accessed | tf_op | source)
XLA Modules:
  0.0 287.0 jit_solution(10741060640872435653)
XLA Ops:
  9.6 4.0 %collective-permute-start.2 = (bf16[128,768]{1,0:T(8,128)(2,1)}, bf16[128,768]{1,0:T(8,128)(2,1)S(1)}, u32[]{:S(2)}, u32[]{:S(2)}) collective-permute-start(bf16[128,768]{1,0:T(8,128)(2,1)} %get-tuple-element.80.refs_2_.refs_1_.refs_3_.refs_6_), channel_id=1, source_target_pairs={{0,3},{1,2},{2,1},{3,0},{4,7},{5,6},{6,5},{7,4},{8,11},{9,10},{10,... | collective-permute-start | bytes 589832 | tf_op jit(solution)/shard_map/ppermute | solution.py:407
  16.1 3.0 %collective-permute-start.9 = (bf16[128,768]{1,0:T(8,128)(2,1)}, bf16[128,768]{1,0:T(8,128)(2,1)S(1)}, u32[]{:S(2)}, u32[]{:S(2)}) collective-permute-start(bf16[128,768]{1,0:T(8,128)(2,1)} %pick_kernel.1.refs_3_), channel_id=1, source_target_pairs={{0,4},{4,0},{1,5},{5,1},{2,6},{6,2},{3,7},{7,3},{8,12},{12,8},{9,1... | collective-permute-start | bytes 589832 | tf_op jit(solution)/shard_map/ppermute | solution.py:403
  19.5 5.6 %all-gather = bf16[64,192]{1,0:T(8,128)(2,1)} all-gather(bf16[16,192]{1,0:T(8,128)(2,1)S(1)} %stack.59), channel_id=2, replica_groups=mesh['y'=2,'c'=2,'h'=2,'zl'=2,'x'=2] {'y','c'}, dimensions={0}, use_global_device_ids=true | all-gather | bytes 30720 | tf_op jit(solution)/shard_map/all_gather | solution.py:971
  25.1 2.2 column_kernel.1.refs_2_
  27.4 3.7 %all-to-all-start = ((bf16[4,192,576]{2,1,0:T(8,128)(2,1)}), bf16[4,192,576]{2,1,0:T(8,128)(2,1)S(1)}, u32[]{:S(2)}, u32[]{:S(2)}) async-start(bf16[4,192,576]{2,1,0:T(8,128)(2,1)} %column_kernel.1.refs_2_), calls=%async_computation | async-start | bytes 1966080 | tf_op jit(solution)/shard_map/all_to_all | solution.py:927
  32.4 2.4 up_kernel.1
  34.8 2.0 collective-permute-start.7
  38.2 2.9 collective-permute-start.6
  41.7 2.1 own_kernel.1
  43.8 7.2 %collective-permute-done.7.refs_14_.refs_7_ = bf16[192,768]{1,0:T(8,128)(2,1)S(1)} collective-permute-done((bf16[192,768]{1,0:T(8,128)(2,1)}, bf16[192,768]{1,0:T(8,128)(2,1)S(1)}, u32[]{:S(2)}, u32[]{:S(2)}) %collective-permute-start.7) | collective-permute-done | bytes 294944 | tf_op jit(solution)/shard_map/ppermute | solution.py:403
  52.4 15.7 %attend_kernel.1 = (bf16[4,256,768]{2,1,0:T(8,128)(2,1)}, bf16[4,576,256]{2,1,0:T(8,128)(2,1)}, f32[4,192,256]{2,1,0:T(8,128)}, bf16[4,192,256]{2,1,0:T(8,128)(2...) custom-call(s32[3]{0:T(128)} %pad_add_fusion.refs_0_, ...), custom_call_target="tpu_custom_call" | custom-call | flops 17250000896 | bytes 1 | tf_op jit(solution)/shard_map/attend_kernel/pallas_call | solution.py:437
  68.1 4.1 %all-to-all-start.1 = ((bf16[4,192,256]{2,1,0:T(8,128)(2,1)}), bf16[4,192,256]{2,1,0:T(8,128)(2,1)S(1)}, u32[]{:S(2)}, u32[]{:S(2)}) async-start(bf16[4,192,256]{2,1,0:T(8,128)(2,1)} %get-tuple-element.87), calls=%async_computation.1 | async-start | bytes 786432 | tf_op jit(solution)/shard_map/all_to_all | solution.py:924
  73.0 8.2 %collective-permute-done.10.refs_7_.refs_9_ = bf16[192,768]{1,0:T(8,128)(2,1)S(1)} collective-permute-done((bf16[192,768]{1,0:T(8,128)(2,1)S(1)}, bf16[192,768]{1,0:T(8,128)(2,1)S(1)}, u32[]{:S(2)}, u32[]{:S(2)}) %collective-permute-start.10) | collective-permute-done | bytes 294944 | tf_op jit(solution)/shard_map/ppermute | solution.py:936
  82.0 3.3 %branch_kernel.1 = (bf16[256,768]{1,0:T(8,128)(2,1)}, f32[256,768]{1,0:T(8,128)}, bf16[4,64,768]{2,1,0:T(8,128)(2,1)}) custom-call(s32[3]{0:T(128)} %pad_add_fusion.refs_0_, bf16[4,192,256]{2,1,0:T(8,128)(2,1)} %copy-done.3, bf16[768,768]{1,0:T(8,128)(2,1)} %all-gather.10.cloned.1.call-done.refs_2_.refs_6_, ...), custom_call_target="tpu_custom_call" | custom-call | flops 34500001792 | bytes 1 | tf_op jit(solution)/shard_map/branch_kernel/pallas_call | solution.py:437
  86.3 16.2 %collective-permute-done.11.refs_2_ = bf16[256,768]{1,0:T(8,128)(2,1)S(1)} collective-permute-done((bf16[256,768]{1,0:T(8,128)(2,1)}, bf16[256,768]{1,0:T(8,128)(2,1)S(1)}, u32[]{:S(2)}, u32[]{:S(2)}) %collective-permute-start.11) | collective-permute-done | bytes 393248 | tf_op jit(solution)/shard_map/ppermute | solution.py:403
  105.0 9.9 %feed_kernel.1 = (f32[256,768]{1,0:T(8,128)}, bf16[256,768]{1,0:T(8,128)(2,1)}, bf16[2,256,768]{2,1,0:T(8,128)(2,1)}, f32[256,768]{1,0:T(8,128)}, bf16[256,768]{...) custom-call(s32[3]{0:T(128)} %pad_add_fusion.refs_0_, ...), custom_call_target="tpu_custom_call" | custom-call | flops 11500000256 | bytes 1 | tf_op jit(solution)/shard_map/feed_kernel/pallas_call | solution.py:437
  115.4 2.0 collective-permute-done.14.refs_2_
  118.3 2.1 second_kernel.1.refs_8_
  120.7 7.6 %feed_grad_kernel.1 = (bf16[400,768]{1,0:T(8,128)(2,1)}, bf16[400,768]{1,0:T(8,128)(2,1)}, bf16[400,768]{1,0:T(8,128)(2,1)}, bf16[400,768]{1,0:T(8,128)(2,1)}) custom-call(s32[3]{0:T(128)} %pad_add_fusion.refs_0_, bf16[256,768]{1,0:T(8,128)(2,1)} %get-tuple-element.92.refs_1_.refs_13_, bf16[256,768]{1,0:T(8,128)(2,1)} %copy-done.13, ...), custom_call_target="tpu_custom_call" | custom-call | flops 8049999872 | bytes 1 | tf_op jit(solution)/shard_map/feed_grad_kernel/pallas_call | solution.py:437
  128.3 3.5 %collective-permute-done.15.refs_3_ = bf16[256,768]{1,0:T(8,128)(2,1)S(1)} collective-permute-done((bf16[256,768]{1,0:T(8,128)(2,1)}, bf16[256,768]{1,0:T(8,128)(2,1)S(1)}, u32[]{:S(2)}, u32[]{:S(2)}) %collective-permute-start.15) | collective-permute-done | bytes 393248 | tf_op jit(solution)/shard_map/ppermute | solution.py:403
  132.5 5.1 %back_kernel.1 = (f32[256,768]{1,0:T(8,128)}, bf16[256,768]{1,0:T(8,128)(2,1)}, bf16[4,192,256]{2,1,0:T(8,128)(2,1)}, f32[8,768]{1,0:T(8,128)}, bf16[384,768]{1,0:T(8,128)(2,1)}) custom-call(s32[3]{0:T(128)} %pad_add_fusion.refs_0_, f32[256,768]{1,0:T(8,128)} %get-tuple-element.94.refs_3_.refs_1_, bf16[2,256,768]{2,1,0:T(8,128)(2,1)} %copy-done.9, ...), custom_call_target="tpu_custom_call" | custom-call | flops 5750000128 | bytes 1 | tf_op jit(solution)/shard_map/back_kernel/pallas_call | solution.py:437
  137.6 3.7 %all-to-all-start.2 = ((bf16[4,192,256]{2,1,0:T(8,128)(2,1)}), bf16[4,192,256]{2,1,0:T(8,128)(2,1)S(1)}, u32[]{:S(2)}, u32[]{:S(2)}) async-start(bf16[4,192,256]{2,1,0:T(8,128)(2,1)} %get-tuple-element.107), calls=%async_computation.2 | async-start | bytes 786432 | tf_op jit(solution)/shard_map/all_to_all | solution.py:924
  145.4 3.9 %all-to-all-done.2.refs_4_ = bf16[4,192,256]{2,1,0:T(8,128)(2,1)S(1)} async-done(((bf16[4,192,256]{2,1,0:T(8,128)(2,1)}), bf16[4,192,256]{2,1,0:T(8,128)(2,1)S(1)}, u32[]{:S(2)}, u32[]{:S(2)}) %all-to-all-start.2) | async-done | bytes 393248 | tf_op jit(solution)/shard_map/all_to_all | solution.py:924
  150.1 14.8 %attend_back_kernel.1 = (bf16[4,576,256]{2,1,0:T(8,128)(2,1)}, bf16[4,256,768]{2,1,0:T(8,128)(2,1)}, f32[8,768]{1,0:T(8,128)}) custom-call(s32[3]{0:T(128)} %pad_add_fusion.refs_0_, bf16[4,576,256]{2,1,0:T(8,128)(2,1)} %get-tuple-element.104.refs_1_, f32[12,8,256]{2,1,0:T(8,128)} %get-tuple-element.105.refs_2_, f32[4,192,256]{2,1,0:T(8,128)} %get-tuple-element.106.refs_3_, ...), custom_call_target="tpu_custom_call" | custom-call | flops 17250000896 | bytes 1 | tf_op jit(solution)/shard_map/attend_back_kernel/pallas_call | solution.py:437
  164.9 3.6 %all-to-all-start.3 = ((bf16[4,256,768]{2,1,0:T(8,128)(2,1)}), bf16[4,256,768]{2,1,0:T(8,128)(2,1)S(1)}, u32[]{:S(2)}, u32[]{:S(2)}) async-start(bf16[4,256,768]{2,1,0:T(8,128)(2,1)} %get-tuple-element.109), calls=%async_computation.3 | async-start | bytes 3145728 | tf_op jit(solution)/shard_map/all_to_all | solution.py:924
  168.5 2.7 out_kernel.1
  171.2 5.5 %collective-permute-done.19.refs_4_ = bf16[400,768]{1,0:T(8,128)(2,1)} collective-permute-done((bf16[400,768]{1,0:T(8,128)(2,1)S(1)}, bf16[400,768]{1,0:T(8,128)(2,1)}, u32[]{:S(2)}, u32[]{:S(2)}) %collective-permute-start.19) | collective-permute-done | bytes 614432 | tf_op jit(solution)/shard_map/ppermute | solution.py:407
  176.8 2.7 pieces_kernel.1
  179.4 4.9 %qkv_grad_kernel.1 = (bf16[2,224,576]{2,1,0:T(8,128)(2,1)}, bf16[2,224,576]{2,1,0:T(8,128)(2,1)}) custom-call(s32[3]{0:T(128)} %pad_add_fusion.refs_0_, bf16[4,256,768]{2,1,0:T(8,128)(2,1)} %get-tuple-element.91.refs_8_.refs_1_, bf16[4,576,256]{2,1,0:T(8,128)(2,1)} %get-tuple-element.115.refs_6_.refs_2_, f32[8,768]{1,0:T(8,128)} %get-tuple-element.118.refs_3_, ...), custom_call_target="tpu_custom_call" | custom-call | flops 5750000128 | bytes 1 | tf_op jit(solution)/shard_map/qkv_grad_kernel/pallas_call | solution.py:437
  185.3 2.5 collective-permute-start.21
  188.6 2.1 chain_kernel.1
  191.2 3.3 %out_grad_kernel.1 = (bf16[64,576]{1,0:T(8,128)(2,1)}, bf16[64,576]{1,0:T(8,128)(2,1)}, bf16[64,576]{1,0:T(8,128)(2,1)}, bf16[64,576]{1,0:T(8,128)(2,1)}) custom-call(s32[3]{0:T(128)} %pad_add_fusion.refs_0_, bf16[4,64,768]{2,1,0:T(8,128)(2,1)} %get-tuple-element.93.refs_12_.refs_10_.refs_1_, bf16[640,768]{1,0:T(8,128)(2,1)} %copy-done.8, ...), custom_call_target="tpu_custom_call" | custom-call | flops 3449999872 | bytes 1 | tf_op jit(solution)/shard_map/out_grad_kernel/pallas_call | solution.py:437
  195.1 2.9 %collective-permute-start.26 = (bf16[64,576]{1,0:T(8,128)(2,1)}, bf16[64,576]{1,0:T(8,128)(2,1)S(1)}, u32[]{:S(2)}, u32[]{:S(2)}) collective-permute-start(bf16[64,576]{1,0:T(8,128)(2,1)} %get-tuple-element.128), channel_id=1, source_target_pairs={{0,3},{1,2},{2,1},{3,0},{4,7},{5,6},{6,5},{7,4},{8,11},{9,10},{10,... | collective-permute-start | bytes 221192 | tf_op jit(solution)/shard_map/ppermute | solution.py:407
  200.9 3.0 %collective-permute-done.25.refs_5_ = bf16[64,576]{1,0:T(8,128)(2,1)S(1)} collective-permute-done((bf16[64,576]{1,0:T(8,128)(2,1)}, bf16[64,576]{1,0:T(8,128)(2,1)S(1)}, u32[]{:S(2)}, u32[]{:S(2)}) %collective-permute-start.25) | collective-permute-done | bytes 73760 | tf_op jit(solution)/shard_map/ppermute | solution.py:403
  206.0 2.0 join_kernel.1.refs_3_.refs_1_
  212.9 2.7 collective-permute-start.34
  218.0 2.6 hidden_grad_kernel.1
  222.4 8.9 %collective-permute-done.29.refs_2_ = bf16[288,576]{1,0:T(8,128)(2,1)S(1)} collective-permute-done((bf16[288,576]{1,0:T(8,128)(2,1)S(1)}, bf16[288,576]{1,0:T(8,128)(2,1)S(1)}, u32[]{:S(2)}, u32[]{:S(2)}) %collective-permute-start.29) | collective-permute-done | bytes 331808 | tf_op jit(solution)/shard_map/ppermute | solution.py:403
  232.0 2.0 both_kernel.5.refs_5_.refs_1_
  234.0 4.9 %collective-permute-start.33 = (bf16[288,576]{1,0:T(8,128)(2,1)}, bf16[288,576]{1,0:T(8,128)(2,1)S(1)}, u32[]{:S(2)}, u32[]{:S(2)}) collective-permute-start(bf16[288,576]{1,0:T(8,128)(2,1)} %both_kernel.5.refs_5_.refs_1_), channel_id=1, source_target_pairs={{0,3},{1,2},{2,1},{3,0},{4,7},{5,6},{6,5},{7,4},{8,11},{9,10},{10,... | collective-permute-start | bytes 995336 | tf_op jit(solution)/shard_map/ppermute | solution.py:407
  242.4 3.5 %all-to-all-start.4 = ((bf16[4,48,768]{2,1,0:T(8,128)(2,1)}), bf16[4,48,768]{2,1,0:T(8,128)(2,1)S(1)}, u32[]{:S(2)}, u32[]{:S(2)}) async-start(bf16[4,48,768]{2,1,0:T(8,128)(2,1)} %both_kernel.4.refs_3_), calls=%async_computation.4 | async-start | bytes 589824 | tf_op jit(solution)/shard_map/all_to_all | solution.py:927
  246.0 2.9 %collective-permute-start.27 = (bf16[128,768]{1,0:T(8,128)(2,1)S(1)}, bf16[128,768]{1,0:T(8,128)(2,1)S(1)}, u32[]{:S(2)}, u32[]{:S(2)}) collective-permute-start(bf16[128,768]{1,0:T(8,128)(2,1)S(1)} %copy-done.44), channel_id=1, source_target_pairs={{0,4},{4,0},{1,5},{5,1},{2,6},{6,2},{3,7},{7,3},{8,12},{12,8},{9,1... | collective-permute-start | bytes 589832 | tf_op jit(solution)/shard_map/ppermute | solution.py:403
  248.9 2.9 %down_total_kernel.1 = (f32[4,192,768]{2,1,0:T(8,128)}, f32[768]{0:T(1024)}, f32[192]{0:T(256)}) custom-call(s32[3]{0:T(128)} %pad_add_fusion.refs_0_, bf16[208,768]{1,0:T(8,128)(2,1)} %both_kernel.3.refs_3_.refs_1_, bf16[208,768]{1,0:T(8,128)(2,1)} %copy-done.26, bf16[208,768]{1,0:T(8,128)(2,1)} %copy-done.25, bf16[208,768]{1,0:T(8,128)(2,1)} %copy-done.23, ...), custom_call_target="tpu_custom_call" | custom-call | flops 3449999872 | bytes 1 | tf_op jit(solution)/shard_map/down_total_kernel/pallas_call | solution.py:437
  253.6 11.3 %collective-permute-done.32.refs_3_ = bf16[288,576]{1,0:T(8,128)(2,1)S(1)} collective-permute-done((bf16[288,576]{1,0:T(8,128)(2,1)}, bf16[288,576]{1,0:T(8,128)(2,1)S(1)}, u32[]{:S(2)}, u32[]{:S(2)}) %collective-permute-start.32) | collective-permute-done | bytes 331808 | tf_op jit(solution)/shard_map/ppermute | solution.py:403
  265.8 3.5 %total_kernel.1 = (f32[192,2304]{1,0:T(8,128)}, f32[4,48,768]{2,1,0:T(8,128)}, f32[192,768]{1,0:T(8,128)}, f32[8,576]{1,0:T(8,128)}, f32[1,192]{1,0:T(1,128)}) custom-call(s32[3]{0:T(128)} %pad_add_fusion.refs_0_, bf16[288,576]{1,0:T(8,128)(2,1)} %both_kernel.5.refs_5_.refs_1_, bf16[288,576]{1,0:T(8,128)(2,1)} %copy-done.19, bf16[288,576]{1,0:T(8,128)(2,1)} %copy-done.18, ...), custom_call_target="tpu_custom_call" | custom-call | flops 3449999872 | bytes 1 | tf_op jit(solution)/shard_map/total_kernel/pallas_call | solution.py:437
  270.0 2.1 pair_kernel.1
  273.7 3.1 %collective-permute-done.38.refs_3_ = bf16[4,48,768]{2,1,0:T(8,128)(2,1)S(1)} collective-permute-done((bf16[4,48,768]{2,1,0:T(8,128)(2,1)S(1)}, bf16[4,48,768]{2,1,0:T(8,128)(2,1)S(1)}, u32[]{:S(2)}, u32[]{:S(2)}) %collective-permute-start.38) | collective-permute-done | bytes 294944 | tf_op jit(solution)/shard_map/ppermute | solution.py:403
  277.6 2.8 up_total_kernel.1
  (232 shorter events, 48.5 us)
Async XLA Ops:
  7.2 44.0 %all-gather.8.cloned.1.call-start = ((), (), s32[]{:S(2)}) async-start(), calls=%async_computation.5 | async-start | bytes 1474560 | tf_op jit(solution)/shard_map/all_gather | solution.py:953
  9.6 28.6 %collective-permute-start.2 = (bf16[128,768]{1,0:T(8,128)(2,1)}, bf16[128,768]{1,0:T(8,128)(2,1)S(1)}, u32[]{:S(2)}, u32[]{:S(2)}) collective-permute-start(bf16[128,768]{1,0:T(8,128)(2,1)} %get-tuple-element.80.refs_2_.refs_1_.refs_3_.refs_6_), channel_id=1, source_target_pairs={{0,3},{1,2},{2,1},{3,0},{4,7},{5,6},{6,5},{7,4},{8,11},{9,10},{10,... | collective-permute-start | bytes 589832 | tf_op jit(solution)/shard_map/ppermute | solution.py:407
  13.6 27.5 %collective-permute-start.1 = (bf16[128,768]{1,0:T(8,128)(2,1)}, bf16[128,768]{1,0:T(8,128)(2,1)S(1)}, u32[]{:S(2)}, u32[]{:S(2)}) collective-permute-start(bf16[128,768]{1,0:T(8,128)(2,1)} %get-tuple-element.80.refs_2_.refs_1_.refs_3_.refs_6_), channel_id=1, source_target_pairs={{0,2},{2,0},{1,3},{3,1},{4,6},{6,4},{5,7},{7,5},{8,10},{10,8},{9,1... | collective-permute-start | bytes 589832 | tf_op jit(solution)/shard_map/ppermute | solution.py:403
  14.0 27.5 %collective-permute-start = (bf16[128,768]{1,0:T(8,128)(2,1)}, bf16[128,768]{1,0:T(8,128)(2,1)S(1)}, u32[]{:S(2)}, u32[]{:S(2)}) collective-permute-start(bf16[128,768]{1,0:T(8,128)(2,1)} %get-tuple-element.80.refs_2_.refs_1_.refs_3_.refs_6_), channel_id=1, source_target_pairs={{0,1},{1,0},{2,3},{3,2},{4,5},{5,4},{6,7},{7,6},{8,9},{9,8},{10,11... | collective-permute-start | bytes 589832 | tf_op jit(solution)/shard_map/ppermute | solution.py:403
  16.1 18.7 %collective-permute-start.9 = (bf16[128,768]{1,0:T(8,128)(2,1)}, bf16[128,768]{1,0:T(8,128)(2,1)S(1)}, u32[]{:S(2)}, u32[]{:S(2)}) collective-permute-start(bf16[128,768]{1,0:T(8,128)(2,1)} %pick_kernel.1.refs_3_), channel_id=1, source_target_pairs={{0,4},{4,0},{1,5},{5,1},{2,6},{6,2},{3,7},{7,3},{8,12},{12,8},{9,1... | collective-permute-start | bytes 589832 | tf_op jit(solution)/shard_map/ppermute | solution.py:403
  19.1 17.7 %collective-permute-start.3 = (bf16[128,768]{1,0:T(8,128)(2,1)S(1)}, bf16[128,768]{1,0:T(8,128)(2,1)S(1)}, u32[]{:S(2)}, u32[]{:S(2)}) collective-permute-start(bf16[128,768]{1,0:T(8,128)(2,1)S(1)} %copy-done.45), channel_id=1, source_target_pairs={{0,4},{4,0},{1,5},{5,1},{2,6},{6,2},{3,7},{7,3},{8,12},{12,8},{9,1... | collective-permute-start | bytes 589832 | tf_op jit(solution)/shard_map/ppermute | solution.py:403
  27.4 23.8 %all-to-all-start = ((bf16[4,192,576]{2,1,0:T(8,128)(2,1)}), bf16[4,192,576]{2,1,0:T(8,128)(2,1)S(1)}, u32[]{:S(2)}, u32[]{:S(2)}) async-start(bf16[4,192,576]{2,1,0:T(8,128)(2,1)} %column_kernel.1.refs_2_), calls=%async_computation | async-start | bytes 1966080 | tf_op jit(solution)/shard_map/all_to_all | solution.py:927
  31.0 50.1 %all-gather.10.cloned.1.call-start = ((), (), s32[]{:S(2)}) async-start(), calls=%async_computation.6 | async-start | bytes 1474560 | tf_op jit(solution)/shard_map/all_gather | solution.py:994
  34.8 16.3 %collective-permute-start.7 = (bf16[192,768]{1,0:T(8,128)(2,1)}, bf16[192,768]{1,0:T(8,128)(2,1)S(1)}, u32[]{:S(2)}, u32[]{:S(2)}) collective-permute-start(bf16[192,768]{1,0:T(8,128)(2,1)} %get-tuple-element.83), channel_id=1, source_target_pairs={{0,16},{16,0},{1,17},{17,1},{2,18},{18,2},{3,19},{19,3},{4,20},{20... | collective-permute-start | bytes 884744 | tf_op jit(solution)/shard_map/ppermute | solution.py:403
  36.8 14.3 %collective-permute-start.8 = (bf16[192,768]{1,0:T(8,128)(2,1)}, bf16[192,768]{1,0:T(8,128)(2,1)S(1)}, u32[]{:S(2)}, u32[]{:S(2)}) collective-permute-start(bf16[192,768]{1,0:T(8,128)(2,1)} %get-tuple-element.84), channel_id=1, source_target_pairs={{0,8},{8,0},{1,9},{9,1},{2,10},{10,2},{3,11},{11,3},{4,12},{12,4},... | collective-permute-start | bytes 884744 | tf_op jit(solution)/shard_map/ppermute | solution.py:403
  38.2 12.9 %collective-permute-start.6 = (bf16[128,768]{1,0:T(8,128)(2,1)S(1)}, bf16[128,768]{1,0:T(8,128)(2,1)S(1)}, u32[]{:S(2)}, u32[]{:S(2)}) collective-permute-start(bf16[128,768]{1,0:T(8,128)(2,1)S(1)} %collective-permute-done.3.refs_5_.refs_4_.refs_10_), channel_id=1, source_target_pairs={{0,3},{1,2},{2,1},{3,0},{4,7},{5,6},{6,5},{7,4},{8,11},{9,10},{10,... | collective-permute-start | bytes 589832 | tf_op jit(solution)/shard_map/ppermute | solution.py:407
  41.1 10.1 %collective-permute-start.5 = (bf16[128,768]{1,0:T(8,128)(2,1)S(1)}, bf16[128,768]{1,0:T(8,128)(2,1)S(1)}, u32[]{:S(2)}, u32[]{:S(2)}) collective-permute-start(bf16[128,768]{1,0:T(8,128)(2,1)S(1)} %collective-permute-done.3.refs_5_.refs_4_.refs_10_), channel_id=1, source_target_pairs={{0,2},{2,0},{1,3},{3,1},{4,6},{6,4},{5,7},{7,5},{8,10},{10,8},{9,1... | collective-permute-start | bytes 589832 | tf_op jit(solution)/shard_map/ppermute | solution.py:403
  41.5 9.6 %collective-permute-start.4 = (bf16[128,768]{1,0:T(8,128)(2,1)S(1)}, bf16[128,768]{1,0:T(8,128)(2,1)S(1)}, u32[]{:S(2)}, u32[]{:S(2)}) collective-permute-start(bf16[128,768]{1,0:T(8,128)(2,1)S(1)} %collective-permute-done.3.refs_5_.refs_4_.refs_10_), channel_id=1, source_target_pairs={{0,1},{1,0},{2,3},{3,2},{4,5},{5,4},{6,7},{7,6},{8,9},{9,8},{10,11... | collective-permute-start | bytes 589832 | tf_op jit(solution)/shard_map/ppermute | solution.py:403
  68.1 13.1 %all-to-all-start.1 = ((bf16[4,192,256]{2,1,0:T(8,128)(2,1)}), bf16[4,192,256]{2,1,0:T(8,128)(2,1)S(1)}, u32[]{:S(2)}, u32[]{:S(2)}) async-start(bf16[4,192,256]{2,1,0:T(8,128)(2,1)} %get-tuple-element.87), calls=%async_computation.1 | async-start | bytes 786432 | tf_op jit(solution)/shard_map/all_to_all | solution.py:924
  72.3 30.9 %all-gather.12.cloned.1.call-start = ((), (), s32[]{:S(2)}) async-start(), calls=%async_computation.7 | async-start | bytes 1966080 | tf_op jit(solution)/shard_map/all_gather | solution.py:995
  72.3 8.9 %collective-permute-start.10 = (bf16[192,768]{1,0:T(8,128)(2,1)S(1)}, bf16[192,768]{1,0:T(8,128)(2,1)S(1)}, u32[]{:S(2)}, u32[]{:S(2)}) collective-permute-start(bf16[192,768]{1,0:T(8,128)(2,1)S(1)} %copy-done.29), channel_id=1, source_target_pairs={{0,24},{8,16},{16,8},{24,0},{1,25},{9,17},{17,9},{25,1},{2,26},{10... | collective-permute-start | bytes 884744 | tf_op jit(solution)/shard_map/ppermute | solution.py:936
  85.4 17.2 %collective-permute-start.11 = (bf16[256,768]{1,0:T(8,128)(2,1)}, bf16[256,768]{1,0:T(8,128)(2,1)S(1)}, u32[]{:S(2)}, u32[]{:S(2)}) collective-permute-start(bf16[256,768]{1,0:T(8,128)(2,1)} %get-tuple-element.92.refs_1_.refs_13_), channel_id=1, source_target_pairs={{0,16},{16,0},{1,17},{17,1},{2,18},{18,2},{3,19},{19,3},{4,20},{20... | collective-permute-start | bytes 1179656 | tf_op jit(solution)/shard_map/ppermute | solution.py:403
  86.3 16.9 %collective-permute-start.12 = (bf16[256,768]{1,0:T(8,128)(2,1)}, bf16[256,768]{1,0:T(8,128)(2,1)S(1)}, u32[]{:S(2)}, u32[]{:S(2)}) collective-permute-start(bf16[256,768]{1,0:T(8,128)(2,1)} %get-tuple-element.92.refs_1_.refs_13_), channel_id=1, source_target_pairs={{0,8},{8,0},{1,9},{9,1},{2,10},{10,2},{3,11},{11,3},{4,12},{12,4},... | collective-permute-start | bytes 1179656 | tf_op jit(solution)/shard_map/ppermute | solution.py:403
  114.9 2.5 collective-permute-start.14
  115.0 13.3 %collective-permute-start.16 = (bf16[640,768]{1,0:T(8,128)(2,1)}, bf16[640,768]{1,0:T(8,128)(2,1)S(1)}, u32[]{:S(2)}, u32[]{:S(2)}) collective-permute-start(bf16[640,768]{1,0:T(8,128)(2,1)} %get-tuple-element.99), channel_id=1, source_target_pairs={{0,8},{8,0},{1,9},{9,1},{2,10},{10,2},{3,11},{11,3},{4,12},{12,4},... | collective-permute-start | bytes 2949128 | tf_op jit(solution)/shard_map/ppermute | solution.py:403
  120.4 11.4 %collective-permute-start.15 = (bf16[256,768]{1,0:T(8,128)(2,1)}, bf16[256,768]{1,0:T(8,128)(2,1)S(1)}, u32[]{:S(2)}, u32[]{:S(2)}) collective-permute-start(bf16[256,768]{1,0:T(8,128)(2,1)} %second_kernel.1.refs_8_), channel_id=1, source_target_pairs={{0,16},{16,0},{1,17},{17,1},{2,18},{18,2},{3,19},{19,3},{4,20},{20... | collective-permute-start | bytes 1179656 | tf_op jit(solution)/shard_map/ppermute | solution.py:403
  137.6 11.7 %all-to-all-start.2 = ((bf16[4,192,256]{2,1,0:T(8,128)(2,1)}), bf16[4,192,256]{2,1,0:T(8,128)(2,1)S(1)}, u32[]{:S(2)}, u32[]{:S(2)}) async-start(bf16[4,192,256]{2,1,0:T(8,128)(2,1)} %get-tuple-element.107), calls=%async_computation.2 | async-start | bytes 786432 | tf_op jit(solution)/shard_map/all_to_all | solution.py:924
  141.3 49.9 %all-gather.14.cloned.1.call-start = ((), (), s32[]{:S(2)}) async-start(), calls=%async_computation.8 | async-start | bytes 1966080 | tf_op jit(solution)/shard_map/all_gather | solution.py:1029
  141.4 29.9 %collective-permute-start.17 = (bf16[400,768]{1,0:T(8,128)(2,1)}, bf16[400,768]{1,0:T(8,128)(2,1)S(1)}, u32[]{:S(2)}, u32[]{:S(2)}) collective-permute-start(bf16[400,768]{1,0:T(8,128)(2,1)} %get-tuple-element.110), channel_id=1, source_target_pairs={{0,1},{1,0},{2,3},{3,2},{4,5},{5,4},{6,7},{7,6},{8,9},{9,8},{10,11... | collective-permute-start | bytes 1843208 | tf_op jit(solution)/shard_map/ppermute | solution.py:403
  143.3 27.9 %collective-permute-start.18 = (bf16[400,768]{1,0:T(8,128)(2,1)}, bf16[400,768]{1,0:T(8,128)(2,1)}, u32[]{:S(2)}, u32[]{:S(2)}) collective-permute-start(bf16[400,768]{1,0:T(8,128)(2,1)} %get-tuple-element.111), channel_id=1, source_target_pairs={{0,2},{2,0},{1,3},{3,1},{4,6},{6,4},{5,7},{7,5},{8,10},{10,8},{9,1... | collective-permute-start | bytes 1843208 | tf_op jit(solution)/shard_map/ppermute | solution.py:403
  144.8 32.0 %collective-permute-start.19 = (bf16[400,768]{1,0:T(8,128)(2,1)S(1)}, bf16[400,768]{1,0:T(8,128)(2,1)}, u32[]{:S(2)}, u32[]{:S(2)}) collective-permute-start(bf16[400,768]{1,0:T(8,128)(2,1)S(1)} %copy-done.10), channel_id=1, source_target_pairs={{0,3},{1,2},{2,1},{3,0},{4,7},{5,6},{6,5},{7,4},{8,11},{9,10},{10,... | collective-permute-start | bytes 1843208 | tf_op jit(solution)/shard_map/ppermute | solution.py:407
  144.9 23.6 %collective-permute-start.20 = (bf16[384,768]{1,0:T(8,128)(2,1)}, bf16[384,768]{1,0:T(8,128)(2,1)}, u32[]{:S(2)}, u32[]{:S(2)}) collective-permute-start(bf16[384,768]{1,0:T(8,128)(2,1)} %get-tuple-element.114), channel_id=1, source_target_pairs={{0,16},{16,0},{1,17},{17,1},{2,18},{18,2},{3,19},{19,3},{4,20},{20... | collective-permute-start | bytes 1769480 | tf_op jit(solution)/shard_map/ppermute | solution.py:403
  164.9 51.9 %all-to-all-start.3 = ((bf16[4,256,768]{2,1,0:T(8,128)(2,1)}), bf16[4,256,768]{2,1,0:T(8,128)(2,1)S(1)}, u32[]{:S(2)}, u32[]{:S(2)}) async-start(bf16[4,256,768]{2,1,0:T(8,128)(2,1)} %get-tuple-element.109), calls=%async_computation.3 | async-start | bytes 3145728 | tf_op jit(solution)/shard_map/all_to_all | solution.py:924
  184.3 3.5 %collective-permute-start.22 = (bf16[2,224,576]{2,1,0:T(8,128)(2,1)}, bf16[2,224,576]{2,1,0:T(8,128)(2,1)S(1)}, u32[]{:S(2)}, u32[]{:S(2)}) collective-permute-start(bf16[2,224,576]{2,1,0:T(8,128)(2,1)} %get-tuple-element.121), channel_id=1, source_target_pairs={{0,8},{8,0},{1,9},{9,1},{2,10},{10,2},{3,11},{11,3},{4,12},{12,4},... | collective-permute-start | bytes 1548296 | tf_op jit(solution)/shard_map/ppermute | solution.py:403
  185.3 24.3 %collective-permute-start.21 = (bf16[208,768]{1,0:T(8,128)(2,1)S(1)}, bf16[208,768]{1,0:T(8,128)(2,1)S(1)}, u32[]{:S(2)}, u32[]{:S(2)}) collective-permute-start(bf16[208,768]{1,0:T(8,128)(2,1)S(1)} %copy-done.22), channel_id=1, source_target_pairs={{0,4},{4,0},{1,5},{5,1},{2,6},{6,2},{3,7},{7,3},{8,12},{12,8},{9,1... | collective-permute-start | bytes 958472 | tf_op jit(solution)/shard_map/ppermute | solution.py:403
  190.7 9.2 %collective-permute-start.23 = (bf16[224,576]{1,0:T(8,128)(2,1)}, bf16[224,576]{1,0:T(8,128)(2,1)S(1)}, u32[]{:S(2)}, u32[]{:S(2)}) collective-permute-start(bf16[224,576]{1,0:T(8,128)(2,1)} %get-tuple-element.123), channel_id=1, source_target_pairs={{0,16},{16,0},{1,17},{17,1},{2,18},{18,2},{3,19},{19,3},{4,20},{20... | collective-permute-start | bytes 774152 | tf_op jit(solution)/shard_map/ppermute | solution.py:403
  194.5 6.4 %collective-permute-start.24 = (bf16[64,576]{1,0:T(8,128)(2,1)}, bf16[64,576]{1,0:T(8,128)(2,1)S(1)}, u32[]{:S(2)}, u32[]{:S(2)}) collective-permute-start(bf16[64,576]{1,0:T(8,128)(2,1)} %get-tuple-element.126), channel_id=1, source_target_pairs={{0,1},{1,0},{2,3},{3,2},{4,5},{5,4},{6,7},{7,6},{8,9},{9,8},{10,11... | collective-permute-start | bytes 221192 | tf_op jit(solution)/shard_map/ppermute | solution.py:403
  195.1 8.8 %collective-permute-start.25 = (bf16[64,576]{1,0:T(8,128)(2,1)}, bf16[64,576]{1,0:T(8,128)(2,1)S(1)}, u32[]{:S(2)}, u32[]{:S(2)}) collective-permute-start(bf16[64,576]{1,0:T(8,128)(2,1)} %get-tuple-element.127), channel_id=1, source_target_pairs={{0,2},{2,0},{1,3},{3,1},{4,6},{6,4},{5,7},{7,5},{8,10},{10,8},{9,1... | collective-permute-start | bytes 221192 | tf_op jit(solution)/shard_map/ppermute | solution.py:403
  195.1 10.3 %collective-permute-start.26 = (bf16[64,576]{1,0:T(8,128)(2,1)}, bf16[64,576]{1,0:T(8,128)(2,1)S(1)}, u32[]{:S(2)}, u32[]{:S(2)}) collective-permute-start(bf16[64,576]{1,0:T(8,128)(2,1)} %get-tuple-element.128), channel_id=1, source_target_pairs={{0,3},{1,2},{2,1},{3,0},{4,7},{5,6},{6,5},{7,4},{8,11},{9,10},{10,... | collective-permute-start | bytes 221192 | tf_op jit(solution)/shard_map/ppermute | solution.py:407
  199.8 20.7 %collective-permute-start.30 = (bf16[4,48,768]{2,1,0:T(8,128)(2,1)}, bf16[4,48,768]{2,1,0:T(8,128)(2,1)}, u32[]{:S(2)}, u32[]{:S(2)}) collective-permute-start(bf16[4,48,768]{2,1,0:T(8,128)(2,1)} %get-tuple-element.132.refs_1_), channel_id=1, source_target_pairs={{0,4},{4,0},{1,5},{5,1},{2,6},{6,2},{3,7},{7,3},{8,12},{12,8},{9,1... | collective-permute-start | bytes 884744 | tf_op jit(solution)/shard_map/ppermute | solution.py:403
  212.1 28.0 %collective-permute-start.36 = (bf16[208,768]{1,0:T(8,128)(2,1)}, bf16[208,768]{1,0:T(8,128)(2,1)S(1)}, u32[]{:S(2)}, u32[]{:S(2)}) collective-permute-start(bf16[208,768]{1,0:T(8,128)(2,1)} %both_kernel.3.refs_3_.refs_1_), channel_id=1, source_target_pairs={{0,3},{1,2},{2,1},{3,0},{4,7},{5,6},{6,5},{7,4},{8,11},{9,10},{10,... | collective-permute-start | bytes 958472 | tf_op jit(solution)/shard_map/ppermute | solution.py:407
  212.1 33.7 %collective-permute-start.35 = (bf16[208,768]{1,0:T(8,128)(2,1)}, bf16[208,768]{1,0:T(8,128)(2,1)S(1)}, u32[]{:S(2)}, u32[]{:S(2)}) collective-permute-start(bf16[208,768]{1,0:T(8,128)(2,1)} %both_kernel.3.refs_3_.refs_1_), channel_id=1, source_target_pairs={{0,2},{2,0},{1,3},{3,1},{4,6},{6,4},{5,7},{7,5},{8,10},{10,8},{9,1... | collective-permute-start | bytes 958472 | tf_op jit(solution)/shard_map/ppermute | solution.py:403
  212.9 33.0 %collective-permute-start.34 = (bf16[208,768]{1,0:T(8,128)(2,1)}, bf16[208,768]{1,0:T(8,128)(2,1)S(1)}, u32[]{:S(2)}, u32[]{:S(2)}) collective-permute-start(bf16[208,768]{1,0:T(8,128)(2,1)} %both_kernel.3.refs_3_.refs_1_), channel_id=1, source_target_pairs={{0,1},{1,0},{2,3},{3,2},{4,5},{5,4},{6,7},{7,6},{8,9},{9,8},{10,11... | collective-permute-start | bytes 958472 | tf_op jit(solution)/shard_map/ppermute | solution.py:403
  215.6 15.7 %collective-permute-start.29 = (bf16[288,576]{1,0:T(8,128)(2,1)S(1)}, bf16[288,576]{1,0:T(8,128)(2,1)S(1)}, u32[]{:S(2)}, u32[]{:S(2)}) collective-permute-start(bf16[288,576]{1,0:T(8,128)(2,1)S(1)} %copy-done.20), channel_id=1, source_target_pairs={{0,4},{4,0},{1,5},{5,1},{2,6},{6,2},{3,7},{7,3},{8,12},{12,8},{9,1... | collective-permute-start | bytes 995336 | tf_op jit(solution)/shard_map/ppermute | solution.py:403
  234.0 18.2 %collective-permute-start.33 = (bf16[288,576]{1,0:T(8,128)(2,1)}, bf16[288,576]{1,0:T(8,128)(2,1)S(1)}, u32[]{:S(2)}, u32[]{:S(2)}) collective-permute-start(bf16[288,576]{1,0:T(8,128)(2,1)} %both_kernel.5.refs_5_.refs_1_), channel_id=1, source_target_pairs={{0,3},{1,2},{2,1},{3,0},{4,7},{5,6},{6,5},{7,4},{8,11},{9,10},{10,... | collective-permute-start | bytes 995336 | tf_op jit(solution)/shard_map/ppermute | solution.py:407
  238.9 26.0 %collective-permute-start.32 = (bf16[288,576]{1,0:T(8,128)(2,1)}, bf16[288,576]{1,0:T(8,128)(2,1)S(1)}, u32[]{:S(2)}, u32[]{:S(2)}) collective-permute-start(bf16[288,576]{1,0:T(8,128)(2,1)} %both_kernel.5.refs_5_.refs_1_), channel_id=1, source_target_pairs={{0,2},{2,0},{1,3},{3,1},{4,6},{6,4},{5,7},{7,5},{8,10},{10,8},{9,1... | collective-permute-start | bytes 995336 | tf_op jit(solution)/shard_map/ppermute | solution.py:403
  240.1 24.8 %collective-permute-start.31 = (bf16[288,576]{1,0:T(8,128)(2,1)}, bf16[288,576]{1,0:T(8,128)(2,1)S(1)}, u32[]{:S(2)}, u32[]{:S(2)}) collective-permute-start(bf16[288,576]{1,0:T(8,128)(2,1)} %both_kernel.5.refs_5_.refs_1_), channel_id=1, source_target_pairs={{0,1},{1,0},{2,3},{3,2},{4,5},{5,4},{6,7},{7,6},{8,9},{9,8},{10,11... | collective-permute-start | bytes 995336 | tf_op jit(solution)/shard_map/ppermute | solution.py:403
  242.4 9.8 %all-to-all-start.4 = ((bf16[4,48,768]{2,1,0:T(8,128)(2,1)}), bf16[4,48,768]{2,1,0:T(8,128)(2,1)S(1)}, u32[]{:S(2)}, u32[]{:S(2)}) async-start(bf16[4,48,768]{2,1,0:T(8,128)(2,1)} %both_kernel.4.refs_3_), calls=%async_computation.4 | async-start | bytes 589824 | tf_op jit(solution)/shard_map/all_to_all | solution.py:927
  245.8 23.4 %collective-permute-start.28 = (bf16[128,768]{1,0:T(8,128)(2,1)S(1)}, bf16[128,768]{1,0:T(8,128)(2,1)S(1)}, u32[]{:S(2)}, u32[]{:S(2)}) collective-permute-start(bf16[128,768]{1,0:T(8,128)(2,1)S(1)} %copy-done.39), channel_id=1, source_target_pairs={{0,4},{4,0},{1,5},{5,1},{2,6},{6,2},{3,7},{7,3},{8,12},{12,8},{9,1... | collective-permute-start | bytes 589832 | tf_op jit(solution)/shard_map/ppermute | solution.py:403
  246.0 23.3 %collective-permute-start.27 = (bf16[128,768]{1,0:T(8,128)(2,1)S(1)}, bf16[128,768]{1,0:T(8,128)(2,1)S(1)}, u32[]{:S(2)}, u32[]{:S(2)}) collective-permute-start(bf16[128,768]{1,0:T(8,128)(2,1)S(1)} %copy-done.44), channel_id=1, source_target_pairs={{0,4},{4,0},{1,5},{5,1},{2,6},{6,2},{3,7},{7,3},{8,12},{12,8},{9,1... | collective-permute-start | bytes 589832 | tf_op jit(solution)/shard_map/ppermute | solution.py:403
  252.2 21.5 %collective-permute-start.39 = (bf16[4,48,768]{2,1,0:T(8,128)(2,1)S(1)}, bf16[4,48,768]{2,1,0:T(8,128)(2,1)S(1)}, u32[]{:S(2)}, u32[]{:S(2)}) collective-permute-start(bf16[4,48,768]{2,1,0:T(8,128)(2,1)S(1)} %all-to-all-done.4.refs_1_), channel_id=1, source_target_pairs={{0,3},{1,2},{2,1},{3,0},{4,7},{5,6},{6,5},{7,4},{8,11},{9,10},{10,... | collective-permute-start | bytes 884744 | tf_op jit(solution)/shard_map/ppermute | solution.py:407
  264.9 11.8 %collective-permute-start.38 = (bf16[4,48,768]{2,1,0:T(8,128)(2,1)S(1)}, bf16[4,48,768]{2,1,0:T(8,128)(2,1)S(1)}, u32[]{:S(2)}, u32[]{:S(2)}) collective-permute-start(bf16[4,48,768]{2,1,0:T(8,128)(2,1)S(1)} %all-to-all-done.4.refs_1_), channel_id=1, source_target_pairs={{0,2},{2,0},{1,3},{3,1},{4,6},{6,4},{5,7},{7,5},{8,10},{10,8},{9,1... | collective-permute-start | bytes 884744 | tf_op jit(solution)/shard_map/ppermute | solution.py:403
  265.0 11.8 %collective-permute-start.37 = (bf16[4,48,768]{2,1,0:T(8,128)(2,1)S(1)}, bf16[4,48,768]{2,1,0:T(8,128)(2,1)S(1)}, u32[]{:S(2)}, u32[]{:S(2)}) collective-permute-start(bf16[4,48,768]{2,1,0:T(8,128)(2,1)S(1)} %all-to-all-done.4.refs_1_), channel_id=1, source_target_pairs={{0,1},{1,0},{2,3},{3,2},{4,5},{5,4},{6,7},{7,6},{8,9},{9,8},{10,11... | collective-permute-start | bytes 884744 | tf_op jit(solution)/shard_map/ppermute | solution.py:403
  (62 other events, 285.1 us)
Sparse Core Ops, SparseCore 0:
  14.3 19.1 all-gather.7
  44.0 18.0 all-gather.9
  75.2 26.4 all-gather.11
  145.1 23.7 all-gather.13
